TPU v7x, 32 devices: a whole 2x2x4 slice. The times are simulated.
32 devices in a mesh: groups: 2 (over x), shard: 16 (over z, y, core).
Axes of the slice: x: 2, y: 2, z: 4, core: 2. Of those that a mesh axis runs over, the one named last changes fastest.
Arguments:
- kv_store: bfloat16 [64, 256, 2048], P(('groups', 'shard')), parts along dimension 0, may hold values from -6 to 6
- block_order: int32 [64], P(('groups', 'shard')), parts along dimension 0, may hold values from 0 to 31, as said below
- lengths: int32 [16], P('groups'), parts along dimension 0, may hold values from 1 to 12, as said below
- row_positions: int32 [16, 128], P('groups'), parts along dimension 0, may hold values from 0 to 3071, as said below
- queries: bfloat16 [256, 65536], P('groups', 'shard'), parts along dimension 0, may hold values from -48 to 48
- fresh_rows: bfloat16 [256, 16384], P('groups', 'shard'), parts along dimension 0, may hold values from -280 to 280
Outputs:
- attended: bfloat16 [256, 65536], P('groups', 'shard'), parts along dimension 0
There are 2 independent parts, one for each index of `groups`. A program takes and returns all parts, laid end to end along the dimension named above; each array names one. Nothing has to cross between parts.
Inputs may be any that keep to these rules, and one draw needn't show every extreme that they name: Each request has at least one block, the lengths sum to 32, and the longest request has exactly 12 blocks. Request r and request r + 4 together have at most 16 blocks, exactly so for the pair of the longest request. `row_positions`: each request's positions are non-decreasing and lie below 256 times its length; its last recomputed row is its last token, 256 lengths[r] - 1. `block_order`: A permutation; the 2 slots of one device (slots 2 d to 2 d + 1) hold blocks of requests r1, r2 with r1 % (4) != r2 % 4.
All inputs are finite; a program needn't handle non-finite values.
Results may differ from a plain program's by a relative error of at most 0.0041.
Values may be sent and summed in bfloat16 or wider, within the bound.
No kernel may reach another device: no remote copies, remote signals or barrier semaphores. Data moves between devices by JAX's collectives and lax.ppermute only.
A program may use at most 64 MiB of HBM per device.

v0:
```python
import functools
import math

import jax
import jax.numpy as jnp
import numpy as np
from jax import lax
from jax.experimental import pallas as pl
from jax.experimental.pallas import tpu as pltpu
from jax.sharding import PartitionSpec as P


HD = 128
ROPE_BASE = 500000.0
TOP_START = -1e30
MASKED = -3e30
STATS = 16
TAG = 8


VMEM = pltpu.MemorySpace.VMEM
SMEM = pltpu.MemorySpace.SMEM


def frequency_row():
    half = HD // 2
    steps = np.arange(half, dtype=np.float32)
    row = np.exp((-math.log(ROPE_BASE) * steps / half).astype(np.float32)).astype(np.float32)
    return np.concatenate([row, row])[None, :]


def signed(sine):
    lane = lax.broadcasted_iota(jnp.int32, sine.shape, len(sine.shape) - 1)
    return jnp.where(lane < HD // 2, -sine, sine)


def turn(vectors, cosine, sine):
    wide = vectors.astype(jnp.float32)
    return (wide * cosine + pltpu.roll(wide, HD // 2, 1) * sine).astype(jnp.bfloat16)


def find_block(block_id, lengths_ref):
    start = jnp.int32(0)
    request = jnp.int32(0)
    position = jnp.int32(0)
    for q in range(lengths_ref.shape[0]):
        end = start + lengths_ref[q]
        inside = (block_id >= start) & (block_id < end)
        request = jnp.where(inside, q, request)
        position = jnp.where(inside, block_id - start, position)
        start = end
    return request, position


def pack_kv(n_sub, order_ref, lengths_ref, freq_ref, kv_ref, *out_refs):
    heads = len(out_refs)
    my_head = lax.axis_index("shard") // n_sub
    block_len = kv_ref.shape[1]
    block_id = order_ref[pl.program_id(0)]
    _, position = find_block(block_id, lengths_ref)
    angle = (position * block_len).astype(jnp.float32) * freq_ref[...]
    cosine, sine = jnp.cos(angle), signed(jnp.sin(angle))
    for mask in range(heads):
        column = pl.multiple_of((my_head ^ mask) * (2 * HD), 2 * HD)
        out_refs[mask][0, :block_len, :HD] = turn(kv_ref[0, :, pl.ds(column, HD)], cosine, sine)
        out_refs[mask][0, :block_len, HD:] = kv_ref[0, :, pl.ds(column + HD, HD)]
        out_refs[mask][0, block_len:, :] = jnp.full((TAG, 2 * HD), block_id, jnp.int32).astype(jnp.float32).astype(jnp.bfloat16)


def pack_queries(n_sub, group_size, freq_ref, rows_ref, queries_ref, fresh_ref, *refs):
    out_refs, key_ref, cos_ref, sin_ref = refs[:-3], refs[-3], refs[-2], refs[-1]
    request = lax.axis_index("shard") // n_sub
    rows = queries_ref.shape[0]
    kv_local = fresh_ref.shape[1] // (2 * HD)
    sub_heads = group_size // n_sub
    position = rows_ref[pl.ds(request, 1), :].astype(jnp.float32)
    angle = jnp.transpose(jnp.broadcast_to(position, (HD, rows))) * freq_ref[...]
    cos_ref[...] = jnp.cos(angle)
    sin_ref[...] = signed(jnp.sin(angle))
    for kv_id in range(kv_local):
        key_ref[kv_id] = turn(fresh_ref[:, 2 * kv_id * HD : (2 * kv_id + 1) * HD], cos_ref[...], sin_ref[...])
    for step, out_ref in enumerate(out_refs):
        kv_id = (step % kv_local) ^ (request % kv_local)
        sub = (step // kv_local) ^ (request // kv_local)
        for head in range(sub_heads):
            column = pl.multiple_of((kv_id * group_size + sub * sub_heads + head) * HD, HD)
            out_ref[head * rows : (head + 1) * rows, :] = turn(
                queries_ref[:, pl.ds(column, HD)], cos_ref[...], sin_ref[...]
            )


def attend(n_sub, n_buf, first, last, blk_dev, lengths_ref, rows_ref, *refs):
    n_req = lengths_ref.shape[0]
    query_refs, refs = refs[:n_req], refs[n_req:]
    kv_refs, refs = refs[:n_buf], refs[n_buf:]
    if not first:
        acc_in, top_in, refs = refs[0], refs[1], refs[2:]
    if last:
        out_refs, refs = refs[:n_req], refs[n_req:]
        acc_ref, top_ref, refs = refs[0], refs[1], refs[2:]
    else:
        acc_ref, top_ref, refs = refs[0], refs[1], refs[2:]
    query_buf, kv_buf, id_ref, query_sem, kv_sem = refs
    query_copies = [pltpu.make_async_copy(ref, query_buf.at[i], query_sem.at[i]) for i, ref in enumerate(query_refs)]
    kv_copies = [
        pltpu.make_async_copy(ref, kv_buf.at[pl.ds(i * blk_dev, blk_dev)], kv_sem.at[i]) for i, ref in enumerate(kv_refs)
    ]
    for copy in query_copies + kv_copies:
        copy.start()
    me = lax.axis_index("shard")
    my_head, my_sub = me // n_sub, me % n_sub
    kv_local = n_req // n_sub
    mixed = my_sub * kv_local + my_head % kv_local
    block_len = kv_buf.shape[1] - TAG
    width = rows_ref.shape[2]
    if first:
        acc_ref[...] = jnp.zeros_like(acc_ref)
        top_ref[...] = jnp.full_like(top_ref, TOP_START)
    else:
        acc_ref[...] = acc_in[...]
        top_ref[...] = top_in[...]
    for copy in query_copies + kv_copies:
        copy.wait()
    for i in range(n_buf * blk_dev):
        id_ref[i] = jnp.max(kv_buf[i, block_len:, :].astype(jnp.float32)).astype(jnp.int32)
    scale = math.log2(math.e) / math.sqrt(HD)
    token = lax.broadcasted_iota(jnp.int32, (block_len, width), 0)

    def one_block(i, carried):
        request, position = find_block(id_ref[i], lengths_ref)
        scores = lax.dot_general(
            kv_buf[i, :block_len, :HD],
            query_buf[request ^ mixed],
            (((1,), (1,)), ((), ())),
            preferred_element_type=jnp.float32,
        )
        limit = rows_ref[request] - position * block_len
        scores = jnp.where(token < limit, scores * scale, MASKED)
        old_top = top_ref[request]
        new_top = jnp.maximum(old_top, jnp.max(scores, axis=0, keepdims=True))
        factor = jnp.exp2(old_top - new_top)
        weights = jnp.exp2(scores - new_top).astype(jnp.bfloat16)
        values = jnp.concatenate(
            [jnp.transpose(kv_buf[i, :block_len, HD:]), jnp.ones((STATS, block_len), jnp.bfloat16)], axis=0
        )
        summed = jnp.dot(values, weights, preferred_element_type=jnp.float32)
        acc_ref[request] = acc_ref[request] * factor + summed[: HD + 8]
        top_ref[request] = new_top
        return carried

    lax.fori_loop(0, n_buf * blk_dev, one_block, 0)

    if last:
        sub_heads = width // HD
        for step, out_ref in enumerate(out_refs):
            request = step ^ mixed
            total = acc_ref[request, HD : HD + 1]
            some = total > 0.0
            result = acc_ref[request, :HD] / jnp.where(some, total, 1.0)
            level = jnp.where(some, top_ref[request] + jnp.log2(jnp.where(some, total, 1.0)), TOP_START)
            for head in range(sub_heads):
                lanes = slice(head * HD, (head + 1) * HD)
                out_ref[lanes, :] = jnp.transpose(result[:, lanes]).astype(jnp.bfloat16)
            level = jnp.concatenate([level[:, head * HD : (head + 1) * HD] for head in range(sub_heads)], axis=0)
            high = level.astype(jnp.bfloat16)
            rest = level - high.astype(jnp.float32)
            middle = rest.astype(jnp.bfloat16)
            low = (rest - middle.astype(jnp.float32)).astype(jnp.bfloat16)
            pieces = [high, middle, low, jnp.zeros((STATS - 3 * sub_heads, HD), jnp.bfloat16)]
            out_ref[width : width + STATS, :] = jnp.concatenate(pieces, axis=0)


def own_scores(n_sub, group_size, key_ref, *refs):
    query_refs, own_ref = refs[:-1], refs[-1]
    request = lax.axis_index("shard") // n_sub
    kv_local, rows = key_ref.shape[:2]
    sub_heads = group_size // n_sub
    scale = math.log2(math.e) / math.sqrt(HD)
    own_ref[...] = jnp.zeros_like(own_ref)
    for step, query_ref in enumerate(query_refs):
        own_key = key_ref[(step % kv_local) ^ (request % kv_local)].astype(jnp.float32)
        for head in range(sub_heads):
            query = query_ref[head * rows : (head + 1) * rows, :].astype(jnp.float32)
            column = step * sub_heads + head
            own_ref[:, column : column + 1] = jnp.sum(query * own_key, axis=1, keepdims=True) * scale


def merge_own(n_sub, group_size, own_ref, fresh_ref, *refs):
    part_refs, out_ref, level_ref = refs[:-2], refs[-2], refs[-1]
    request = lax.axis_index("shard") // n_sub
    rows = out_ref.shape[0]
    kv_local = fresh_ref.shape[1] // (2 * HD)
    sub_heads = group_size // n_sub
    level_ref[...] = jnp.zeros_like(level_ref)
    for step, part_ref in enumerate(part_refs):
        stats = part_ref[sub_heads * rows :, :].astype(jnp.float32)
        level_ref[step * sub_heads : (step + 1) * sub_heads] = (
            stats[:sub_heads] + stats[sub_heads : 2 * sub_heads] + stats[2 * sub_heads : 3 * sub_heads]
        )
    level = jnp.transpose(level_ref[...])
    own = own_ref[...]
    top = jnp.maximum(own, level)
    own_share = jnp.exp2(own - top)
    share = jnp.exp2(level - top)
    norm = 1.0 / (own_share + share)
    own_share, share = own_share * norm, share * norm
    for step, part_ref in enumerate(part_refs):
        kv_id = (step % kv_local) ^ (request % kv_local)
        sub = (step // kv_local) ^ (request // kv_local)
        value_column = pl.multiple_of((2 * kv_id + 1) * HD, HD)
        own_value = fresh_ref[:, pl.ds(value_column, HD)].astype(jnp.float32)
        for head in range(sub_heads):
            lane = step * sub_heads + head
            part = part_ref[head * rows : (head + 1) * rows, :].astype(jnp.float32)
            column = pl.multiple_of((kv_id * group_size + sub * sub_heads + head) * HD, HD)
            out_ref[:, pl.ds(column, HD)] = (
                part * share[:, lane : lane + 1] + own_value * own_share[:, lane : lane + 1]
            ).astype(jnp.bfloat16)


def moved(x, pairs):
    return lax.ppermute(x, "shard", pairs)


def shards(kv_store, block_order, lengths, row_positions, queries, fresh_rows):
    n_shard = lax.axis_size("shard")
    n_req, rows = row_positions.shape
    n_sub = n_shard // n_req
    blk_dev, block_len, full_width = kv_store.shape
    kv_heads = full_width // (2 * HD)
    kv_local = kv_heads // n_sub
    group_size = queries.shape[1] // (kv_local * HD)
    sub_heads = group_size // n_sub
    width = sub_heads * rows
    bf16 = jnp.bfloat16
    freq = jnp.asarray(frequency_row())
    spec = functools.partial(pl.BlockSpec, memory_space=VMEM)
    smem = pl.BlockSpec(memory_space=SMEM)
    anywhere = pl.BlockSpec(memory_space=pl.ANY)

    packed = pl.pallas_call(
        functools.partial(pack_queries, n_sub, group_size),
        out_shape=[jax.ShapeDtypeStruct((width, HD), bf16)] * n_req + [jax.ShapeDtypeStruct((kv_local, rows, HD), bf16)],
        in_specs=[spec()] * 4,
        out_specs=[spec()] * (n_req + 1),
        scratch_shapes=[pltpu.VMEM((rows, HD), jnp.float32)] * 2,
        name="pack_queries",
    )(freq, row_positions, queries, fresh_rows)
    sent_queries, own_key = packed[:n_req], packed[n_req]

    level_rows = max(HD, n_req * sub_heads)
    own = pl.pallas_call(
        functools.partial(own_scores, n_sub, group_size),
        out_shape=jax.ShapeDtypeStruct((rows, level_rows), jnp.float32),
        in_specs=[spec()] * (1 + n_req),
        out_specs=spec(),
        name="own_scores",
    )(own_key, *sent_queries)
    lengths_after = lax.optimization_barrier((lengths, sent_queries[0]))[0]

    packed_kv = pl.pallas_call(
        functools.partial(pack_kv, n_sub),
        grid=(blk_dev,),
        out_shape=[jax.ShapeDtypeStruct((blk_dev, block_len + TAG, 2 * HD), bf16)] * kv_heads,
        in_specs=[smem, smem, pl.BlockSpec((1, HD), lambda i: (0, 0)), pl.BlockSpec((1, block_len, full_width), lambda i: (i, 0, 0))],
        out_specs=[pl.BlockSpec((1, block_len + TAG, 2 * HD), lambda i: (i, 0, 0))] * kv_heads,
        name="pack_kv",
    )(block_order, lengths_after, freq, kv_store)

    to_compute = []
    for step in range(n_req):
        pairs = []
        for request in range(n_req):
            for h in range(n_sub):
                head = kv_local * h + ((step % kv_local) ^ (request % kv_local))
                sub = (step // kv_local) ^ (request // kv_local)
                pairs.append((request * n_sub + h, head * n_sub + sub))
        to_compute.append(pairs)
    held_queries = [moved(x, pairs) for x, pairs in zip(sent_queries, to_compute)]

    wide_rows = jnp.tile(row_positions, (1, sub_heads))[:, None, :]

    def after(x, *others):
        return lax.optimization_barrier((x, *others))[0] if others else x

    def at_head(mask, *others):
        pairs = [(d, ((d // n_sub) ^ mask) * n_sub + d % n_sub) for d in range(n_shard)]
        return packed_kv[0] if mask == 0 else moved(after(packed_kv[mask], *others), pairs)

    def from_sub(mask, back, *others):
        x = landed[mask]
        pairs = [(d, (d // n_sub) * n_sub + (d % n_sub + back) % n_sub) for d in range(n_shard)]
        return x if back == 0 else moved(after(x, *others), pairs)

    half = kv_heads // 2
    groups = [[0], list(range(1, half)), [half, half + 1]] + [[mask] for mask in range(half + 2, kv_heads)]
    landed = {mask: at_head(mask) for mask in range(half + 2)}
    landed[half + 2] = at_head(half + 2, *held_queries)
    state_shapes = [
        jax.ShapeDtypeStruct((n_req, HD + 8, width), jnp.float32),
        jax.ShapeDtypeStruct((n_req, 1, width), jnp.float32),
    ]
    part_shapes = [jax.ShapeDtypeStruct((width + STATS, HD), bf16)] * n_req
    state, older = [], []
    for index, masks in enumerate(groups):
        if index == 2:
            for mask in range(half + 3, kv_heads):
                if mask not in landed:
                    landed[mask] = at_head(mask, *state[-1:], landed[masks[0]])
        gate = state if index <= 2 else older
        arrived = [from_sub(mask, back, *gate[-1:]) for mask in masks for back in range(n_sub)]
        buffers = [(mask, back) for mask in masks for back in range(n_sub)]
        first, last = index == 0, index == len(groups) - 1
        blocks = len(buffers) * blk_dev
        results = pl.pallas_call(
            functools.partial(attend, n_sub, len(buffers), first, last, blk_dev),
            out_shape=part_shapes if last else state_shapes,
            in_specs=[smem, spec()] + [anywhere] * (n_req + len(buffers)) + [spec()] * len(state),
            out_specs=[spec()] * (n_req if last else 2),
            scratch_shapes=([pltpu.VMEM(s.shape, s.dtype) for s in state_shapes] if last else [])
            + [
                pltpu.VMEM((n_req, width, HD), bf16),
                pltpu.VMEM((blocks, block_len + TAG, 2 * HD), bf16),
                pltpu.SMEM((blocks,), jnp.int32),
                pltpu.SemaphoreType.DMA((n_req,)),
                pltpu.SemaphoreType.DMA((len(buffers),)),
            ],
        )(lengths, wide_rows, *held_queries, *arrived, *state)
        older, state = state, list(results)
    returned = []
    for part, pairs in zip(state, to_compute):
        returned.append(lax.ppermute(part, "shard", [(b, a) for a, b in pairs]))

    return pl.pallas_call(
        functools.partial(merge_own, n_sub, group_size),
        out_shape=jax.ShapeDtypeStruct((rows, kv_local * group_size * HD), bf16),
        in_specs=[spec()] * (2 + n_req),
        out_specs=spec(),
        scratch_shapes=[pltpu.VMEM((level_rows, rows), jnp.float32)],
        name="merge_own",
    )(own, fresh_rows, *returned)


def solution(mesh):
    in_specs = (
        P(("groups", "shard"), None, None),
        P(("groups", "shard")),
        P("groups"),
        P("groups", None),
        P("groups", "shard"),
        P("groups", "shard"),
    )
    return jax.shard_map(shards, mesh=mesh, in_specs=in_specs, out_specs=P("groups", "shard"), check_vma=False)
```

profile of v0, /device:TPU:0, one launch (start us, length us, event | category | flops | bytes accessed | tf_op | source)
XLA Modules:
  0.0 156.5 jit_solution(10309406264616617578)
XLA Ops:
  0.0 3.0 %pack_queries.1 = (bf16[512,128]{1,0:T(8,128)(2,1)}, bf16[512,128]{1,0:T(8,128)(2,1)}, bf16[512,128]{1,0:T(8,128)(2,1)}, bf16[512,128]{1,0:T(8,128)(2,1)}, bf16[...) custom-call(f32[1,128]{1,0:T(1,128)} %constant.2.clone.freq_ref, ...), custom_call_target="tpu_custom_call" | custom-call | tf_op jit(solution)/shard_map/pack_queries/pallas_call | solution.py:241
  3.0 3.0 %collective-permute-start.1 = (bf16[512,128]{1,0:T(8,128)(2,1)}, bf16[512,128]{1,0:T(8,128)(2,1)S(1)}, u32[]{:S(2)}, u32[]{:S(2)}) collective-permute-start(bf16[512,128]{1,0:T(8,128)(2,1)} %get-tuple-element.50.refs_1_), channel_id=1, source_target_pairs={{0,2},{1,10},{2,0},{3,8},{4,6},{5,14},{6,4},{7,12},{8,3},{9,11},{1... | collective-permute-start | bytes 393224 | tf_op jit(solution)/shard_map/ppermute | solution.py:222
  6.0 1.6 %collective-permute-start.2 = (bf16[512,128]{1,0:T(8,128)(2,1)}, bf16[512,128]{1,0:T(8,128)(2,1)S(1)}, u32[]{:S(2)}, u32[]{:S(2)}) collective-permute-start(bf16[512,128]{1,0:T(8,128)(2,1)} %get-tuple-element.51.refs_2_), channel_id=1, source_target_pairs={{0,4},{1,12},{2,6},{3,14},{4,0},{5,8},{6,2},{7,10},{8,5},{9,13},{1... | collective-permute-start | bytes 393224 | tf_op jit(solution)/shard_map/ppermute | solution.py:222
  7.6 4.1 %collective-permute-start.4 = (bf16[512,128]{1,0:T(8,128)(2,1)}, bf16[512,128]{1,0:T(8,128)(2,1)S(1)}, u32[]{:S(2)}, u32[]{:S(2)}) collective-permute-start(bf16[512,128]{1,0:T(8,128)(2,1)} %get-tuple-element.53.refs_4_), channel_id=1, source_target_pairs={{0,1},{1,9},{2,3},{3,11},{4,5},{5,13},{6,7},{7,15},{8,0},{9,8},{10... | collective-permute-start | bytes 393224 | tf_op jit(solution)/shard_map/ppermute | solution.py:222
  11.7 1.1 collective-permute-start.5
  13.7 3.2 %pack_kv.1 = (bf16[2,264,256]{2,1,0:T(8,128)(2,1)}, bf16[2,264,256]{2,1,0:T(8,128)(2,1)}, bf16[2,264,256]{2,1,0:T(8,128)(2,1)}, bf16[2,264,256]{2,1,0:T(8,128)(2...) custom-call(s32[2]{0:T(128)} %order_ref.1, ...), custom_call_target="tpu_custom_call" | custom-call | tf_op jit(solution)/shard_map/pack_kv/pallas_call | solution.py:261
  18.0 6.3 %collective-permute-done.4.refs_4_ = bf16[512,128]{1,0:T(8,128)(2,1)S(1)} collective-permute-done((bf16[512,128]{1,0:T(8,128)(2,1)}, bf16[512,128]{1,0:T(8,128)(2,1)S(1)}, u32[]{:S(2)}, u32[]{:S(2)}) %collective-permute-start.4) | collective-permute-done | bytes 131104 | tf_op jit(solution)/shard_map/ppermute | solution.py:222
  24.3 1.5 collective-permute-done.5.refs_5_
  25.8 1.4 collective-permute-start.8
  27.2 10.5 %collective-permute-done.7.refs_7_ = bf16[512,128]{1,0:T(8,128)(2,1)S(1)} collective-permute-done((bf16[512,128]{1,0:T(8,128)(2,1)}, bf16[512,128]{1,0:T(8,128)(2,1)S(1)}, u32[]{:S(2)}, u32[]{:S(2)}) %collective-permute-start.7) | collective-permute-done | bytes 131104 | tf_op jit(solution)/shard_map/ppermute | solution.py:222
  37.7 1.6 collective-permute-start
  40.0 5.9 %shard_map.73 = (f32[8,136,512]{2,1,0:T(8,128)}, f32[8,1,512]{2,1,0:T(1,128)}) custom-call(s32[8]{0:T(128)} %lengths_ref.10, s32[8,1,512]{2,1,0:T(1,128)} %bitcast.1, bf16[512,128]{1,0:T(8,128)(2,1)} %copy-done.7, bf16[512,128]{1,0:T(8,128)(2,1)} %copy-done, bf16[512,128]{1,0:T(8,128)(2,1)} %copy-done.1, bf16[512,128]{1,0:T(8,128)(2,1)} %copy-done.2, ...), custom_call_target="tpu_custom_call" | custom-call | tf_op jit(solution)/shard_map/pallas_call | solution.py:315
  45.9 9.6 %collective-permute-start.10 = (bf16[2,264,256]{2,1,0:T(8,128)(2,1)S(1)}, bf16[2,264,256]{2,1,0:T(8,128)(2,1)S(1)}, u32[]{:S(2)}, u32[]{:S(2)}) collective-permute-start(bf16[2,264,256]{2,1,0:T(8,128)(2,1)S(1)} %collective-permute-done.8.refs_8_), channel_id=1, source_target_pairs={{0,1},{1,0},{2,3},{3,2},{4,5},{5,4},{6,7},{7,6},{8,9},{9,8},{10,11... | collective-permute-start | bytes 811016 | tf_op jit(solution)/shard_map/ppermute | solution.py:222
  56.4 3.0 %collective-permute-start.15 = (bf16[2,264,256]{2,1,0:T(8,128)(2,1)}, bf16[2,264,256]{2,1,0:T(8,128)(2,1)S(1)}, u32[]{:S(2)}, u32[]{:S(2)}) collective-permute-start(bf16[2,264,256]{2,1,0:T(8,128)(2,1)} %get-tuple-element.69), channel_id=1, source_target_pairs={{0,8},{1,9},{2,10},{3,11},{4,12},{5,13},{6,14},{7,15},{8,0},{9,1},... | collective-permute-start | bytes 811016 | tf_op jit(solution)/shard_map/ppermute | solution.py:222
  59.5 1.3 collective-permute-start.21
  61.6 11.1 %shard_map.74 = (f32[8,136,512]{2,1,0:T(8,128)}, f32[8,1,512]{2,1,0:T(1,128)}) custom-call(s32[8]{0:T(128)} %lengths_ref.10, s32[8,1,512]{2,1,0:T(1,128)} %bitcast.2, bf16[512,128]{1,0:T(8,128)(2,1)} %copy-done.7, bf16[512,128]{1,0:T(8,128)(2,1)} %copy-done, bf16[512,128]{1,0:T(8,128)(2,1)} %copy-done.1, bf16[512,128]{1,0:T(8,128)(2,1)} %copy-done.2, ...), custom_call_target="tpu_custom_call" | custom-call | tf_op jit(solution)/shard_map/pallas_call | solution.py:315
  72.7 10.1 %collective-permute-done.18.refs_10_ = bf16[2,264,256]{2,1,0:T(8,128)(2,1)S(1)} collective-permute-done((bf16[2,264,256]{2,1,0:T(8,128)(2,1)}, bf16[2,264,256]{2,1,0:T(8,128)(2,1)S(1)}, u32[]{:S(2)}, u32[]{:S(2)}) %collective-permute-start.18) | collective-permute-done | bytes 270368 | tf_op jit(solution)/shard_map/ppermute | solution.py:222
  82.8 5.4 %collective-permute-done.15.refs_8_ = bf16[2,264,256]{2,1,0:T(8,128)(2,1)S(1)} collective-permute-done((bf16[2,264,256]{2,1,0:T(8,128)(2,1)}, bf16[2,264,256]{2,1,0:T(8,128)(2,1)S(1)}, u32[]{:S(2)}, u32[]{:S(2)}) %collective-permute-start.15) | collective-permute-done | bytes 270368 | tf_op jit(solution)/shard_map/ppermute | solution.py:222
  88.7 2.7 %collective-permute-start.16 = (bf16[2,264,256]{2,1,0:T(8,128)(2,1)S(1)}, bf16[2,264,256]{2,1,0:T(8,128)(2,1)S(1)}, u32[]{:S(2)}, u32[]{:S(2)}) collective-permute-start(bf16[2,264,256]{2,1,0:T(8,128)(2,1)S(1)} %copy-done.32), channel_id=1, source_target_pairs={{0,14},{1,15},{2,12},{3,13},{4,10},{5,11},{6,8},{7,9},{8,6},{9,7},... | collective-permute-start | bytes 811016 | tf_op jit(solution)/shard_map/ppermute | solution.py:222
  92.3 9.0 %shard_map.75 = (f32[8,136,512]{2,1,0:T(8,128)}, f32[8,1,512]{2,1,0:T(1,128)}) custom-call(s32[8]{0:T(128)} %lengths_ref.10, s32[8,1,512]{2,1,0:T(1,128)} %bitcast.3, bf16[512,128]{1,0:T(8,128)(2,1)} %copy-done.7, bf16[512,128]{1,0:T(8,128)(2,1)} %copy-done, bf16[512,128]{1,0:T(8,128)(2,1)} %copy-done.1, bf16[512,128]{1,0:T(8,128)(2,1)} %copy-done.2, ...), custom_call_target="tpu_custom_call" | custom-call | tf_op jit(solution)/shard_map/pallas_call | solution.py:315
  102.5 6.7 %shard_map.76 = (f32[8,136,512]{2,1,0:T(8,128)}, f32[8,1,512]{2,1,0:T(1,128)}) custom-call(s32[8]{0:T(128)} %lengths_ref.10, s32[8,1,512]{2,1,0:T(1,128)} %bitcast.4, bf16[512,128]{1,0:T(8,128)(2,1)} %copy-done.7, bf16[512,128]{1,0:T(8,128)(2,1)} %copy-done, bf16[512,128]{1,0:T(8,128)(2,1)} %copy-done.1, bf16[512,128]{1,0:T(8,128)(2,1)} %copy-done.2, ...), custom_call_target="tpu_custom_call" | custom-call | tf_op jit(solution)/shard_map/pallas_call | solution.py:315
  109.9 6.6 %shard_map.77 = (bf16[528,128]{1,0:T(8,128)(2,1)}, bf16[528,128]{1,0:T(8,128)(2,1)}, bf16[528,128]{1,0:T(8,128)(2,1)}, bf16[528,128]{1,0:T(8,128)(2,1)}, bf16[52...) custom-call(s32[8]{0:T(128)} %lengths_ref.10, ...), custom_call_target="tpu_custom_call" | custom-call | tf_op jit(solution)/shard_map/pallas_call | solution.py:315
  116.6 1.6 collective-permute-start.23
  118.1 1.1 collective-permute-start.24
  119.2 8.9 %collective-permute-start.25 = (bf16[528,128]{1,0:T(8,128)(2,1)}, bf16[528,128]{1,0:T(8,128)(2,1)S(1)}, u32[]{:S(2)}, u32[]{:S(2)}) collective-permute-start(bf16[528,128]{1,0:T(8,128)(2,1)} %get-tuple-element.85), channel_id=1, source_target_pairs={{4,0},{12,1},{6,2},{14,3},{0,4},{8,5},{2,6},{10,7},{5,8},{13,9},{7... | collective-permute-start | bytes 405512 | tf_op jit(solution)/shard_map/ppermute | solution.py:332
  128.5 5.1 %collective-permute-start.27 = (bf16[528,128]{1,0:T(8,128)(2,1)}, bf16[528,128]{1,0:T(8,128)(2,1)S(1)}, u32[]{:S(2)}, u32[]{:S(2)}) collective-permute-start(bf16[528,128]{1,0:T(8,128)(2,1)} %get-tuple-element.87), channel_id=1, source_target_pairs={{1,0},{9,1},{3,2},{11,3},{5,4},{13,5},{7,6},{15,7},{0,8},{8,9},{2,... | collective-permute-start | bytes 405512 | tf_op jit(solution)/shard_map/ppermute | solution.py:332
  133.6 1.5 collective-permute-start.28
  135.1 2.2 %collective-permute-start.29 = (bf16[528,128]{1,0:T(8,128)(2,1)}, bf16[528,128]{1,0:T(8,128)(2,1)S(1)}, u32[]{:S(2)}, u32[]{:S(2)}) collective-permute-start(bf16[528,128]{1,0:T(8,128)(2,1)} %get-tuple-element.89), channel_id=1, source_target_pairs={{5,0},{13,1},{7,2},{15,3},{1,4},{9,5},{3,6},{11,7},{4,8},{12,9},{6... | collective-permute-start | bytes 405512 | tf_op jit(solution)/shard_map/ppermute | solution.py:332
  137.4 4.5 %collective-permute-start.30 = (bf16[528,128]{1,0:T(8,128)(2,1)}, bf16[528,128]{1,0:T(8,128)(2,1)S(1)}, u32[]{:S(2)}, u32[]{:S(2)}) collective-permute-start(bf16[528,128]{1,0:T(8,128)(2,1)} %get-tuple-element.90), channel_id=1, source_target_pairs={{7,0},{15,1},{5,2},{13,3},{3,4},{11,5},{1,6},{9,7},{6,8},{14,9},{4... | collective-permute-start | bytes 405512 | tf_op jit(solution)/shard_map/ppermute | solution.py:332
  141.9 2.6 %own_scores.1.own_ref = f32[128,128]{1,0:T(8,128)} custom-call(bf16[4,128,128]{2,1,0:T(8,128)(2,1)} %get-tuple-element.48.key_ref, bf16[512,128]{1,0:T(8,128)(2,1)} %get-tuple-element.49.refs_0_, bf16[512,128]{1,0:T(8,128)(2,1)} %get-tuple-element.50.refs_1_, bf16[512,128]{1,0:T(8,128)(2,1)} %get-tuple-element.51.refs_2_, ...), custom_call_target="tpu_custom_call" | custom-call | tf_op jit(solution)/shard_map/own_scores/pallas_call | solution.py:252
  144.6 7.6 %collective-permute-done.30.refs_7_ = bf16[528,128]{1,0:T(8,128)(2,1)S(1)} collective-permute-done((bf16[528,128]{1,0:T(8,128)(2,1)}, bf16[528,128]{1,0:T(8,128)(2,1)S(1)}, u32[]{:S(2)}, u32[]{:S(2)}) %collective-permute-start.30) | collective-permute-done | bytes 135200 | tf_op jit(solution)/shard_map/ppermute | solution.py:332
  152.8 3.7 %merge_own.1 = bf16[128,4096]{1,0:T(8,128)(2,1)} custom-call(f32[128,128]{1,0:T(8,128)} %own_scores.1.own_ref, bf16[128,1024]{1,0:T(8,128)(2,1)} %fresh_ref.3, bf16[528,128]{1,0:T(8,128)(2,1)} %copy-done.23, bf16[528,128]{1,0:T(8,128)(2,1)} %copy-done.24, bf16[528,128]{1,0:T(8,128)(2,1)} %copy-done.25, bf16[528,128]{1,0:T(8,128)(2,1)} %copy-done.26, ...), custom_call_target="tpu_custom_call" | custom-call | tf_op jit(solution)/shard_map/merge_own/pallas_call | solution.py:334
  (106 shorter events, 8.8 us)
Async XLA Ops:
  0.0 39.2 %copy-start.31 = (s32[8,128]{1,0:T(8,128)S(1)}, s32[8,128]{1,0:T(8,128)}, u32[]{:S(2)}) copy-start(s32[8,128]{1,0:T(8,128)} %rows_ref.1) | copy-start | bytes 12292
  3.0 9.8 %collective-permute-start.1 = (bf16[512,128]{1,0:T(8,128)(2,1)}, bf16[512,128]{1,0:T(8,128)(2,1)S(1)}, u32[]{:S(2)}, u32[]{:S(2)}) collective-permute-start(bf16[512,128]{1,0:T(8,128)(2,1)} %get-tuple-element.50.refs_1_), channel_id=1, source_target_pairs={{0,2},{1,10},{2,0},{3,8},{4,6},{5,14},{6,4},{7,12},{8,3},{9,11},{1... | collective-permute-start | bytes 393224 | tf_op jit(solution)/shard_map/ppermute | solution.py:222
  6.0 10.8 %collective-permute-start.2 = (bf16[512,128]{1,0:T(8,128)(2,1)}, bf16[512,128]{1,0:T(8,128)(2,1)S(1)}, u32[]{:S(2)}, u32[]{:S(2)}) collective-permute-start(bf16[512,128]{1,0:T(8,128)(2,1)} %get-tuple-element.51.refs_2_), channel_id=1, source_target_pairs={{0,4},{1,12},{2,6},{3,14},{4,0},{5,8},{6,2},{7,10},{8,5},{9,13},{1... | collective-permute-start | bytes 393224 | tf_op jit(solution)/shard_map/ppermute | solution.py:222
  7.6 9.3 %collective-permute-start.3 = (bf16[512,128]{1,0:T(8,128)(2,1)}, bf16[512,128]{1,0:T(8,128)(2,1)S(1)}, u32[]{:S(2)}, u32[]{:S(2)}) collective-permute-start(bf16[512,128]{1,0:T(8,128)(2,1)} %get-tuple-element.52.refs_3_), channel_id=1, source_target_pairs={{0,6},{1,14},{2,4},{3,12},{4,2},{5,10},{6,0},{7,8},{8,7},{9,15},{1... | collective-permute-start | bytes 393224 | tf_op jit(solution)/shard_map/ppermute | solution.py:222
  7.6 16.7 %collective-permute-start.4 = (bf16[512,128]{1,0:T(8,128)(2,1)}, bf16[512,128]{1,0:T(8,128)(2,1)S(1)}, u32[]{:S(2)}, u32[]{:S(2)}) collective-permute-start(bf16[512,128]{1,0:T(8,128)(2,1)} %get-tuple-element.53.refs_4_), channel_id=1, source_target_pairs={{0,1},{1,9},{2,3},{3,11},{4,5},{5,13},{6,7},{7,15},{8,0},{9,8},{10... | collective-permute-start | bytes 393224 | tf_op jit(solution)/shard_map/ppermute | solution.py:222
  11.7 14.1 %collective-permute-start.5 = (bf16[512,128]{1,0:T(8,128)(2,1)}, bf16[512,128]{1,0:T(8,128)(2,1)S(1)}, u32[]{:S(2)}, u32[]{:S(2)}) collective-permute-start(bf16[512,128]{1,0:T(8,128)(2,1)} %get-tuple-element.54.refs_5_), channel_id=1, source_target_pairs={{0,3},{1,11},{2,1},{3,9},{4,7},{5,15},{6,5},{7,13},{8,2},{9,10},{1... | collective-permute-start | bytes 393224 | tf_op jit(solution)/shard_map/ppermute | solution.py:222
  12.8 14.4 %collective-permute-start.6 = (bf16[512,128]{1,0:T(8,128)(2,1)}, bf16[512,128]{1,0:T(8,128)(2,1)S(1)}, u32[]{:S(2)}, u32[]{:S(2)}) collective-permute-start(bf16[512,128]{1,0:T(8,128)(2,1)} %get-tuple-element.55.refs_6_), channel_id=1, source_target_pairs={{0,5},{1,13},{2,7},{3,15},{4,1},{5,9},{6,3},{7,11},{8,4},{9,12},{1... | collective-permute-start | bytes 393224 | tf_op jit(solution)/shard_map/ppermute | solution.py:222
  16.9 22.4 %collective-permute-start.9 = (bf16[2,264,256]{2,1,0:T(8,128)(2,1)}, bf16[2,264,256]{2,1,0:T(8,128)(2,1)S(1)}, u32[]{:S(2)}, u32[]{:S(2)}) collective-permute-start(bf16[2,264,256]{2,1,0:T(8,128)(2,1)} %get-tuple-element.60.refs_8_), channel_id=1, source_target_pairs={{0,1},{1,0},{2,3},{3,2},{4,5},{5,4},{6,7},{7,6},{8,9},{9,8},{10,11... | collective-permute-start | bytes 811016 | tf_op jit(solution)/shard_map/ppermute | solution.py:222
  17.0 28.9 %collective-permute-start.13 = (bf16[2,264,256]{2,1,0:T(8,128)(2,1)}, bf16[2,264,256]{2,1,0:T(8,128)(2,1)S(1)}, u32[]{:S(2)}, u32[]{:S(2)}) collective-permute-start(bf16[2,264,256]{2,1,0:T(8,128)(2,1)} %get-tuple-element.65), channel_id=1, source_target_pairs={{0,6},{1,7},{2,4},{3,5},{4,2},{5,3},{6,0},{7,1},{8,14},{9,15},{10,... | collective-permute-start | bytes 811016 | tf_op jit(solution)/shard_map/ppermute | solution.py:222
  24.3 21.6 %collective-permute-start.11 = (bf16[2,264,256]{2,1,0:T(8,128)(2,1)}, bf16[2,264,256]{2,1,0:T(8,128)(2,1)S(1)}, u32[]{:S(2)}, u32[]{:S(2)}) collective-permute-start(bf16[2,264,256]{2,1,0:T(8,128)(2,1)} %get-tuple-element.63), channel_id=1, source_target_pairs={{0,4},{1,5},{2,6},{3,7},{4,0},{5,1},{6,2},{7,3},{8,12},{9,13},{10,... | collective-permute-start | bytes 811016 | tf_op jit(solution)/shard_map/ppermute | solution.py:222
  25.8 20.1 %collective-permute-start.8 = (bf16[2,264,256]{2,1,0:T(8,128)(2,1)}, bf16[2,264,256]{2,1,0:T(8,128)(2,1)S(1)}, u32[]{:S(2)}, u32[]{:S(2)}) collective-permute-start(bf16[2,264,256]{2,1,0:T(8,128)(2,1)} %get-tuple-element.59), channel_id=1, source_target_pairs={{0,2},{1,3},{2,0},{3,1},{4,6},{5,7},{6,4},{7,5},{8,10},{9,11},{10,... | collective-permute-start | bytes 811016 | tf_op jit(solution)/shard_map/ppermute | solution.py:222
  27.2 10.5 %collective-permute-start.7 = (bf16[512,128]{1,0:T(8,128)(2,1)}, bf16[512,128]{1,0:T(8,128)(2,1)S(1)}, u32[]{:S(2)}, u32[]{:S(2)}) collective-permute-start(bf16[512,128]{1,0:T(8,128)(2,1)} %get-tuple-element.56.refs_7_), channel_id=1, source_target_pairs={{0,7},{1,15},{2,5},{3,13},{4,3},{5,11},{6,1},{7,9},{8,6},{9,14},{1... | collective-permute-start | bytes 393224 | tf_op jit(solution)/shard_map/ppermute | solution.py:222
  37.7 1.6 collective-permute-start
  45.9 13.5 %collective-permute-start.10 = (bf16[2,264,256]{2,1,0:T(8,128)(2,1)S(1)}, bf16[2,264,256]{2,1,0:T(8,128)(2,1)S(1)}, u32[]{:S(2)}, u32[]{:S(2)}) collective-permute-start(bf16[2,264,256]{2,1,0:T(8,128)(2,1)S(1)} %collective-permute-done.8.refs_8_), channel_id=1, source_target_pairs={{0,1},{1,0},{2,3},{3,2},{4,5},{5,4},{6,7},{7,6},{8,9},{9,8},{10,11... | collective-permute-start | bytes 811016 | tf_op jit(solution)/shard_map/ppermute | solution.py:222
  55.5 5.3 %collective-permute-start.12 = (bf16[2,264,256]{2,1,0:T(8,128)(2,1)S(1)}, bf16[2,264,256]{2,1,0:T(8,128)(2,1)S(1)}, u32[]{:S(2)}, u32[]{:S(2)}) collective-permute-start(bf16[2,264,256]{2,1,0:T(8,128)(2,1)S(1)} %collective-permute-done.11.refs_10_), channel_id=1, source_target_pairs={{0,1},{1,0},{2,3},{3,2},{4,5},{5,4},{6,7},{7,6},{8,9},{9,8},{10,11... | collective-permute-start | bytes 811016 | tf_op jit(solution)/shard_map/ppermute | solution.py:222
  55.6 5.2 %collective-permute-start.14 = (bf16[2,264,256]{2,1,0:T(8,128)(2,1)S(1)}, bf16[2,264,256]{2,1,0:T(8,128)(2,1)S(1)}, u32[]{:S(2)}, u32[]{:S(2)}) collective-permute-start(bf16[2,264,256]{2,1,0:T(8,128)(2,1)S(1)} %collective-permute-done.13.refs_12_), channel_id=1, source_target_pairs={{0,1},{1,0},{2,3},{3,2},{4,5},{5,4},{6,7},{7,6},{8,9},{9,8},{10,11... | collective-permute-start | bytes 811016 | tf_op jit(solution)/shard_map/ppermute | solution.py:222
  56.0 26.8 %collective-permute-start.18 = (bf16[2,264,256]{2,1,0:T(8,128)(2,1)}, bf16[2,264,256]{2,1,0:T(8,128)(2,1)S(1)}, u32[]{:S(2)}, u32[]{:S(2)}) collective-permute-start(bf16[2,264,256]{2,1,0:T(8,128)(2,1)} %get-tuple-element.72), channel_id=1, source_target_pairs={{0,10},{1,11},{2,8},{3,9},{4,14},{5,15},{6,12},{7,13},{8,2},{9,3},... | collective-permute-start | bytes 811016 | tf_op jit(solution)/shard_map/ppermute | solution.py:222
  56.4 31.7 %collective-permute-start.15 = (bf16[2,264,256]{2,1,0:T(8,128)(2,1)}, bf16[2,264,256]{2,1,0:T(8,128)(2,1)S(1)}, u32[]{:S(2)}, u32[]{:S(2)}) collective-permute-start(bf16[2,264,256]{2,1,0:T(8,128)(2,1)} %get-tuple-element.69), channel_id=1, source_target_pairs={{0,8},{1,9},{2,10},{3,11},{4,12},{5,13},{6,14},{7,15},{8,0},{9,1},... | collective-permute-start | bytes 811016 | tf_op jit(solution)/shard_map/ppermute | solution.py:222
  59.5 31.9 %collective-permute-start.21 = (bf16[2,264,256]{2,1,0:T(8,128)(2,1)}, bf16[2,264,256]{2,1,0:T(8,128)(2,1)S(1)}, u32[]{:S(2)}, u32[]{:S(2)}) collective-permute-start(bf16[2,264,256]{2,1,0:T(8,128)(2,1)} %get-tuple-element.78), channel_id=1, source_target_pairs={{0,12},{1,13},{2,14},{3,15},{4,8},{5,9},{6,10},{7,11},{8,4},{9,5},... | collective-permute-start | bytes 811016 | tf_op jit(solution)/shard_map/ppermute | solution.py:222
  88.2 3.2 %collective-permute-start.17 = (bf16[2,264,256]{2,1,0:T(8,128)(2,1)S(1)}, bf16[2,264,256]{2,1,0:T(8,128)(2,1)S(1)}, u32[]{:S(2)}, u32[]{:S(2)}) collective-permute-start(bf16[2,264,256]{2,1,0:T(8,128)(2,1)S(1)} %collective-permute-done.15.refs_8_), channel_id=1, source_target_pairs={{0,1},{1,0},{2,3},{3,2},{4,5},{5,4},{6,7},{7,6},{8,9},{9,8},{10,11... | collective-permute-start | bytes 811016 | tf_op jit(solution)/shard_map/ppermute | solution.py:222
  88.2 3.2 %collective-permute-start.19 = (bf16[2,264,256]{2,1,0:T(8,128)(2,1)S(1)}, bf16[2,264,256]{2,1,0:T(8,128)(2,1)S(1)}, u32[]{:S(2)}, u32[]{:S(2)}) collective-permute-start(bf16[2,264,256]{2,1,0:T(8,128)(2,1)S(1)} %collective-permute-done.18.refs_10_), channel_id=1, source_target_pairs={{0,1},{1,0},{2,3},{3,2},{4,5},{5,4},{6,7},{7,6},{8,9},{9,8},{10,11... | collective-permute-start | bytes 811016 | tf_op jit(solution)/shard_map/ppermute | solution.py:222
  88.7 12.6 %collective-permute-start.16 = (bf16[2,264,256]{2,1,0:T(8,128)(2,1)S(1)}, bf16[2,264,256]{2,1,0:T(8,128)(2,1)S(1)}, u32[]{:S(2)}, u32[]{:S(2)}) collective-permute-start(bf16[2,264,256]{2,1,0:T(8,128)(2,1)S(1)} %copy-done.32), channel_id=1, source_target_pairs={{0,14},{1,15},{2,12},{3,13},{4,10},{5,11},{6,8},{7,9},{8,6},{9,7},... | collective-permute-start | bytes 811016 | tf_op jit(solution)/shard_map/ppermute | solution.py:222
  91.4 10.4 %collective-permute-start.22 = (bf16[2,264,256]{2,1,0:T(8,128)(2,1)S(1)}, bf16[2,264,256]{2,1,0:T(8,128)(2,1)S(1)}, u32[]{:S(2)}, u32[]{:S(2)}) collective-permute-start(bf16[2,264,256]{2,1,0:T(8,128)(2,1)S(1)} %collective-permute-done.21.refs_8_), channel_id=1, source_target_pairs={{0,1},{1,0},{2,3},{3,2},{4,5},{5,4},{6,7},{7,6},{8,9},{9,8},{10,11... | collective-permute-start | bytes 811016 | tf_op jit(solution)/shard_map/ppermute | solution.py:222
  101.3 7.9 %collective-permute-start.20 = (bf16[2,264,256]{2,1,0:T(8,128)(2,1)S(1)}, bf16[2,264,256]{2,1,0:T(8,128)(2,1)S(1)}, u32[]{:S(2)}, u32[]{:S(2)}) collective-permute-start(bf16[2,264,256]{2,1,0:T(8,128)(2,1)S(1)} %collective-permute-done.16.refs_8_), channel_id=1, source_target_pairs={{0,1},{1,0},{2,3},{3,2},{4,5},{5,4},{6,7},{7,6},{8,9},{9,8},{10,11... | collective-permute-start | bytes 811016 | tf_op jit(solution)/shard_map/ppermute | solution.py:222
  116.6 17.0 %collective-permute-start.23 = (bf16[528,128]{1,0:T(8,128)(2,1)}, bf16[528,128]{1,0:T(8,128)(2,1)S(1)}, u32[]{:S(2)}, u32[]{:S(2)}) collective-permute-start(bf16[528,128]{1,0:T(8,128)(2,1)} %get-tuple-element.83), channel_id=1, source_target_pairs={{0,0},{8,1},{2,2},{10,3},{4,4},{12,5},{6,6},{14,7},{1,8},{9,9},{3,... | collective-permute-start | bytes 405512 | tf_op jit(solution)/shard_map/ppermute | solution.py:332
  118.1 17.0 %collective-permute-start.24 = (bf16[528,128]{1,0:T(8,128)(2,1)}, bf16[528,128]{1,0:T(8,128)(2,1)S(1)}, u32[]{:S(2)}, u32[]{:S(2)}) collective-permute-start(bf16[528,128]{1,0:T(8,128)(2,1)} %get-tuple-element.84), channel_id=1, source_target_pairs={{2,0},{10,1},{0,2},{8,3},{6,4},{14,5},{4,6},{12,7},{3,8},{11,9},{1... | collective-permute-start | bytes 405512 | tf_op jit(solution)/shard_map/ppermute | solution.py:332
  119.2 18.2 %collective-permute-start.25 = (bf16[528,128]{1,0:T(8,128)(2,1)}, bf16[528,128]{1,0:T(8,128)(2,1)S(1)}, u32[]{:S(2)}, u32[]{:S(2)}) collective-permute-start(bf16[528,128]{1,0:T(8,128)(2,1)} %get-tuple-element.85), channel_id=1, source_target_pairs={{4,0},{12,1},{6,2},{14,3},{0,4},{8,5},{2,6},{10,7},{5,8},{13,9},{7... | collective-permute-start | bytes 405512 | tf_op jit(solution)/shard_map/ppermute | solution.py:332
  128.1 16.4 %collective-permute-start.26 = (bf16[528,128]{1,0:T(8,128)(2,1)}, bf16[528,128]{1,0:T(8,128)(2,1)S(1)}, u32[]{:S(2)}, u32[]{:S(2)}) collective-permute-start(bf16[528,128]{1,0:T(8,128)(2,1)} %get-tuple-element.86), channel_id=1, source_target_pairs={{6,0},{14,1},{4,2},{12,3},{2,4},{10,5},{0,6},{8,7},{7,8},{15,9},{5... | collective-permute-start | bytes 405512 | tf_op jit(solution)/shard_map/ppermute | solution.py:332
  128.5 16.0 %collective-permute-start.27 = (bf16[528,128]{1,0:T(8,128)(2,1)}, bf16[528,128]{1,0:T(8,128)(2,1)S(1)}, u32[]{:S(2)}, u32[]{:S(2)}) collective-permute-start(bf16[528,128]{1,0:T(8,128)(2,1)} %get-tuple-element.87), channel_id=1, source_target_pairs={{1,0},{9,1},{3,2},{11,3},{5,4},{13,5},{7,6},{15,7},{0,8},{8,9},{2,... | collective-permute-start | bytes 405512 | tf_op jit(solution)/shard_map/ppermute | solution.py:332
  133.6 10.9 %collective-permute-start.28 = (bf16[528,128]{1,0:T(8,128)(2,1)}, bf16[528,128]{1,0:T(8,128)(2,1)S(1)}, u32[]{:S(2)}, u32[]{:S(2)}) collective-permute-start(bf16[528,128]{1,0:T(8,128)(2,1)} %get-tuple-element.88), channel_id=1, source_target_pairs={{3,0},{11,1},{1,2},{9,3},{7,4},{15,5},{5,6},{13,7},{2,8},{10,9},{0... | collective-permute-start | bytes 405512 | tf_op jit(solution)/shard_map/ppermute | solution.py:332
  135.1 9.4 %collective-permute-start.29 = (bf16[528,128]{1,0:T(8,128)(2,1)}, bf16[528,128]{1,0:T(8,128)(2,1)S(1)}, u32[]{:S(2)}, u32[]{:S(2)}) collective-permute-start(bf16[528,128]{1,0:T(8,128)(2,1)} %get-tuple-element.89), channel_id=1, source_target_pairs={{5,0},{13,1},{7,2},{15,3},{1,4},{9,5},{3,6},{11,7},{4,8},{12,9},{6... | collective-permute-start | bytes 405512 | tf_op jit(solution)/shard_map/ppermute | solution.py:332
  137.4 14.7 %collective-permute-start.30 = (bf16[528,128]{1,0:T(8,128)(2,1)}, bf16[528,128]{1,0:T(8,128)(2,1)S(1)}, u32[]{:S(2)}, u32[]{:S(2)}) collective-permute-start(bf16[528,128]{1,0:T(8,128)(2,1)} %get-tuple-element.90), channel_id=1, source_target_pairs={{7,0},{15,1},{5,2},{13,3},{3,4},{11,5},{1,6},{9,7},{6,8},{14,9},{4... | collective-permute-start | bytes 405512 | tf_op jit(solution)/shard_map/ppermute | solution.py:332
  (32 other events, 308.9 us)
where the time goes:
time: 157 us; the launch traced here: 156 us
  starting transfers between devices  58.6 us (37%)
  Pallas kernels  51.7 us (33%)
  waiting for transfers between devices  41.4 us (26%)
  local copies, waits for them, and re-layouts  4.38 us (3%)
    pallas_call x5, Pallas kernels, shards(): pl.pallas_call(functools.partial(attend, n_sub, len(buffers), first, last...  39.3 us
    ppermute x23, waiting for transfers between devices, moved(): return lax.ppermute(x, 'shard', pairs)  33.8 us
    ppermute x23, starting transfers between devices, moved(): return lax.ppermute(x, 'shard', pairs)  33.2 us
    ppermute x8, starting transfers between devices, shards(): returned.append(lax.ppermute(part, 'shard', [(b, a) for a, b in pairs]))  25.3 us
    ppermute x8, waiting for transfers between devices, shards(): returned.append(lax.ppermute(part, 'shard', [(b, a) for a, b in pairs]))  7.59 us
    unnamed x66, local copies, waits for them, and re-layouts  3.72 us
    pallas_call x1, Pallas kernels, shards(): pl.pallas_call(functools.partial(merge_own, n_sub, group_size), out_shape...  3.66 us
    pallas_call x1, Pallas kernels, shards(): pl.pallas_call(functools.partial(pack_kv, n_sub), grid=(blk_dev,), out_sh...  3.15 us
  transfers between devices with their start and end apart: 31, of which 6 were waited for; matrix products, arithmetic and copies ran while one was open for 0% of the time, Pallas kernels for 25%

commit v1 on v0

v1 whole, which is shorter than its diff:
```python
import functools
import math

import jax
import jax.numpy as jnp
import numpy as np
from jax import lax
from jax.experimental import pallas as pl
from jax.experimental.pallas import tpu as pltpu
from jax.sharding import PartitionSpec as P


HD = 128
ROPE_BASE = 500000.0
TOP_START = -1e30
MASKED = -3e30
STATS = 16
TAG = 8
NOWHERE = 1 << 28
GRANT = 24 << 20


def tiles_of(width):
    return 2 if width % (4 * HD) == 0 else 1


def chunks_of(sub_heads, rows):
    tiles = tiles_of(sub_heads * rows)
    size = rows // tiles
    for tile in range(tiles):
        for head in range(sub_heads):
            start = (tile * sub_heads + head) * size
            yield head, slice(tile * size, (tile + 1) * size), slice(start, start + size)


VMEM = pltpu.MemorySpace.VMEM
SMEM = pltpu.MemorySpace.SMEM


def frequency_row():
    half = HD // 2
    steps = np.arange(half, dtype=np.float32)
    row = np.exp((-math.log(ROPE_BASE) * steps / half).astype(np.float32)).astype(np.float32)
    return np.concatenate([row, row])[None, :]


def signed(sine):
    lane = lax.broadcasted_iota(jnp.int32, sine.shape, len(sine.shape) - 1)
    return jnp.where(lane < HD // 2, -sine, sine)


def turn(vectors, cosine, sine):
    wide = vectors.astype(jnp.float32)
    return (wide * cosine + pltpu.roll(wide, HD // 2, 1) * sine).astype(jnp.bfloat16)


def find_block(block_id, lengths_ref):
    start = jnp.int32(0)
    request = jnp.int32(0)
    position = jnp.int32(0)
    for q in range(lengths_ref.shape[0]):
        end = start + lengths_ref[q]
        inside = (block_id >= start) & (block_id < end)
        request = jnp.where(inside, q, request)
        position = jnp.where(inside, block_id - start, position)
        start = end
    return request, position


def pack_kv(n_sub, order_ref, lengths_ref, freq_ref, kv_ref, *out_refs):
    heads = len(out_refs)
    my_head = lax.axis_index("shard") // n_sub
    block_len = kv_ref.shape[1]
    block_id = order_ref[pl.program_id(0)]
    request, position = find_block(block_id, lengths_ref)
    left = lax.broadcasted_iota(jnp.int32, (TAG, 2 * HD), 1) < HD
    tag = jnp.where(left, request, position).astype(jnp.float32).astype(jnp.bfloat16)
    angle = (position * block_len).astype(jnp.float32) * freq_ref[...]
    cosine, sine = jnp.cos(angle), signed(jnp.sin(angle))
    for mask in range(heads):
        column = pl.multiple_of((my_head ^ mask) * (2 * HD), 2 * HD)
        out_refs[mask][0, :block_len, :HD] = turn(kv_ref[0, :, pl.ds(column, HD)], cosine, sine)
        out_refs[mask][0, :block_len, HD:] = kv_ref[0, :, pl.ds(column + HD, HD)]
        out_refs[mask][0, block_len:, :] = tag


def pack_queries(n_sub, group_size, freq_ref, rows_ref, queries_ref, fresh_ref, *refs):
    out_refs, key_ref, wide_ref, cos_ref, sin_ref = refs[:-4], refs[-4], refs[-3], refs[-2], refs[-1]
    request = lax.axis_index("shard") // n_sub
    rows = queries_ref.shape[0]
    kv_local = fresh_ref.shape[1] // (2 * HD)
    sub_heads = group_size // n_sub
    position = rows_ref[pl.ds(request, 1), :].astype(jnp.float32)
    angle = jnp.transpose(jnp.broadcast_to(position, (HD, rows))) * freq_ref[...]
    cos_ref[...] = jnp.cos(angle)
    sin_ref[...] = signed(jnp.sin(angle))
    for step, out_ref in enumerate(out_refs):
        kv_id = (step % kv_local) ^ (request % kv_local)
        sub = (step // kv_local) ^ (request // kv_local)
        for head, row_part, flat in chunks_of(sub_heads, rows):
            column = pl.multiple_of((kv_id * group_size + sub * sub_heads + head) * HD, HD)
            out_ref[flat, :] = turn(queries_ref[row_part, pl.ds(column, HD)], cos_ref[row_part, :], sin_ref[row_part, :])
    for kv_id in range(kv_local):
        key_ref[kv_id] = turn(fresh_ref[:, 2 * kv_id * HD : (2 * kv_id + 1) * HD], cos_ref[...], sin_ref[...])
    tiles = tiles_of(sub_heads * rows)
    size = rows // tiles
    n_req = rows_ref.shape[0]
    for tile in range(tiles):
        wide = jnp.concatenate([rows_ref[:, tile * size : (tile + 1) * size]] * sub_heads, axis=1)
        for r in range(n_req):
            wide_ref[tile * n_req + r] = wide[r : r + 1]


def attend(n_sub, n_buf, first, last, blk_dev, rows_smem, wide_ref, *refs):
    n_req = rows_smem.shape[0]
    rows = rows_smem.shape[1]
    if first:
        query_refs, refs = refs[:n_req], refs[n_req:]
    kv_refs, refs = refs[:n_buf], refs[n_buf:]
    if not first:
        refs = refs[3:]
    if last:
        out_refs, refs = refs[:n_req], refs[n_req:]
    acc_ref, top_ref, query_buf, kv_buf, score_a, score_b, best_a, best_b, item_ref, query_sem, kv_sem = refs
    tiles, half = query_buf.shape[1:3]
    query_copies = [
        pltpu.make_async_copy(ref.at[pl.ds(tile * half, half)], query_buf.at[i, tile], query_sem.at[i, tile])
        for i, ref in enumerate(query_refs)
        for tile in range(tiles)
    ] if first else []
    kv_copies = [
        pltpu.make_async_copy(ref, kv_buf.at[pl.ds(i * blk_dev, blk_dev)], kv_sem.at[i]) for i, ref in enumerate(kv_refs)
    ]
    for copy in kv_copies + query_copies:
        copy.start()
    me = lax.axis_index("shard")
    my_head, my_sub = me // n_sub, me % n_sub
    kv_local = n_req // n_sub
    mixed = my_sub * kv_local + my_head % kv_local
    block_len = kv_buf.shape[1] - TAG
    if first:
        acc_ref[...] = jnp.zeros_like(acc_ref)
        top_ref[...] = jnp.full_like(top_ref, TOP_START)
    for copy in kv_copies:
        copy.wait()
    count = jnp.int32(0)
    for i in range(n_buf * blk_dev):
        tag = kv_buf[i, block_len:, :].astype(jnp.float32)
        request = jnp.max(tag[:, :HD]).astype(jnp.int32)
        offset = jnp.max(tag[:, HD:]).astype(jnp.int32) * block_len
        for tile in reversed(range(tiles)):
            item_ref[0, count] = i
            item_ref[1, count] = request
            item_ref[2, count] = tile
            item_ref[3, count] = offset
            used = rows_smem[request, (tile + 1) * (rows // tiles) - 1] > offset
            count = count + jnp.where(used, 1, 0)
    for pad in range(2):
        item_ref[0, count + pad] = 0
        item_ref[1, count + pad] = 0
        item_ref[2, count + pad] = 0
        item_ref[3, count + pad] = NOWHERE
    for copy in query_copies:
        copy.wait()
    scale = math.log2(math.e) / math.sqrt(HD)
    token = lax.broadcasted_iota(jnp.int32, (block_len, half), 0)

    def score(item, score_ref, best_ref):
        i, request, tile = item_ref[0, item], item_ref[1, item], item_ref[2, item]
        scores = lax.dot_general(
            kv_buf[i, :block_len, :HD],
            query_buf[request ^ mixed, tile],
            (((1,), (1,)), ((), ())),
            preferred_element_type=jnp.float32,
        )
        limit = wide_ref[tile * n_req + request] - item_ref[3, item]
        scores = jnp.where(token < limit, scores * scale, MASKED)
        score_ref[...] = scores
        best_ref[...] = jnp.max(scores, axis=0, keepdims=True)

    def add(item, score_ref, best_ref):
        i = item_ref[0, item]
        place = item_ref[2, item] * n_req + item_ref[1, item]
        old_top = top_ref[place]
        new_top = jnp.maximum(old_top, best_ref[...])
        factor = jnp.exp2(old_top - new_top)
        weights = jnp.exp2(score_ref[...] - new_top).astype(jnp.bfloat16)
        values = jnp.concatenate(
            [jnp.transpose(kv_buf[i, :block_len, HD:]), jnp.ones((STATS, block_len), jnp.bfloat16)], axis=0
        )
        summed = jnp.dot(values, weights, preferred_element_type=jnp.float32)
        acc_ref[place] = acc_ref[place] * factor + summed[: HD + 8]
        top_ref[place] = new_top

    score(0, score_a, best_a)

    def two_items(j, carried):
        score(2 * j + 1, score_b, best_b)
        add(2 * j, score_a, best_a)
        score(2 * j + 2, score_a, best_a)
        add(2 * j + 1, score_b, best_b)
        return carried

    lax.fori_loop(0, (count + 1) // 2, two_items, 0)

    if last:
        for step, out_ref in enumerate(out_refs):
            request = step ^ mixed
            levels = []
            for tile in range(tiles):
                place = tile * n_req + request
                total = acc_ref[place, HD : HD + 1]
                some = total > 0.0
                safe = jnp.where(some, total, 1.0)
                result = acc_ref[place, :HD] * (1.0 / safe)
                out_ref[tile * half : (tile + 1) * half, :] = jnp.transpose(result).astype(jnp.bfloat16)
                level = jnp.where(some, top_ref[place] + jnp.log2(safe), TOP_START)
                levels += [level[:, at * HD : (at + 1) * HD] for at in range(half // HD)]
            level = jnp.concatenate(levels, axis=0)
            high = level.astype(jnp.bfloat16)
            rest = level - high.astype(jnp.float32)
            middle = rest.astype(jnp.bfloat16)
            low = (rest - middle.astype(jnp.float32)).astype(jnp.bfloat16)
            pieces = [high, middle, low, jnp.zeros((STATS - 3 * len(levels), HD), jnp.bfloat16)]
            out_ref[tiles * half :, :] = jnp.concatenate(pieces, axis=0)


def own_scores(n_sub, group_size, key_ref, *refs):
    query_refs, own_ref = refs[:-1], refs[-1]
    request = lax.axis_index("shard") // n_sub
    kv_local, rows = key_ref.shape[:2]
    sub_heads = group_size // n_sub
    lines = sub_heads * rows // HD
    scale = math.log2(math.e) / math.sqrt(HD)
    own_ref[...] = jnp.zeros_like(own_ref)
    for step, query_ref in enumerate(query_refs):
        own_key = key_ref[(step % kv_local) ^ (request % kv_local)].astype(jnp.float32)
        for head, row_part, flat in chunks_of(sub_heads, rows):
            query = query_ref[flat, :].astype(jnp.float32)
            line, at = step * lines + flat.start // HD, flat.start % HD
            own = jnp.sum(query * own_key[row_part, :], axis=1, keepdims=True) * scale
            own_ref[at : at + own.shape[0], line : line + 1] = own


def merge_own(n_sub, group_size, own_ref, fresh_ref, *refs):
    part_refs, out_ref, level_ref = refs[:-2], refs[-2], refs[-1]
    request = lax.axis_index("shard") // n_sub
    rows = out_ref.shape[0]
    kv_local = fresh_ref.shape[1] // (2 * HD)
    sub_heads = group_size // n_sub
    width = sub_heads * rows
    lines = width // HD
    level_ref[...] = jnp.zeros_like(level_ref)
    for step, part_ref in enumerate(part_refs):
        stats = part_ref[width:, :].astype(jnp.float32)
        level_ref[step * lines : (step + 1) * lines] = stats[:lines] + stats[lines : 2 * lines] + stats[2 * lines : 3 * lines]
    level = jnp.transpose(level_ref[...])
    own = own_ref[...]
    top = jnp.maximum(own, level)
    own_share = jnp.exp2(own - top)
    share = jnp.exp2(level - top)
    norm = 1.0 / (own_share + share)
    own_share, share = own_share * norm, share * norm
    for step, part_ref in enumerate(part_refs):
        kv_id = (step % kv_local) ^ (request % kv_local)
        sub = (step // kv_local) ^ (request // kv_local)
        value_column = pl.multiple_of((2 * kv_id + 1) * HD, HD)
        own_value = fresh_ref[:, pl.ds(value_column, HD)].astype(jnp.float32)
        for head, row_part, flat in chunks_of(sub_heads, rows):
            line, at = step * lines + flat.start // HD, flat.start % HD
            size = flat.stop - flat.start
            part = part_ref[flat, :].astype(jnp.float32)
            column = pl.multiple_of((kv_id * group_size + sub * sub_heads + head) * HD, HD)
            out_ref[row_part, pl.ds(column, HD)] = (
                part * share[at : at + size, line : line + 1]
                + own_value[row_part, :] * own_share[at : at + size, line : line + 1]
            ).astype(jnp.bfloat16)


def moved(x, pairs):
    return lax.ppermute(x, "shard", pairs)


def shards(kv_store, block_order, lengths, row_positions, queries, fresh_rows):
    n_shard = lax.axis_size("shard")
    n_req, rows = row_positions.shape
    n_sub = n_shard // n_req
    blk_dev, block_len, full_width = kv_store.shape
    kv_heads = full_width // (2 * HD)
    kv_local = kv_heads // n_sub
    group_size = queries.shape[1] // (kv_local * HD)
    sub_heads = group_size // n_sub
    width = sub_heads * rows
    tiles = tiles_of(width)
    half_width = width // tiles
    bf16 = jnp.bfloat16
    freq = jnp.asarray(frequency_row())
    spec = functools.partial(pl.BlockSpec, memory_space=VMEM)
    smem = pl.BlockSpec(memory_space=SMEM)
    anywhere = pl.BlockSpec(memory_space=pl.ANY)

    packed = pl.pallas_call(
        functools.partial(pack_queries, n_sub, group_size),
        out_shape=[jax.ShapeDtypeStruct((width, HD), bf16)] * n_req + [
            jax.ShapeDtypeStruct((kv_local, rows, HD), bf16),
            jax.ShapeDtypeStruct((n_req * tiles, 1, width // tiles), jnp.int32),
        ],
        in_specs=[spec()] * 4,
        out_specs=[spec()] * (n_req + 2),
        scratch_shapes=[pltpu.VMEM((rows, HD), jnp.float32)] * 2,
        compiler_params=pltpu.CompilerParams(vmem_limit_bytes=GRANT),
        name="pack_queries",
    )(freq, row_positions, queries, fresh_rows)
    sent_queries, own_key, wide_rows = packed[:n_req], packed[n_req], packed[n_req + 1]

    level_rows = max(HD, n_req * width // HD)
    own = pl.pallas_call(
        functools.partial(own_scores, n_sub, group_size),
        out_shape=jax.ShapeDtypeStruct((rows, level_rows), jnp.float32),
        in_specs=[spec()] * (1 + n_req),
        out_specs=spec(),
        compiler_params=pltpu.CompilerParams(vmem_limit_bytes=GRANT),
        name="own_scores",
    )(own_key, *sent_queries)
    lengths_after = lax.optimization_barrier((lengths, sent_queries[0]))[0]

    packed_kv = pl.pallas_call(
        functools.partial(pack_kv, n_sub),
        grid=(blk_dev,),
        out_shape=[jax.ShapeDtypeStruct((blk_dev, block_len + TAG, 2 * HD), bf16)] * kv_heads,
        in_specs=[smem, smem, pl.BlockSpec((1, HD), lambda i: (0, 0)), pl.BlockSpec((1, block_len, full_width), lambda i: (i, 0, 0))],
        out_specs=[pl.BlockSpec((1, block_len + TAG, 2 * HD), lambda i: (i, 0, 0))] * kv_heads,
        compiler_params=pltpu.CompilerParams(vmem_limit_bytes=GRANT),
        name="pack_kv",
    )(block_order, lengths_after, freq, kv_store)

    to_compute = []
    for step in range(n_req):
        pairs = []
        for request in range(n_req):
            for h in range(n_sub):
                head = kv_local * h + ((step % kv_local) ^ (request % kv_local))
                sub = (step // kv_local) ^ (request // kv_local)
                pairs.append((request * n_sub + h, head * n_sub + sub))
        to_compute.append(pairs)
    held_queries = [moved(x, pairs) for x, pairs in zip(sent_queries, to_compute)]


    def after(x, *others):
        return lax.optimization_barrier((x, *others))[0] if others else x

    def at_head(mask, *others):
        pairs = [(d, ((d // n_sub) ^ mask) * n_sub + d % n_sub) for d in range(n_shard)]
        return packed_kv[0] if mask == 0 else moved(after(packed_kv[mask], *others), pairs)

    def from_sub(mask, back, *others):
        x = landed[mask]
        pairs = [(d, (d // n_sub) * n_sub + (d % n_sub + back) % n_sub) for d in range(n_shard)]
        return x if back == 0 else moved(after(x, *others), pairs)

    half = kv_heads // 2
    groups = [[0], list(range(1, half)), [half, half + 1]] + [[mask] for mask in range(half + 2, kv_heads)]
    landed = {mask: at_head(mask) for mask in range(half + 2)}
    landed[half + 2] = at_head(half + 2, *held_queries)
    state_shapes = [
        pltpu.VMEM((n_req * tiles, HD + 8, half_width), jnp.float32),
        pltpu.VMEM((n_req * tiles, 1, half_width), jnp.float32),
        pltpu.VMEM((n_req, tiles, half_width, HD), bf16),
    ]
    part_shapes = [jax.ShapeDtypeStruct((width + STATS, HD), bf16)] * n_req
    state, older = [], []
    for index, masks in enumerate(groups):
        if index == 1:
            for mask in range(half + 3, kv_heads):
                if mask not in landed:
                    landed[mask] = at_head(mask, landed[half - 1])
        gate = state if index <= 2 else older
        arrived = [from_sub(mask, back, *gate[-1:]) for mask in masks for back in range(n_sub)]
        buffers = [(mask, back) for mask in masks for back in range(n_sub)]
        first, last = index == 0, index == len(groups) - 1
        blocks = len(buffers) * blk_dev
        inputs = [*(held_queries if first else []), *arrived]
        results = pl.pallas_call(
            functools.partial(attend, n_sub, len(buffers), first, last, blk_dev),
            out_shape=(part_shapes if last else []) + state_shapes,
            in_specs=[smem, spec()] + [anywhere] * len(inputs) + [spec()] * len(state),
            out_specs=[spec()] * ((n_req if last else 0) + 3),
            input_output_aliases={2 + len(inputs) + k: (n_req if last else 0) + k for k in range(len(state))},
            scratch_shapes=[
                pltpu.VMEM((blocks, block_len + TAG, 2 * HD), bf16),
                pltpu.VMEM((block_len, half_width), jnp.float32),
                pltpu.VMEM((block_len, half_width), jnp.float32),
                pltpu.VMEM((1, half_width), jnp.float32),
                pltpu.VMEM((1, half_width), jnp.float32),
                pltpu.SMEM((4, blocks * tiles + 2), jnp.int32),
                pltpu.SemaphoreType.DMA((n_req, tiles)),
                pltpu.SemaphoreType.DMA((len(buffers),)),
            ],
            compiler_params=pltpu.CompilerParams(vmem_limit_bytes=GRANT),
        )(row_positions, wide_rows, *inputs, *state)
        older, state = state, list(results)
    returned = []
    for part, pairs in zip(state, to_compute):
        returned.append(lax.ppermute(part, "shard", [(b, a) for a, b in pairs]))

    return pl.pallas_call(
        functools.partial(merge_own, n_sub, group_size),
        out_shape=jax.ShapeDtypeStruct((rows, kv_local * group_size * HD), bf16),
        in_specs=[spec()] * (2 + n_req),
        out_specs=spec(),
        scratch_shapes=[pltpu.VMEM((level_rows, rows), jnp.float32)],
        compiler_params=pltpu.CompilerParams(vmem_limit_bytes=GRANT),
        name="merge_own",
    )(own, fresh_rows, *returned)


def solution(mesh):
    in_specs = (
        P(("groups", "shard"), None, None),
        P(("groups", "shard")),
        P("groups"),
        P("groups", None),
        P("groups", "shard"),
        P("groups", "shard"),
    )
    return jax.shard_map(shards, mesh=mesh, in_specs=in_specs, out_specs=P("groups", "shard"), check_vma=False)
```

time: 157 us -> 141 us (0.90)
  the two profiles are of different devices: /device:TPU:0 before, /device:TPU:11 now
where the time goes in v1:
time: 141 us; the launch traced here: 140 us
  waiting for transfers between devices  71.6 us (51%)
  starting transfers between devices  36.1 us (26%)
  Pallas kernels  26.1 us (19%)
  local copies, waits for them, and re-layouts  6.42 us (5%)
    ppermute x23, waiting for transfers between devices, moved(): return lax.ppermute(x, 'shard', pairs)  52.2 us
    ppermute x23, starting transfers between devices, moved(): return lax.ppermute(x, 'shard', pairs)  26.7 us
    pallas_call x5, Pallas kernels, shards(): pl.pallas_call(functools.partial(attend, n_sub, len(buffers), first, last...  20.8 us
    ppermute x8, waiting for transfers between devices, shards(): returned.append(lax.ppermute(part, 'shard', [(b, a) for a, b in pairs]))  19.4 us
    ppermute x8, starting transfers between devices, shards(): returned.append(lax.ppermute(part, 'shard', [(b, a) for a, b in pairs]))  9.34 us
    unnamed x18, local copies, waits for them, and re-layouts  6.42 us
  transfers between devices with their start and end apart: 31, of which 16 were waited for; matrix products, arithmetic and copies ran while one was open for 0% of the time, Pallas kernels for 14%

profile of v1, /device:TPU:11, one launch (start us, length us, event | category | flops | bytes accessed | tf_op | source)
XLA Modules:
  0.0 140.4 jit_solution(16719096492099024862)
XLA Ops:
  1.0 1.2 copy-done.3
  4.4 3.9 %collective-permute-start.5 = (bf16[512,128]{1,0:T(8,128)(2,1)S(1)}, bf16[512,128]{1,0:T(8,128)(2,1)S(1)}, u32[]{:S(2)}, u32[]{:S(2)}) collective-permute-start(bf16[512,128]{1,0:T(8,128)(2,1)S(1)} %get-tuple-element.55.refs_1_), channel_id=1, source_target_pairs={{0,2},{1,10},{2,0},{3,8},{4,6},{5,14},{6,4},{7,12},{8,3},{9,11},{1... | collective-permute-start | bytes 393224 | tf_op jit(solution)/shard_map/ppermute | solution.py:281
  8.3 1.7 %collective-permute-start.7 = (bf16[512,128]{1,0:T(8,128)(2,1)S(1)}, bf16[512,128]{1,0:T(8,128)(2,1)S(1)}, u32[]{:S(2)}, u32[]{:S(2)}) collective-permute-start(bf16[512,128]{1,0:T(8,128)(2,1)S(1)} %get-tuple-element.57.refs_3_), channel_id=1, source_target_pairs={{0,6},{1,14},{2,4},{3,12},{4,2},{5,10},{6,0},{7,8},{8,7},{9,15},{1... | collective-permute-start | bytes 393224 | tf_op jit(solution)/shard_map/ppermute | solution.py:281
  10.0 2.6 %collective-permute-start.9 = (bf16[512,128]{1,0:T(8,128)(2,1)S(1)}, bf16[512,128]{1,0:T(8,128)(2,1)S(1)}, u32[]{:S(2)}, u32[]{:S(2)}) collective-permute-start(bf16[512,128]{1,0:T(8,128)(2,1)S(1)} %get-tuple-element.59.refs_5_), channel_id=1, source_target_pairs={{0,3},{1,11},{2,1},{3,9},{4,7},{5,15},{6,5},{7,13},{8,2},{9,10},{1... | collective-permute-start | bytes 393224 | tf_op jit(solution)/shard_map/ppermute | solution.py:281
  12.6 1.6 %copy-done = bf16[2,256,2048]{2,1,0:T(8,128)(2,1)S(1)} copy-done((bf16[2,256,2048]{2,1,0:T(8,128)(2,1)S(1)}, bf16[2,256,2048]{2,1,0:T(8,128)(2,1)}, u32[]{:S(2)}) %copy-start) | copy-done | bytes 2097176
  15.5 1.5 %pack_kv.1 = (bf16[2,264,256]{2,1,0:T(8,128)(2,1)S(1)}, bf16[2,264,256]{2,1,0:T(8,128)(2,1)S(1)}, bf16[2,264,256]{2,1,0:T(8,128)(2,1)S(1)}, bf16[2,264,256]{2,1,...) custom-call(s32[2]{0:T(128)S(1)} %copy-done.7, ...), custom_call_target="tpu_custom_call" | custom-call | tf_op jit(solution)/shard_map/pack_kv/pallas_call | solution.py:327
  17.1 2.7 %collective-permute-done.7.refs_3_ = bf16[512,128]{1,0:T(8,128)(2,1)S(1)} collective-permute-done((bf16[512,128]{1,0:T(8,128)(2,1)S(1)}, bf16[512,128]{1,0:T(8,128)(2,1)S(1)}, u32[]{:S(2)}, u32[]{:S(2)}) %collective-permute-start.7) | collective-permute-done | bytes 131104 | tf_op jit(solution)/shard_map/ppermute | solution.py:281
  19.8 3.0 %collective-permute-done.8.refs_4_ = bf16[512,128]{1,0:T(8,128)(2,1)S(1)} collective-permute-done((bf16[512,128]{1,0:T(8,128)(2,1)S(1)}, bf16[512,128]{1,0:T(8,128)(2,1)S(1)}, u32[]{:S(2)}, u32[]{:S(2)}) %collective-permute-start.8) | collective-permute-done | bytes 131104 | tf_op jit(solution)/shard_map/ppermute | solution.py:281
  22.8 1.4 collective-permute-done.9.refs_5_
  24.4 1.2 collective-permute-done.10.refs_6_
  25.6 2.1 %collective-permute-start.11 = (bf16[512,128]{1,0:T(8,128)(2,1)S(1)}, bf16[512,128]{1,0:T(8,128)(2,1)S(1)}, u32[]{:S(2)}, u32[]{:S(2)}) collective-permute-start(bf16[512,128]{1,0:T(8,128)(2,1)S(1)} %get-tuple-element.61.refs_7_), channel_id=1, source_target_pairs={{0,7},{1,15},{2,5},{3,13},{4,3},{5,11},{6,1},{7,9},{8,6},{9,14},{1... | collective-permute-start | bytes 393224 | tf_op jit(solution)/shard_map/ppermute | solution.py:281
  27.7 7.6 %collective-permute-done.11.refs_7_ = bf16[512,128]{1,0:T(8,128)(2,1)S(1)} collective-permute-done((bf16[512,128]{1,0:T(8,128)(2,1)S(1)}, bf16[512,128]{1,0:T(8,128)(2,1)S(1)}, u32[]{:S(2)}, u32[]{:S(2)}) %collective-permute-start.11) | collective-permute-done | bytes 131104 | tf_op jit(solution)/shard_map/ppermute | solution.py:281
  35.3 8.5 %collective-permute-start.4 = (bf16[512,128]{1,0:T(8,128)(2,1)S(1)}, bf16[512,128]{1,0:T(8,128)(2,1)S(1)}, u32[]{:S(2)}, u32[]{:S(2)}) collective-permute-start(bf16[512,128]{1,0:T(8,128)(2,1)S(1)} %get-tuple-element.54.refs_0_), channel_id=1, source_target_pairs={{0,0},{1,8},{2,2},{3,10},{4,4},{5,12},{6,6},{7,14},{8,1},{9,9},{10... | collective-permute-start | bytes 393224 | tf_op jit(solution)/shard_map/ppermute | solution.py:281
  43.8 2.7 %collective-permute-done.4.refs_0_ = bf16[512,128]{1,0:T(8,128)(2,1)S(1)} collective-permute-done((bf16[512,128]{1,0:T(8,128)(2,1)S(1)}, bf16[512,128]{1,0:T(8,128)(2,1)S(1)}, u32[]{:S(2)}, u32[]{:S(2)}) %collective-permute-start.4) | collective-permute-done | bytes 131104 | tf_op jit(solution)/shard_map/ppermute | solution.py:281
  46.5 4.6 %shard_map.73 = (f32[16,136,256]{2,1,0:T(8,128)S(1)}, f32[16,1,256]{2,1,0:T(1,128)S(1)}, bf16[8,2,256,128]{3,2,1,0:T(8,128)(2,1)S(1)}) custom-call(s32[8,128]{1,0:T(8,128)S(1)} %copy-done.5, s32[16,1,256]{2,1,0:T(1,128)S(1)} %get-tuple-element.62.wide_ref, bf16[512,128]{1,0:T(8,128)(2,1)S(1)} %collective-permute-done.4.refs_0_, ...), custom_call_target="tpu_custom_call" | custom-call | tf_op jit(solution)/shard_map/pallas_call | solution.py:383
  51.8 3.1 %collective-permute-start.18 = (bf16[2,264,256]{2,1,0:T(8,128)(2,1)S(1)}, bf16[2,264,256]{2,1,0:T(8,128)(2,1)S(1)}, u32[]{:S(2)}, u32[]{:S(2)}) collective-permute-start(bf16[2,264,256]{2,1,0:T(8,128)(2,1)S(1)} %get-tuple-element.79), channel_id=1, source_target_pairs={{0,10},{1,11},{2,8},{3,9},{4,14},{5,15},{6,12},{7,13},{8,2},{9,3},... | collective-permute-start | bytes 811016 | tf_op jit(solution)/shard_map/ppermute | solution.py:281
  55.9 6.1 %shard_map.74 = (f32[16,136,256]{2,1,0:T(8,128)S(1)}, f32[16,1,256]{2,1,0:T(1,128)S(1)}, bf16[8,2,256,128]{3,2,1,0:T(8,128)(2,1)S(1)}) custom-call(s32[8,128]{1,0:T(8,128)S(1)} %copy-done.5, s32[16,1,256]{2,1,0:T(1,128)S(1)} %get-tuple-element.62.wide_ref, ...), custom_call_target="tpu_custom_call", output_to_operand_aliasing={{0}: (8, {}), {1}: (9, {}), {2}: (10, {})} | custom-call | tf_op jit(solution)/shard_map/pallas_call | solution.py:383
  62.0 15.5 %collective-permute-done.18.refs_2_ = bf16[2,264,256]{2,1,0:T(8,128)(2,1)S(1)} collective-permute-done((bf16[2,264,256]{2,1,0:T(8,128)(2,1)S(1)}, bf16[2,264,256]{2,1,0:T(8,128)(2,1)S(1)}, u32[]{:S(2)}, u32[]{:S(2)}) %collective-permute-start.18) | collective-permute-done | bytes 270368 | tf_op jit(solution)/shard_map/ppermute | solution.py:281
  77.5 5.8 %collective-permute-done.2.refs_0_ = bf16[2,264,256]{2,1,0:T(8,128)(2,1)S(1)} collective-permute-done((bf16[2,264,256]{2,1,0:T(8,128)(2,1)S(1)}, bf16[2,264,256]{2,1,0:T(8,128)(2,1)S(1)}, u32[]{:S(2)}, u32[]{:S(2)}) %collective-permute-start.2) | collective-permute-done | bytes 270368 | tf_op jit(solution)/shard_map/ppermute | solution.py:281
  83.8 1.3 collective-permute-start.1
  85.0 11.8 %collective-permute-done.21.refs_0_ = bf16[2,264,256]{2,1,0:T(8,128)(2,1)S(1)} collective-permute-done((bf16[2,264,256]{2,1,0:T(8,128)(2,1)S(1)}, bf16[2,264,256]{2,1,0:T(8,128)(2,1)S(1)}, u32[]{:S(2)}, u32[]{:S(2)}) %collective-permute-start.21) | collective-permute-done | bytes 270368 | tf_op jit(solution)/shard_map/ppermute | solution.py:281
  97.4 4.6 %shard_map.75 = (f32[16,136,256]{2,1,0:T(8,128)S(1)}, f32[16,1,256]{2,1,0:T(1,128)S(1)}, bf16[8,2,256,128]{3,2,1,0:T(8,128)(2,1)S(1)}) custom-call(s32[8,128]{1,0:T(8,128)S(1)} %copy-done.5, s32[16,1,256]{2,1,0:T(1,128)S(1)} %get-tuple-element.62.wide_ref, ...), custom_call_target="tpu_custom_call", output_to_operand_aliasing={{0}: (6, {}), {1}: (7, {}), {2}: (8, {})} | custom-call | tf_op jit(solution)/shard_map/pallas_call | solution.py:383
  103.1 2.6 %shard_map.76 = (f32[16,136,256]{2,1,0:T(8,128)S(1)}, f32[16,1,256]{2,1,0:T(1,128)S(1)}, bf16[8,2,256,128]{3,2,1,0:T(8,128)(2,1)S(1)}) custom-call(s32[8,128]{1,0:T(8,128)S(1)} %copy-done.5, s32[16,1,256]{2,1,0:T(1,128)S(1)} %get-tuple-element.62.wide_ref, ...), custom_call_target="tpu_custom_call", output_to_operand_aliasing={{0}: (4, {}), {1}: (5, {}), {2}: (6, {})} | custom-call | tf_op jit(solution)/shard_map/pallas_call | solution.py:383
  105.7 3.0 %shard_map.77 = (bf16[528,128]{1,0:T(8,128)(2,1)S(1)}, bf16[528,128]{1,0:T(8,128)(2,1)S(1)}, bf16[528,128]{1,0:T(8,128)(2,1)S(1)}, bf16[528,128]{1,0:T(8,128)(2,...) custom-call(s32[8,128]{1,0:T(8,128)S(1)} %copy-done.5, ...), custom_call_target="tpu_custom_call", output_to_operand_aliasing={{8}: (4, {}), {9}: (5, {}), {10}: (6, {})} | custom-call | tf_op jit(solution)/shard_map/pallas_call | solution.py:383
  108.7 1.9 %collective-permute-start.23 = (bf16[528,128]{1,0:T(8,128)(2,1)S(1)}, bf16[528,128]{1,0:T(8,128)(2,1)S(1)}, u32[]{:S(2)}, u32[]{:S(2)}) collective-permute-start(bf16[528,128]{1,0:T(8,128)(2,1)S(1)} %get-tuple-element.93), channel_id=1, source_target_pairs={{0,0},{8,1},{2,2},{10,3},{4,4},{12,5},{6,6},{14,7},{1,8},{9,9},{3,... | collective-permute-start | bytes 405512 | tf_op jit(solution)/shard_map/ppermute | solution.py:404
  110.6 3.7 %collective-permute-start.24 = (bf16[528,128]{1,0:T(8,128)(2,1)S(1)}, bf16[528,128]{1,0:T(8,128)(2,1)S(1)}, u32[]{:S(2)}, u32[]{:S(2)}) collective-permute-start(bf16[528,128]{1,0:T(8,128)(2,1)S(1)} %get-tuple-element.94), channel_id=1, source_target_pairs={{2,0},{10,1},{0,2},{8,3},{6,4},{14,5},{4,6},{12,7},{3,8},{11,9},{1... | collective-permute-start | bytes 405512 | tf_op jit(solution)/shard_map/ppermute | solution.py:404
  116.0 1.7 %collective-permute-done.23.refs_0_ = bf16[528,128]{1,0:T(8,128)(2,1)S(1)} collective-permute-done((bf16[528,128]{1,0:T(8,128)(2,1)S(1)}, bf16[528,128]{1,0:T(8,128)(2,1)S(1)}, u32[]{:S(2)}, u32[]{:S(2)}) %collective-permute-start.23) | collective-permute-done | bytes 135200 | tf_op jit(solution)/shard_map/ppermute | solution.py:404
  117.6 1.6 %collective-permute-start.28 = (bf16[528,128]{1,0:T(8,128)(2,1)S(1)}, bf16[528,128]{1,0:T(8,128)(2,1)S(1)}, u32[]{:S(2)}, u32[]{:S(2)}) collective-permute-start(bf16[528,128]{1,0:T(8,128)(2,1)S(1)} %get-tuple-element.98), channel_id=1, source_target_pairs={{3,0},{11,1},{1,2},{9,3},{7,4},{15,5},{5,6},{13,7},{2,8},{10,9},{0... | collective-permute-start | bytes 405512 | tf_op jit(solution)/shard_map/ppermute | solution.py:404
  120.8 8.9 %collective-permute-done.25.refs_2_ = bf16[528,128]{1,0:T(8,128)(2,1)S(1)} collective-permute-done((bf16[528,128]{1,0:T(8,128)(2,1)S(1)}, bf16[528,128]{1,0:T(8,128)(2,1)S(1)}, u32[]{:S(2)}, u32[]{:S(2)}) %collective-permute-start.25) | collective-permute-done | bytes 135200 | tf_op jit(solution)/shard_map/ppermute | solution.py:404
  130.3 5.1 %collective-permute-done.26.refs_3_ = bf16[528,128]{1,0:T(8,128)(2,1)S(1)} collective-permute-done((bf16[528,128]{1,0:T(8,128)(2,1)S(1)}, bf16[528,128]{1,0:T(8,128)(2,1)S(1)}, u32[]{:S(2)}, u32[]{:S(2)}) %collective-permute-start.26) | collective-permute-done | bytes 135200 | tf_op jit(solution)/shard_map/ppermute | solution.py:404
  135.8 2.2 %collective-permute-done.30.refs_7_ = bf16[528,128]{1,0:T(8,128)(2,1)S(1)} collective-permute-done((bf16[528,128]{1,0:T(8,128)(2,1)S(1)}, bf16[528,128]{1,0:T(8,128)(2,1)S(1)}, u32[]{:S(2)}, u32[]{:S(2)}) %collective-permute-start.30) | collective-permute-done | bytes 135200 | tf_op jit(solution)/shard_map/ppermute | solution.py:404
  138.0 2.3 %merge_own.1 = bf16[128,4096]{1,0:T(8,128)(2,1)} custom-call(f32[128,128]{1,0:T(8,128)S(1)} %own_scores.1.own_ref, bf16[128,1024]{1,0:T(8,128)(2,1)S(1)} %copy-done.2, bf16[528,128]{1,0:T(8,128)(2,1)S(1)} %collective-permute-done.23.refs_0_, bf16[528,128]{1,0:T(8,128)(2,1)S(1)} %collective-permute-done.24.refs_1_, ...), custom_call_target="tpu_custom_call" | custom-call | tf_op jit(solution)/shard_map/merge_own/pallas_call | solution.py:406
  (57 shorter events, 12.9 us)
Async XLA Ops:
  3.5 43.0 %copy-start.5 = (s32[8,128]{1,0:T(8,128)S(1)}, s32[8,128]{1,0:T(8,128)}, u32[]{:S(2)}) copy-start(s32[8,128]{1,0:T(8,128)} %rows_smem.9) | copy-start | bytes 12292
  4.4 8.2 %collective-permute-start.5 = (bf16[512,128]{1,0:T(8,128)(2,1)S(1)}, bf16[512,128]{1,0:T(8,128)(2,1)S(1)}, u32[]{:S(2)}, u32[]{:S(2)}) collective-permute-start(bf16[512,128]{1,0:T(8,128)(2,1)S(1)} %get-tuple-element.55.refs_1_), channel_id=1, source_target_pairs={{0,2},{1,10},{2,0},{3,8},{4,6},{5,14},{6,4},{7,12},{8,3},{9,11},{1... | collective-permute-start | bytes 393224 | tf_op jit(solution)/shard_map/ppermute | solution.py:281
  8.3 8.7 %collective-permute-start.6 = (bf16[512,128]{1,0:T(8,128)(2,1)S(1)}, bf16[512,128]{1,0:T(8,128)(2,1)S(1)}, u32[]{:S(2)}, u32[]{:S(2)}) collective-permute-start(bf16[512,128]{1,0:T(8,128)(2,1)S(1)} %get-tuple-element.56.refs_2_), channel_id=1, source_target_pairs={{0,4},{1,12},{2,6},{3,14},{4,0},{5,8},{6,2},{7,10},{8,5},{9,13},{1... | collective-permute-start | bytes 393224 | tf_op jit(solution)/shard_map/ppermute | solution.py:281
  8.3 11.5 %collective-permute-start.7 = (bf16[512,128]{1,0:T(8,128)(2,1)S(1)}, bf16[512,128]{1,0:T(8,128)(2,1)S(1)}, u32[]{:S(2)}, u32[]{:S(2)}) collective-permute-start(bf16[512,128]{1,0:T(8,128)(2,1)S(1)} %get-tuple-element.57.refs_3_), channel_id=1, source_target_pairs={{0,6},{1,14},{2,4},{3,12},{4,2},{5,10},{6,0},{7,8},{8,7},{9,15},{1... | collective-permute-start | bytes 393224 | tf_op jit(solution)/shard_map/ppermute | solution.py:281
  10.0 12.8 %collective-permute-start.8 = (bf16[512,128]{1,0:T(8,128)(2,1)S(1)}, bf16[512,128]{1,0:T(8,128)(2,1)S(1)}, u32[]{:S(2)}, u32[]{:S(2)}) collective-permute-start(bf16[512,128]{1,0:T(8,128)(2,1)S(1)} %get-tuple-element.58.refs_4_), channel_id=1, source_target_pairs={{0,1},{1,9},{2,3},{3,11},{4,5},{5,13},{6,7},{7,15},{8,0},{9,8},{10... | collective-permute-start | bytes 393224 | tf_op jit(solution)/shard_map/ppermute | solution.py:281
  10.0 14.2 %collective-permute-start.9 = (bf16[512,128]{1,0:T(8,128)(2,1)S(1)}, bf16[512,128]{1,0:T(8,128)(2,1)S(1)}, u32[]{:S(2)}, u32[]{:S(2)}) collective-permute-start(bf16[512,128]{1,0:T(8,128)(2,1)S(1)} %get-tuple-element.59.refs_5_), channel_id=1, source_target_pairs={{0,3},{1,11},{2,1},{3,9},{4,7},{5,15},{6,5},{7,13},{8,2},{9,10},{1... | collective-permute-start | bytes 393224 | tf_op jit(solution)/shard_map/ppermute | solution.py:281
  12.6 13.0 %collective-permute-start.10 = (bf16[512,128]{1,0:T(8,128)(2,1)S(1)}, bf16[512,128]{1,0:T(8,128)(2,1)S(1)}, u32[]{:S(2)}, u32[]{:S(2)}) collective-permute-start(bf16[512,128]{1,0:T(8,128)(2,1)S(1)} %get-tuple-element.60.refs_6_), channel_id=1, source_target_pairs={{0,5},{1,13},{2,7},{3,15},{4,1},{5,9},{6,3},{7,11},{8,4},{9,12},{1... | collective-permute-start | bytes 393224 | tf_op jit(solution)/shard_map/ppermute | solution.py:281
  17.0 29.5 %collective-permute-start.12 = (bf16[2,264,256]{2,1,0:T(8,128)(2,1)S(1)}, bf16[2,264,256]{2,1,0:T(8,128)(2,1)S(1)}, u32[]{:S(2)}, u32[]{:S(2)}) collective-permute-start(bf16[2,264,256]{2,1,0:T(8,128)(2,1)S(1)} %get-tuple-element.69.refs_8_), channel_id=1, source_target_pairs={{0,1},{1,0},{2,3},{3,2},{4,5},{5,4},{6,7},{7,6},{8,9},{9,8},{10,11... | collective-permute-start | bytes 811016 | tf_op jit(solution)/shard_map/ppermute | solution.py:281
  19.8 31.3 %collective-permute-start = (bf16[2,264,256]{2,1,0:T(8,128)(2,1)S(1)}, bf16[2,264,256]{2,1,0:T(8,128)(2,1)S(1)}, u32[]{:S(2)}, u32[]{:S(2)}) collective-permute-start(bf16[2,264,256]{2,1,0:T(8,128)(2,1)S(1)} %get-tuple-element.65), channel_id=1, source_target_pairs={{0,6},{1,7},{2,4},{3,5},{4,2},{5,3},{6,0},{7,1},{8,14},{9,15},{10,... | collective-permute-start | bytes 811016 | tf_op jit(solution)/shard_map/ppermute | solution.py:281
  22.8 28.4 %collective-permute-start.14 = (bf16[2,264,256]{2,1,0:T(8,128)(2,1)S(1)}, bf16[2,264,256]{2,1,0:T(8,128)(2,1)S(1)}, u32[]{:S(2)}, u32[]{:S(2)}) collective-permute-start(bf16[2,264,256]{2,1,0:T(8,128)(2,1)S(1)} %get-tuple-element.72), channel_id=1, source_target_pairs={{0,4},{1,5},{2,6},{3,7},{4,0},{5,1},{6,2},{7,3},{8,12},{9,13},{10,... | collective-permute-start | bytes 811016 | tf_op jit(solution)/shard_map/ppermute | solution.py:281
  24.2 27.0 %collective-permute-start.3 = (bf16[2,264,256]{2,1,0:T(8,128)(2,1)S(1)}, bf16[2,264,256]{2,1,0:T(8,128)(2,1)S(1)}, u32[]{:S(2)}, u32[]{:S(2)}) collective-permute-start(bf16[2,264,256]{2,1,0:T(8,128)(2,1)S(1)} %get-tuple-element.68), channel_id=1, source_target_pairs={{0,2},{1,3},{2,0},{3,1},{4,6},{5,7},{6,4},{7,5},{8,10},{9,11},{10,... | collective-permute-start | bytes 811016 | tf_op jit(solution)/shard_map/ppermute | solution.py:281
  25.6 9.7 %collective-permute-start.11 = (bf16[512,128]{1,0:T(8,128)(2,1)S(1)}, bf16[512,128]{1,0:T(8,128)(2,1)S(1)}, u32[]{:S(2)}, u32[]{:S(2)}) collective-permute-start(bf16[512,128]{1,0:T(8,128)(2,1)S(1)} %get-tuple-element.61.refs_7_), channel_id=1, source_target_pairs={{0,7},{1,15},{2,5},{3,13},{4,3},{5,11},{6,1},{7,9},{8,6},{9,14},{1... | collective-permute-start | bytes 393224 | tf_op jit(solution)/shard_map/ppermute | solution.py:281
  35.3 11.3 %collective-permute-start.4 = (bf16[512,128]{1,0:T(8,128)(2,1)S(1)}, bf16[512,128]{1,0:T(8,128)(2,1)S(1)}, u32[]{:S(2)}, u32[]{:S(2)}) collective-permute-start(bf16[512,128]{1,0:T(8,128)(2,1)S(1)} %get-tuple-element.54.refs_0_), channel_id=1, source_target_pairs={{0,0},{1,8},{2,2},{3,10},{4,4},{5,12},{6,6},{7,14},{8,1},{9,9},{10... | collective-permute-start | bytes 393224 | tf_op jit(solution)/shard_map/ppermute | solution.py:281
  51.1 4.0 %collective-permute-start.13 = (bf16[2,264,256]{2,1,0:T(8,128)(2,1)S(1)}, bf16[2,264,256]{2,1,0:T(8,128)(2,1)S(1)}, u32[]{:S(2)}, u32[]{:S(2)}) collective-permute-start(bf16[2,264,256]{2,1,0:T(8,128)(2,1)S(1)} %collective-permute-done.3.refs_0_), channel_id=1, source_target_pairs={{0,1},{1,0},{2,3},{3,2},{4,5},{5,4},{6,7},{7,6},{8,9},{9,8},{10,11... | collective-permute-start | bytes 811016 | tf_op jit(solution)/shard_map/ppermute | solution.py:281
  51.2 4.7 %collective-permute-start.15 = (bf16[2,264,256]{2,1,0:T(8,128)(2,1)S(1)}, bf16[2,264,256]{2,1,0:T(8,128)(2,1)S(1)}, u32[]{:S(2)}, u32[]{:S(2)}) collective-permute-start(bf16[2,264,256]{2,1,0:T(8,128)(2,1)S(1)} %collective-permute-done.14.refs_2_), channel_id=1, source_target_pairs={{0,1},{1,0},{2,3},{3,2},{4,5},{5,4},{6,7},{7,6},{8,9},{9,8},{10,11... | collective-permute-start | bytes 811016 | tf_op jit(solution)/shard_map/ppermute | solution.py:281
  51.7 4.2 %collective-permute-start.16 = (bf16[2,264,256]{2,1,0:T(8,128)(2,1)S(1)}, bf16[2,264,256]{2,1,0:T(8,128)(2,1)S(1)}, u32[]{:S(2)}, u32[]{:S(2)}) collective-permute-start(bf16[2,264,256]{2,1,0:T(8,128)(2,1)S(1)} %collective-permute-done.refs_4_), channel_id=1, source_target_pairs={{0,1},{1,0},{2,3},{3,2},{4,5},{5,4},{6,7},{7,6},{8,9},{9,8},{10,11... | collective-permute-start | bytes 811016 | tf_op jit(solution)/shard_map/ppermute | solution.py:281
  51.8 25.7 %collective-permute-start.18 = (bf16[2,264,256]{2,1,0:T(8,128)(2,1)S(1)}, bf16[2,264,256]{2,1,0:T(8,128)(2,1)S(1)}, u32[]{:S(2)}, u32[]{:S(2)}) collective-permute-start(bf16[2,264,256]{2,1,0:T(8,128)(2,1)S(1)} %get-tuple-element.79), channel_id=1, source_target_pairs={{0,10},{1,11},{2,8},{3,9},{4,14},{5,15},{6,12},{7,13},{8,2},{9,3},... | collective-permute-start | bytes 811016 | tf_op jit(solution)/shard_map/ppermute | solution.py:281
  54.9 28.4 %collective-permute-start.2 = (bf16[2,264,256]{2,1,0:T(8,128)(2,1)S(1)}, bf16[2,264,256]{2,1,0:T(8,128)(2,1)S(1)}, u32[]{:S(2)}, u32[]{:S(2)}) collective-permute-start(bf16[2,264,256]{2,1,0:T(8,128)(2,1)S(1)} %get-tuple-element.67), channel_id=1, source_target_pairs={{0,8},{1,9},{2,10},{3,11},{4,12},{5,13},{6,14},{7,15},{8,0},{9,1},... | collective-permute-start | bytes 811016 | tf_op jit(solution)/shard_map/ppermute | solution.py:281
  55.1 41.7 %collective-permute-start.21 = (bf16[2,264,256]{2,1,0:T(8,128)(2,1)S(1)}, bf16[2,264,256]{2,1,0:T(8,128)(2,1)S(1)}, u32[]{:S(2)}, u32[]{:S(2)}) collective-permute-start(bf16[2,264,256]{2,1,0:T(8,128)(2,1)S(1)} %get-tuple-element.86), channel_id=1, source_target_pairs={{0,12},{1,13},{2,14},{3,15},{4,8},{5,9},{6,10},{7,11},{8,4},{9,5},... | collective-permute-start | bytes 811016 | tf_op jit(solution)/shard_map/ppermute | solution.py:281
  83.3 14.1 %collective-permute-start.17 = (bf16[2,264,256]{2,1,0:T(8,128)(2,1)S(1)}, bf16[2,264,256]{2,1,0:T(8,128)(2,1)S(1)}, u32[]{:S(2)}, u32[]{:S(2)}) collective-permute-start(bf16[2,264,256]{2,1,0:T(8,128)(2,1)S(1)} %collective-permute-done.2.refs_0_), channel_id=1, source_target_pairs={{0,1},{1,0},{2,3},{3,2},{4,5},{5,4},{6,7},{7,6},{8,9},{9,8},{10,11... | collective-permute-start | bytes 811016 | tf_op jit(solution)/shard_map/ppermute | solution.py:281
  83.7 13.7 %collective-permute-start.19 = (bf16[2,264,256]{2,1,0:T(8,128)(2,1)S(1)}, bf16[2,264,256]{2,1,0:T(8,128)(2,1)S(1)}, u32[]{:S(2)}, u32[]{:S(2)}) collective-permute-start(bf16[2,264,256]{2,1,0:T(8,128)(2,1)S(1)} %collective-permute-done.18.refs_2_), channel_id=1, source_target_pairs={{0,1},{1,0},{2,3},{3,2},{4,5},{5,4},{6,7},{7,6},{8,9},{9,8},{10,11... | collective-permute-start | bytes 811016 | tf_op jit(solution)/shard_map/ppermute | solution.py:281
  83.8 18.8 %collective-permute-start.1 = (bf16[2,264,256]{2,1,0:T(8,128)(2,1)S(1)}, bf16[2,264,256]{2,1,0:T(8,128)(2,1)S(1)}, u32[]{:S(2)}, u32[]{:S(2)}) collective-permute-start(bf16[2,264,256]{2,1,0:T(8,128)(2,1)S(1)} %get-tuple-element.66), channel_id=1, source_target_pairs={{0,14},{1,15},{2,12},{3,13},{4,10},{5,11},{6,8},{7,9},{8,6},{9,7},... | collective-permute-start | bytes 811016 | tf_op jit(solution)/shard_map/ppermute | solution.py:281
  96.8 6.2 %collective-permute-start.22 = (bf16[2,264,256]{2,1,0:T(8,128)(2,1)S(1)}, bf16[2,264,256]{2,1,0:T(8,128)(2,1)S(1)}, u32[]{:S(2)}, u32[]{:S(2)}) collective-permute-start(bf16[2,264,256]{2,1,0:T(8,128)(2,1)S(1)} %collective-permute-done.21.refs_0_), channel_id=1, source_target_pairs={{0,1},{1,0},{2,3},{3,2},{4,5},{5,4},{6,7},{7,6},{8,9},{9,8},{10,11... | collective-permute-start | bytes 811016 | tf_op jit(solution)/shard_map/ppermute | solution.py:281
  102.6 3.1 %collective-permute-start.20 = (bf16[2,264,256]{2,1,0:T(8,128)(2,1)S(1)}, bf16[2,264,256]{2,1,0:T(8,128)(2,1)S(1)}, u32[]{:S(2)}, u32[]{:S(2)}) collective-permute-start(bf16[2,264,256]{2,1,0:T(8,128)(2,1)S(1)} %collective-permute-done.1.refs_0_), channel_id=1, source_target_pairs={{0,1},{1,0},{2,3},{3,2},{4,5},{5,4},{6,7},{7,6},{8,9},{9,8},{10,11... | collective-permute-start | bytes 811016 | tf_op jit(solution)/shard_map/ppermute | solution.py:281
  108.7 9.0 %collective-permute-start.23 = (bf16[528,128]{1,0:T(8,128)(2,1)S(1)}, bf16[528,128]{1,0:T(8,128)(2,1)S(1)}, u32[]{:S(2)}, u32[]{:S(2)}) collective-permute-start(bf16[528,128]{1,0:T(8,128)(2,1)S(1)} %get-tuple-element.93), channel_id=1, source_target_pairs={{0,0},{8,1},{2,2},{10,3},{4,4},{12,5},{6,6},{14,7},{1,8},{9,9},{3,... | collective-permute-start | bytes 405512 | tf_op jit(solution)/shard_map/ppermute | solution.py:404
  110.6 9.8 %collective-permute-start.24 = (bf16[528,128]{1,0:T(8,128)(2,1)S(1)}, bf16[528,128]{1,0:T(8,128)(2,1)S(1)}, u32[]{:S(2)}, u32[]{:S(2)}) collective-permute-start(bf16[528,128]{1,0:T(8,128)(2,1)S(1)} %get-tuple-element.94), channel_id=1, source_target_pairs={{2,0},{10,1},{0,2},{8,3},{6,4},{14,5},{4,6},{12,7},{3,8},{11,9},{1... | collective-permute-start | bytes 405512 | tf_op jit(solution)/shard_map/ppermute | solution.py:404
  114.3 15.4 %collective-permute-start.25 = (bf16[528,128]{1,0:T(8,128)(2,1)S(1)}, bf16[528,128]{1,0:T(8,128)(2,1)S(1)}, u32[]{:S(2)}, u32[]{:S(2)}) collective-permute-start(bf16[528,128]{1,0:T(8,128)(2,1)S(1)} %get-tuple-element.95), channel_id=1, source_target_pairs={{4,0},{12,1},{6,2},{14,3},{0,4},{8,5},{2,6},{10,7},{5,8},{13,9},{7... | collective-permute-start | bytes 405512 | tf_op jit(solution)/shard_map/ppermute | solution.py:404
  115.3 20.1 %collective-permute-start.26 = (bf16[528,128]{1,0:T(8,128)(2,1)S(1)}, bf16[528,128]{1,0:T(8,128)(2,1)S(1)}, u32[]{:S(2)}, u32[]{:S(2)}) collective-permute-start(bf16[528,128]{1,0:T(8,128)(2,1)S(1)} %get-tuple-element.96), channel_id=1, source_target_pairs={{6,0},{14,1},{4,2},{12,3},{2,4},{10,5},{0,6},{8,7},{7,8},{15,9},{5... | collective-permute-start | bytes 405512 | tf_op jit(solution)/shard_map/ppermute | solution.py:404
  115.9 19.5 %collective-permute-start.27 = (bf16[528,128]{1,0:T(8,128)(2,1)S(1)}, bf16[528,128]{1,0:T(8,128)(2,1)S(1)}, u32[]{:S(2)}, u32[]{:S(2)}) collective-permute-start(bf16[528,128]{1,0:T(8,128)(2,1)S(1)} %get-tuple-element.97), channel_id=1, source_target_pairs={{1,0},{9,1},{3,2},{11,3},{5,4},{13,5},{7,6},{15,7},{0,8},{8,9},{2,... | collective-permute-start | bytes 405512 | tf_op jit(solution)/shard_map/ppermute | solution.py:404
  117.6 17.8 %collective-permute-start.28 = (bf16[528,128]{1,0:T(8,128)(2,1)S(1)}, bf16[528,128]{1,0:T(8,128)(2,1)S(1)}, u32[]{:S(2)}, u32[]{:S(2)}) collective-permute-start(bf16[528,128]{1,0:T(8,128)(2,1)S(1)} %get-tuple-element.98), channel_id=1, source_target_pairs={{3,0},{11,1},{1,2},{9,3},{7,4},{15,5},{5,6},{13,7},{2,8},{10,9},{0... | collective-permute-start | bytes 405512 | tf_op jit(solution)/shard_map/ppermute | solution.py:404
  120.4 15.4 %collective-permute-start.29 = (bf16[528,128]{1,0:T(8,128)(2,1)S(1)}, bf16[528,128]{1,0:T(8,128)(2,1)S(1)}, u32[]{:S(2)}, u32[]{:S(2)}) collective-permute-start(bf16[528,128]{1,0:T(8,128)(2,1)S(1)} %get-tuple-element.99), channel_id=1, source_target_pairs={{5,0},{13,1},{7,2},{15,3},{1,4},{9,5},{3,6},{11,7},{4,8},{12,9},{6... | collective-permute-start | bytes 405512 | tf_op jit(solution)/shard_map/ppermute | solution.py:404
  129.7 8.3 %collective-permute-start.30 = (bf16[528,128]{1,0:T(8,128)(2,1)S(1)}, bf16[528,128]{1,0:T(8,128)(2,1)S(1)}, u32[]{:S(2)}, u32[]{:S(2)}) collective-permute-start(bf16[528,128]{1,0:T(8,128)(2,1)S(1)} %get-tuple-element.100), channel_id=1, source_target_pairs={{7,0},{15,1},{5,2},{13,3},{3,4},{11,5},{1,6},{9,7},{6,8},{14,9},{4... | collective-permute-start | bytes 405512 | tf_op jit(solution)/shard_map/ppermute | solution.py:404
  (8 other events, 38.8 us)

commit v2 on v1

--- a/solution.py
+++ b/solution.py
@@ -3,7 +3,6 @@
 
 import jax
 import jax.numpy as jnp
-import numpy as np
 from jax import lax
 from jax.experimental import pallas as pl
 from jax.experimental.pallas import tpu as pltpu
@@ -37,11 +36,10 @@
 SMEM = pltpu.MemorySpace.SMEM
 
 
-def frequency_row():
+def frequencies():
     half = HD // 2
-    steps = np.arange(half, dtype=np.float32)
-    row = np.exp((-math.log(ROPE_BASE) * steps / half).astype(np.float32)).astype(np.float32)
-    return np.concatenate([row, row])[None, :]
+    steps = lax.broadcasted_iota(jnp.int32, (1, HD), 1) % half
+    return jnp.exp(-math.log(ROPE_BASE) * steps.astype(jnp.float32) / half)
 
 
 def signed(sine):
@@ -67,48 +65,59 @@
     return request, position
 
 
-def pack_kv(n_sub, order_ref, lengths_ref, freq_ref, kv_ref, *out_refs):
+def pack_kv(n_sub, order_ref, lengths_ref, kv_ref, *refs):
+    out_refs, buf, sem = refs[:-2], refs[-2], refs[-1]
     heads = len(out_refs)
+    slots = buf.shape[0]
+    copies = [pltpu.make_async_copy(kv_ref.at[slot], buf.at[slot], sem.at[slot]) for slot in range(slots)]
+    for copy in copies:
+        copy.start()
     my_head = lax.axis_index("shard") // n_sub
-    block_len = kv_ref.shape[1]
-    block_id = order_ref[pl.program_id(0)]
-    request, position = find_block(block_id, lengths_ref)
+    block_len = buf.shape[1]
     left = lax.broadcasted_iota(jnp.int32, (TAG, 2 * HD), 1) < HD
-    tag = jnp.where(left, request, position).astype(jnp.float32).astype(jnp.bfloat16)
-    angle = (position * block_len).astype(jnp.float32) * freq_ref[...]
-    cosine, sine = jnp.cos(angle), signed(jnp.sin(angle))
-    for mask in range(heads):
-        column = pl.multiple_of((my_head ^ mask) * (2 * HD), 2 * HD)
-        out_refs[mask][0, :block_len, :HD] = turn(kv_ref[0, :, pl.ds(column, HD)], cosine, sine)
-        out_refs[mask][0, :block_len, HD:] = kv_ref[0, :, pl.ds(column + HD, HD)]
-        out_refs[mask][0, block_len:, :] = tag
-
-
-def pack_queries(n_sub, group_size, freq_ref, rows_ref, queries_ref, fresh_ref, *refs):
-    out_refs, key_ref, wide_ref, cos_ref, sin_ref = refs[:-4], refs[-4], refs[-3], refs[-2], refs[-1]
+    for slot in range(slots):
+        request, position = find_block(order_ref[slot], lengths_ref)
+        tag = jnp.where(left, request, position).astype(jnp.float32).astype(jnp.bfloat16)
+        angle = (position * block_len).astype(jnp.float32) * frequencies()
+        cosine, sine = jnp.cos(angle), signed(jnp.sin(angle))
+        copies[slot].wait()
+        for mask in range(heads):
+            column = pl.multiple_of((my_head ^ mask) * (2 * HD), 2 * HD)
+            out_refs[mask][slot, :block_len, :HD] = turn(buf[slot, :, pl.ds(column, HD)], cosine, sine)
+            out_refs[mask][slot, :block_len, HD:] = buf[slot, :, pl.ds(column + HD, HD)]
+            out_refs[mask][slot, block_len:, :] = tag
+
+
+def row_turns(row):
+    angle = jnp.transpose(jnp.broadcast_to(row.astype(jnp.float32), (HD, row.shape[1]))) * frequencies()
+    return jnp.cos(angle), signed(jnp.sin(angle))
+
+
+def pack_queries(n_sub, group_size, rows_ref, queries_ref, *refs):
+    out_refs, (cos_ref, sin_ref, rows_buf, buf, sem) = refs[:-5], refs[-5:]
     request = lax.axis_index("shard") // n_sub
-    rows = queries_ref.shape[0]
-    kv_local = fresh_ref.shape[1] // (2 * HD)
+    kv_local = buf.shape[0]
+    rows = buf.shape[1]
+    span = group_size * HD
+    rows_copy = pltpu.make_async_copy(rows_ref, rows_buf, sem.at[kv_local])
+    rows_copy.start()
+    copies = [
+        pltpu.make_async_copy(queries_ref.at[:, pl.ds(kv_id * span, span)], buf.at[kv_id], sem.at[kv_id])
+        for kv_id in range(kv_local)
+    ]
+    for copy in copies:
+        copy.start()
     sub_heads = group_size // n_sub
-    position = rows_ref[pl.ds(request, 1), :].astype(jnp.float32)
-    angle = jnp.transpose(jnp.broadcast_to(position, (HD, rows))) * freq_ref[...]
-    cos_ref[...] = jnp.cos(angle)
-    sin_ref[...] = signed(jnp.sin(angle))
+    rows_copy.wait()
+    cos_ref[...], sin_ref[...] = row_turns(rows_buf[pl.ds(request, 1), :])
+    for copy in copies:
+        copy.wait()
     for step, out_ref in enumerate(out_refs):
         kv_id = (step % kv_local) ^ (request % kv_local)
         sub = (step // kv_local) ^ (request // kv_local)
         for head, row_part, flat in chunks_of(sub_heads, rows):
-            column = pl.multiple_of((kv_id * group_size + sub * sub_heads + head) * HD, HD)
-            out_ref[flat, :] = turn(queries_ref[row_part, pl.ds(column, HD)], cos_ref[row_part, :], sin_ref[row_part, :])
-    for kv_id in range(kv_local):
-        key_ref[kv_id] = turn(fresh_ref[:, 2 * kv_id * HD : (2 * kv_id + 1) * HD], cos_ref[...], sin_ref[...])
-    tiles = tiles_of(sub_heads * rows)
-    size = rows // tiles
-    n_req = rows_ref.shape[0]
-    for tile in range(tiles):
-        wide = jnp.concatenate([rows_ref[:, tile * size : (tile + 1) * size]] * sub_heads, axis=1)
-        for r in range(n_req):
-            wide_ref[tile * n_req + r] = wide[r : r + 1]
+            column = pl.multiple_of((sub * sub_heads + head) * HD, HD)
+            out_ref[flat, :] = turn(buf[kv_id, row_part, pl.ds(column, HD)], cos_ref[row_part, :], sin_ref[row_part, :])
 
 
 def attend(n_sub, n_buf, first, last, blk_dev, rows_smem, wide_ref, *refs):
@@ -225,21 +234,31 @@
             out_ref[tiles * half :, :] = jnp.concatenate(pieces, axis=0)
 
 
-def own_scores(n_sub, group_size, key_ref, *refs):
-    query_refs, own_ref = refs[:-1], refs[-1]
+def own_scores(n_sub, group_size, rows_ref, fresh_ref, *refs):
+    query_refs, own_ref, wide_ref = refs[:-2], refs[-2], refs[-1]
     request = lax.axis_index("shard") // n_sub
-    kv_local, rows = key_ref.shape[:2]
+    n_req, rows = rows_ref.shape
+    kv_local = fresh_ref.shape[1] // (2 * HD)
     sub_heads = group_size // n_sub
     lines = sub_heads * rows // HD
     scale = math.log2(math.e) / math.sqrt(HD)
     own_ref[...] = jnp.zeros_like(own_ref)
+    cosine, sine = row_turns(rows_ref[pl.ds(request, 1), :])
     for step, query_ref in enumerate(query_refs):
-        own_key = key_ref[(step % kv_local) ^ (request % kv_local)].astype(jnp.float32)
+        kv_id = (step % kv_local) ^ (request % kv_local)
+        column = pl.multiple_of(2 * kv_id * HD, HD)
+        own_key = turn(fresh_ref[:, pl.ds(column, HD)], cosine, sine).astype(jnp.float32)
         for head, row_part, flat in chunks_of(sub_heads, rows):
             query = query_ref[flat, :].astype(jnp.float32)
             line, at = step * lines + flat.start // HD, flat.start % HD
             own = jnp.sum(query * own_key[row_part, :], axis=1, keepdims=True) * scale
             own_ref[at : at + own.shape[0], line : line + 1] = own
+    tiles = tiles_of(sub_heads * rows)
+    size = rows // tiles
+    for tile in range(tiles):
+        wide = jnp.concatenate([rows_ref[:, tile * size : (tile + 1) * size]] * sub_heads, axis=1)
+        for r in range(n_req):
+            wide_ref[tile * n_req + r] = wide[r : r + 1]
 
 
 def merge_own(n_sub, group_size, own_ref, fresh_ref, *refs):
@@ -294,45 +313,49 @@
     tiles = tiles_of(width)
     half_width = width // tiles
     bf16 = jnp.bfloat16
-    freq = jnp.asarray(frequency_row())
     spec = functools.partial(pl.BlockSpec, memory_space=VMEM)
     smem = pl.BlockSpec(memory_space=SMEM)
     anywhere = pl.BlockSpec(memory_space=pl.ANY)
 
-    packed = pl.pallas_call(
+    grant = pltpu.CompilerParams(vmem_limit_bytes=GRANT)
+    sent_queries = pl.pallas_call(
         functools.partial(pack_queries, n_sub, group_size),
-        out_shape=[jax.ShapeDtypeStruct((width, HD), bf16)] * n_req + [
-            jax.ShapeDtypeStruct((kv_local, rows, HD), bf16),
+        out_shape=[jax.ShapeDtypeStruct((width, HD), bf16)] * n_req,
+        in_specs=[anywhere] * 2,
+        out_specs=[spec()] * n_req,
+        scratch_shapes=[
+            pltpu.VMEM((rows, HD), jnp.float32),
+            pltpu.VMEM((rows, HD), jnp.float32),
+            pltpu.VMEM((n_req, rows), jnp.int32),
+            pltpu.VMEM((kv_local, rows, group_size * HD), bf16),
+            pltpu.SemaphoreType.DMA((kv_local + 1,)),
+        ],
+        compiler_params=grant,
+        name="pack_queries",
+    )(row_positions, queries)
+    level_rows = max(HD, n_req * width // HD)
+    own, wide_rows = pl.pallas_call(
+        functools.partial(own_scores, n_sub, group_size),
+        out_shape=[
+            jax.ShapeDtypeStruct((rows, level_rows), jnp.float32),
             jax.ShapeDtypeStruct((n_req * tiles, 1, width // tiles), jnp.int32),
         ],
-        in_specs=[spec()] * 4,
-        out_specs=[spec()] * (n_req + 2),
-        scratch_shapes=[pltpu.VMEM((rows, HD), jnp.float32)] * 2,
-        compiler_params=pltpu.CompilerParams(vmem_limit_bytes=GRANT),
-        name="pack_queries",
-    )(freq, row_positions, queries, fresh_rows)
-    sent_queries, own_key, wide_rows = packed[:n_req], packed[n_req], packed[n_req + 1]
-
-    level_rows = max(HD, n_req * width // HD)
-    own = pl.pallas_call(
-        functools.partial(own_scores, n_sub, group_size),
-        out_shape=jax.ShapeDtypeStruct((rows, level_rows), jnp.float32),
-        in_specs=[spec()] * (1 + n_req),
-        out_specs=spec(),
-        compiler_params=pltpu.CompilerParams(vmem_limit_bytes=GRANT),
+        in_specs=[spec()] * (2 + n_req),
+        out_specs=[spec()] * 2,
+        compiler_params=grant,
         name="own_scores",
-    )(own_key, *sent_queries)
+    )(row_positions, fresh_rows, *sent_queries)
     lengths_after = lax.optimization_barrier((lengths, sent_queries[0]))[0]
 
     packed_kv = pl.pallas_call(
         functools.partial(pack_kv, n_sub),
-        grid=(blk_dev,),
         out_shape=[jax.ShapeDtypeStruct((blk_dev, block_len + TAG, 2 * HD), bf16)] * kv_heads,
-        in_specs=[smem, smem, pl.BlockSpec((1, HD), lambda i: (0, 0)), pl.BlockSpec((1, block_len, full_width), lambda i: (i, 0, 0))],
-        out_specs=[pl.BlockSpec((1, block_len + TAG, 2 * HD), lambda i: (i, 0, 0))] * kv_heads,
-        compiler_params=pltpu.CompilerParams(vmem_limit_bytes=GRANT),
+        in_specs=[smem, smem, anywhere],
+        out_specs=[spec()] * kv_heads,
+        scratch_shapes=[pltpu.VMEM((blk_dev, block_len, full_width), bf16), pltpu.SemaphoreType.DMA((blk_dev,))],
+        compiler_params=grant,
         name="pack_kv",
-    )(block_order, lengths_after, freq, kv_store)
+    )(block_order, lengths_after, kv_store)
 
     to_compute = []
     for step in range(n_req):
@@ -396,12 +419,10 @@
                 pltpu.SemaphoreType.DMA((n_req, tiles)),
                 pltpu.SemaphoreType.DMA((len(buffers),)),
             ],
-            compiler_params=pltpu.CompilerParams(vmem_limit_bytes=GRANT),
+            compiler_params=grant,
         )(row_positions, wide_rows, *inputs, *state)
         older, state = state, list(results)
-    returned = []
-    for part, pairs in zip(state, to_compute):
-        returned.append(lax.ppermute(part, "shard", [(b, a) for a, b in pairs]))
+    returned = [moved(part, [(b, a) for a, b in pairs]) for part, pairs in zip(state, to_compute)]
 
     return pl.pallas_call(
         functools.partial(merge_own, n_sub, group_size),
@@ -409,7 +430,7 @@
         in_specs=[spec()] * (2 + n_req),
         out_specs=spec(),
         scratch_shapes=[pltpu.VMEM((level_rows, rows), jnp.float32)],
-        compiler_params=pltpu.CompilerParams(vmem_limit_bytes=GRANT),
+        compiler_params=grant,
         name="merge_own",
     )(own, fresh_rows, *returned)
 

time: 141 us -> 139 us (0.986)
  local copies, waits for them, and re-layouts: 6.42 us -> 4.82 us
    ppermute x8 -> x0, waiting for transfers between devices: 19.4 us -> none  [shards(): returned.append(lax.ppermute(part, 'shard', [(b, a) for a, b in pairs]))]
    ppermute x23 -> x31, waiting for transfers between devices: 52.2 us -> 70.6 us  [moved(): return lax.ppermute(x, 'shard', pairs)]
    ppermute x8 -> x0, starting transfers between devices: 9.34 us -> none  [shards(): returned.append(lax.ppermute(part, 'shard', [(b, a) for a, b in pairs]))]
    ppermute x23 -> x31, starting transfers between devices: 26.7 us -> 36 us  [moved(): return lax.ppermute(x, 'shard', pairs)]
    unnamed x18 -> x14, local copies, waits for them, and re-layouts: 6.42 us -> 4.82 us
  transfers between devices with their start and end apart: 31 -> 31, of which waited for: 16 -> 16; matrix products, arithmetic and copies ran while one was open for 0% -> 0% of each run, Pallas kernels for 14% -> 15%
where the time goes in v2:
time: 139 us
  waiting for transfers between devices  70.6 us (51%)
  starting transfers between devices  36 us (26%)
  Pallas kernels  27.2 us (20%)
  local copies, waits for them, and re-layouts  4.82 us (3%)
    ppermute x31, waiting for transfers between devices, moved(): return lax.ppermute(x, 'shard', pairs)  70.6 us
    ppermute x31, starting transfers between devices, moved(): return lax.ppermute(x, 'shard', pairs)  36 us
    pallas_call x5, Pallas kernels, shards(): pl.pallas_call(functools.partial(attend, n_sub, len(buffers), first, last...  20.8 us
    unnamed x14, local copies, waits for them, and re-layouts  4.82 us
  transfers between devices with their start and end apart: 31, of which 16 were waited for; matrix products, arithmetic and copies ran while one was open for 0% of the time, Pallas kernels for 15%

profile of v2, /device:TPU:11, one launch (start us, length us, event | category | flops | bytes accessed | tf_op | source)
XLA Modules:
  0.0 138.9 jit_solution(2160616532236165222)
XLA Ops:
  0.0 1.2 copy-done.2
  2.9 3.9 %collective-permute-start.5 = (bf16[512,128]{1,0:T(8,128)(2,1)S(1)}, bf16[512,128]{1,0:T(8,128)(2,1)S(1)}, u32[]{:S(2)}, u32[]{:S(2)}) collective-permute-start(bf16[512,128]{1,0:T(8,128)(2,1)S(1)} %get-tuple-element.54.refs_1_), channel_id=1, source_target_pairs={{0,2},{1,10},{2,0},{3,8},{4,6},{5,14},{6,4},{7,12},{8,3},{9,11},{1... | collective-permute-start | bytes 393224 | tf_op jit(solution)/shard_map/ppermute | solution.py:300
  6.8 1.7 %collective-permute-start.7 = (bf16[512,128]{1,0:T(8,128)(2,1)S(1)}, bf16[512,128]{1,0:T(8,128)(2,1)S(1)}, u32[]{:S(2)}, u32[]{:S(2)}) collective-permute-start(bf16[512,128]{1,0:T(8,128)(2,1)S(1)} %get-tuple-element.56.refs_3_), channel_id=1, source_target_pairs={{0,6},{1,14},{2,4},{3,12},{4,2},{5,10},{6,0},{7,8},{8,7},{9,15},{1... | collective-permute-start | bytes 393224 | tf_op jit(solution)/shard_map/ppermute | solution.py:300
  8.5 2.6 %collective-permute-start.9 = (bf16[512,128]{1,0:T(8,128)(2,1)S(1)}, bf16[512,128]{1,0:T(8,128)(2,1)S(1)}, u32[]{:S(2)}, u32[]{:S(2)}) collective-permute-start(bf16[512,128]{1,0:T(8,128)(2,1)S(1)} %get-tuple-element.58.refs_5_), channel_id=1, source_target_pairs={{0,3},{1,11},{2,1},{3,9},{4,7},{5,15},{6,5},{7,13},{8,2},{9,10},{1... | collective-permute-start | bytes 393224 | tf_op jit(solution)/shard_map/ppermute | solution.py:300
  11.2 1.6 %copy-done = bf16[2,256,2048]{2,1,0:T(8,128)(2,1)S(1)} copy-done((bf16[2,256,2048]{2,1,0:T(8,128)(2,1)S(1)}, bf16[2,256,2048]{2,1,0:T(8,128)(2,1)}, u32[]{:S(2)}) %copy-start) | copy-done | bytes 2097176
  14.1 1.6 %pack_kv.1 = (bf16[2,264,256]{2,1,0:T(8,128)(2,1)S(1)}, bf16[2,264,256]{2,1,0:T(8,128)(2,1)S(1)}, bf16[2,264,256]{2,1,0:T(8,128)(2,1)S(1)}, bf16[2,264,256]{2,1,...) custom-call(s32[2]{0:T(128)S(1)} %copy-done.5, ...), custom_call_target="tpu_custom_call" | custom-call | tf_op jit(solution)/shard_map/pack_kv/pallas_call | solution.py:350
  15.8 2.5 %collective-permute-done.7.refs_3_ = bf16[512,128]{1,0:T(8,128)(2,1)S(1)} collective-permute-done((bf16[512,128]{1,0:T(8,128)(2,1)S(1)}, bf16[512,128]{1,0:T(8,128)(2,1)S(1)}, u32[]{:S(2)}, u32[]{:S(2)}) %collective-permute-start.7) | collective-permute-done | bytes 131104 | tf_op jit(solution)/shard_map/ppermute | solution.py:300
  18.3 3.0 %collective-permute-done.8.refs_4_ = bf16[512,128]{1,0:T(8,128)(2,1)S(1)} collective-permute-done((bf16[512,128]{1,0:T(8,128)(2,1)S(1)}, bf16[512,128]{1,0:T(8,128)(2,1)S(1)}, u32[]{:S(2)}, u32[]{:S(2)}) %collective-permute-start.8) | collective-permute-done | bytes 131104 | tf_op jit(solution)/shard_map/ppermute | solution.py:300
  21.3 1.4 %collective-permute-done.9.refs_5_ = bf16[512,128]{1,0:T(8,128)(2,1)S(1)} collective-permute-done((bf16[512,128]{1,0:T(8,128)(2,1)S(1)}, bf16[512,128]{1,0:T(8,128)(2,1)S(1)}, u32[]{:S(2)}, u32[]{:S(2)}) %collective-permute-start.9) | collective-permute-done | bytes 131104 | tf_op jit(solution)/shard_map/ppermute | solution.py:300
  24.1 2.1 %collective-permute-start.11 = (bf16[512,128]{1,0:T(8,128)(2,1)S(1)}, bf16[512,128]{1,0:T(8,128)(2,1)S(1)}, u32[]{:S(2)}, u32[]{:S(2)}) collective-permute-start(bf16[512,128]{1,0:T(8,128)(2,1)S(1)} %get-tuple-element.60.refs_7_), channel_id=1, source_target_pairs={{0,7},{1,15},{2,5},{3,13},{4,3},{5,11},{6,1},{7,9},{8,6},{9,14},{1... | collective-permute-start | bytes 393224 | tf_op jit(solution)/shard_map/ppermute | solution.py:300
  26.3 7.6 %collective-permute-done.11.refs_7_ = bf16[512,128]{1,0:T(8,128)(2,1)S(1)} collective-permute-done((bf16[512,128]{1,0:T(8,128)(2,1)S(1)}, bf16[512,128]{1,0:T(8,128)(2,1)S(1)}, u32[]{:S(2)}, u32[]{:S(2)}) %collective-permute-start.11) | collective-permute-done | bytes 131104 | tf_op jit(solution)/shard_map/ppermute | solution.py:300
  33.8 8.5 %collective-permute-start.4 = (bf16[512,128]{1,0:T(8,128)(2,1)S(1)}, bf16[512,128]{1,0:T(8,128)(2,1)S(1)}, u32[]{:S(2)}, u32[]{:S(2)}) collective-permute-start(bf16[512,128]{1,0:T(8,128)(2,1)S(1)} %get-tuple-element.53.refs_0_), channel_id=1, source_target_pairs={{0,0},{1,8},{2,2},{3,10},{4,4},{5,12},{6,6},{7,14},{8,1},{9,9},{10... | collective-permute-start | bytes 393224 | tf_op jit(solution)/shard_map/ppermute | solution.py:300
  42.4 1.5 %own_scores.1 = (f32[128,128]{1,0:T(8,128)S(1)}, s32[16,1,256]{2,1,0:T(1,128)S(1)}) custom-call(s32[8,128]{1,0:T(8,128)S(1)} %copy-done.4, bf16[128,1024]{1,0:T(8,128)(2,1)S(1)} %copy-done.1, bf16[512,128]{1,0:T(8,128)(2,1)S(1)} %get-tuple-element.53.refs_0_, bf16[512,128]{1,0:T(8,128)(2,1)S(1)} %get-tuple-element.54.refs_1_, ...), custom_call_target="tpu_custom_call" | custom-call | tf_op jit(solution)/shard_map/own_scores/pallas_call | solution.py:337
  43.8 1.2 collective-permute-done.4.refs_0_
  45.1 4.6 %shard_map.64 = (f32[16,136,256]{2,1,0:T(8,128)S(1)}, f32[16,1,256]{2,1,0:T(1,128)S(1)}, bf16[8,2,256,128]{3,2,1,0:T(8,128)(2,1)S(1)}) custom-call(s32[8,128]{1,0:T(8,128)S(1)} %copy-done.4, s32[16,1,256]{2,1,0:T(1,128)S(1)} %get-tuple-element.62.wide_ref, bf16[512,128]{1,0:T(8,128)(2,1)S(1)} %collective-permute-done.4.refs_0_, ...), custom_call_target="tpu_custom_call" | custom-call | tf_op jit(solution)/shard_map/pallas_call | solution.py:406
  50.3 3.1 %collective-permute-start.18 = (bf16[2,264,256]{2,1,0:T(8,128)(2,1)S(1)}, bf16[2,264,256]{2,1,0:T(8,128)(2,1)S(1)}, u32[]{:S(2)}, u32[]{:S(2)}) collective-permute-start(bf16[2,264,256]{2,1,0:T(8,128)(2,1)S(1)} %get-tuple-element.79), channel_id=1, source_target_pairs={{0,10},{1,11},{2,8},{3,9},{4,14},{5,15},{6,12},{7,13},{8,2},{9,3},... | collective-permute-start | bytes 811016 | tf_op jit(solution)/shard_map/ppermute | solution.py:300
  54.4 6.1 %shard_map.65 = (f32[16,136,256]{2,1,0:T(8,128)S(1)}, f32[16,1,256]{2,1,0:T(1,128)S(1)}, bf16[8,2,256,128]{3,2,1,0:T(8,128)(2,1)S(1)}) custom-call(s32[8,128]{1,0:T(8,128)S(1)} %copy-done.4, s32[16,1,256]{2,1,0:T(1,128)S(1)} %get-tuple-element.62.wide_ref, ...), custom_call_target="tpu_custom_call", output_to_operand_aliasing={{0}: (8, {}), {1}: (9, {}), {2}: (10, {})} | custom-call | tf_op jit(solution)/shard_map/pallas_call | solution.py:406
  60.5 15.5 %collective-permute-done.18.refs_2_ = bf16[2,264,256]{2,1,0:T(8,128)(2,1)S(1)} collective-permute-done((bf16[2,264,256]{2,1,0:T(8,128)(2,1)S(1)}, bf16[2,264,256]{2,1,0:T(8,128)(2,1)S(1)}, u32[]{:S(2)}, u32[]{:S(2)}) %collective-permute-start.18) | collective-permute-done | bytes 270368 | tf_op jit(solution)/shard_map/ppermute | solution.py:300
  76.0 5.8 %collective-permute-done.2.refs_0_ = bf16[2,264,256]{2,1,0:T(8,128)(2,1)S(1)} collective-permute-done((bf16[2,264,256]{2,1,0:T(8,128)(2,1)S(1)}, bf16[2,264,256]{2,1,0:T(8,128)(2,1)S(1)}, u32[]{:S(2)}, u32[]{:S(2)}) %collective-permute-start.2) | collective-permute-done | bytes 270368 | tf_op jit(solution)/shard_map/ppermute | solution.py:300
  82.3 1.3 collective-permute-start.1
  83.6 11.8 %collective-permute-done.21.refs_0_ = bf16[2,264,256]{2,1,0:T(8,128)(2,1)S(1)} collective-permute-done((bf16[2,264,256]{2,1,0:T(8,128)(2,1)S(1)}, bf16[2,264,256]{2,1,0:T(8,128)(2,1)S(1)}, u32[]{:S(2)}, u32[]{:S(2)}) %collective-permute-start.21) | collective-permute-done | bytes 270368 | tf_op jit(solution)/shard_map/ppermute | solution.py:300
  95.9 4.6 %shard_map.66 = (f32[16,136,256]{2,1,0:T(8,128)S(1)}, f32[16,1,256]{2,1,0:T(1,128)S(1)}, bf16[8,2,256,128]{3,2,1,0:T(8,128)(2,1)S(1)}) custom-call(s32[8,128]{1,0:T(8,128)S(1)} %copy-done.4, s32[16,1,256]{2,1,0:T(1,128)S(1)} %get-tuple-element.62.wide_ref, ...), custom_call_target="tpu_custom_call", output_to_operand_aliasing={{0}: (6, {}), {1}: (7, {}), {2}: (8, {})} | custom-call | tf_op jit(solution)/shard_map/pallas_call | solution.py:406
  101.6 2.6 %shard_map.67 = (f32[16,136,256]{2,1,0:T(8,128)S(1)}, f32[16,1,256]{2,1,0:T(1,128)S(1)}, bf16[8,2,256,128]{3,2,1,0:T(8,128)(2,1)S(1)}) custom-call(s32[8,128]{1,0:T(8,128)S(1)} %copy-done.4, s32[16,1,256]{2,1,0:T(1,128)S(1)} %get-tuple-element.62.wide_ref, ...), custom_call_target="tpu_custom_call", output_to_operand_aliasing={{0}: (4, {}), {1}: (5, {}), {2}: (6, {})} | custom-call | tf_op jit(solution)/shard_map/pallas_call | solution.py:406
  104.2 3.0 %shard_map.68 = (bf16[528,128]{1,0:T(8,128)(2,1)S(1)}, bf16[528,128]{1,0:T(8,128)(2,1)S(1)}, bf16[528,128]{1,0:T(8,128)(2,1)S(1)}, bf16[528,128]{1,0:T(8,128)(2,...) custom-call(s32[8,128]{1,0:T(8,128)S(1)} %copy-done.4, ...), custom_call_target="tpu_custom_call", output_to_operand_aliasing={{8}: (4, {}), {9}: (5, {}), {10}: (6, {})} | custom-call | tf_op jit(solution)/shard_map/pallas_call | solution.py:406
  107.2 1.9 %collective-permute-start.23 = (bf16[528,128]{1,0:T(8,128)(2,1)S(1)}, bf16[528,128]{1,0:T(8,128)(2,1)S(1)}, u32[]{:S(2)}, u32[]{:S(2)}) collective-permute-start(bf16[528,128]{1,0:T(8,128)(2,1)S(1)} %get-tuple-element.93), channel_id=1, source_target_pairs={{0,0},{8,1},{2,2},{10,3},{4,4},{12,5},{6,6},{14,7},{1,8},{9,9},{3,... | collective-permute-start | bytes 405512 | tf_op jit(solution)/shard_map/ppermute | solution.py:300
  109.1 3.7 %collective-permute-start.24 = (bf16[528,128]{1,0:T(8,128)(2,1)S(1)}, bf16[528,128]{1,0:T(8,128)(2,1)S(1)}, u32[]{:S(2)}, u32[]{:S(2)}) collective-permute-start(bf16[528,128]{1,0:T(8,128)(2,1)S(1)} %get-tuple-element.94), channel_id=1, source_target_pairs={{2,0},{10,1},{0,2},{8,3},{6,4},{14,5},{4,6},{12,7},{3,8},{11,9},{1... | collective-permute-start | bytes 405512 | tf_op jit(solution)/shard_map/ppermute | solution.py:300
  114.5 1.7 %collective-permute-done.23.refs_0_ = bf16[528,128]{1,0:T(8,128)(2,1)S(1)} collective-permute-done((bf16[528,128]{1,0:T(8,128)(2,1)S(1)}, bf16[528,128]{1,0:T(8,128)(2,1)S(1)}, u32[]{:S(2)}, u32[]{:S(2)}) %collective-permute-start.23) | collective-permute-done | bytes 135200 | tf_op jit(solution)/shard_map/ppermute | solution.py:300
  116.2 1.6 %collective-permute-start.28 = (bf16[528,128]{1,0:T(8,128)(2,1)S(1)}, bf16[528,128]{1,0:T(8,128)(2,1)S(1)}, u32[]{:S(2)}, u32[]{:S(2)}) collective-permute-start(bf16[528,128]{1,0:T(8,128)(2,1)S(1)} %get-tuple-element.98), channel_id=1, source_target_pairs={{3,0},{11,1},{1,2},{9,3},{7,4},{15,5},{5,6},{13,7},{2,8},{10,9},{0... | collective-permute-start | bytes 405512 | tf_op jit(solution)/shard_map/ppermute | solution.py:300
  119.4 8.9 %collective-permute-done.25.refs_2_ = bf16[528,128]{1,0:T(8,128)(2,1)S(1)} collective-permute-done((bf16[528,128]{1,0:T(8,128)(2,1)S(1)}, bf16[528,128]{1,0:T(8,128)(2,1)S(1)}, u32[]{:S(2)}, u32[]{:S(2)}) %collective-permute-start.25) | collective-permute-done | bytes 135200 | tf_op jit(solution)/shard_map/ppermute | solution.py:300
  128.2 5.7 %collective-permute-done.26.refs_3_ = bf16[528,128]{1,0:T(8,128)(2,1)S(1)} collective-permute-done((bf16[528,128]{1,0:T(8,128)(2,1)S(1)}, bf16[528,128]{1,0:T(8,128)(2,1)S(1)}, u32[]{:S(2)}, u32[]{:S(2)}) %collective-permute-start.26) | collective-permute-done | bytes 135200 | tf_op jit(solution)/shard_map/ppermute | solution.py:300
  134.4 2.2 %collective-permute-done.30.refs_7_ = bf16[528,128]{1,0:T(8,128)(2,1)S(1)} collective-permute-done((bf16[528,128]{1,0:T(8,128)(2,1)S(1)}, bf16[528,128]{1,0:T(8,128)(2,1)S(1)}, u32[]{:S(2)}, u32[]{:S(2)}) %collective-permute-start.30) | collective-permute-done | bytes 135200 | tf_op jit(solution)/shard_map/ppermute | solution.py:300
  136.6 2.3 %merge_own.1 = bf16[128,4096]{1,0:T(8,128)(2,1)} custom-call(f32[128,128]{1,0:T(8,128)S(1)} %get-tuple-element.61.own_ref, bf16[128,1024]{1,0:T(8,128)(2,1)S(1)} %copy-done.1, bf16[528,128]{1,0:T(8,128)(2,1)S(1)} %collective-permute-done.23.refs_0_, bf16[528,128]{1,0:T(8,128)(2,1)S(1)} %collective-permute-done.24.refs_1_, ...), custom_call_target="tpu_custom_call" | custom-call | tf_op jit(solution)/shard_map/merge_own/pallas_call | solution.py:427
  (53 shorter events, 12.0 us)
Async XLA Ops:
  1.9 40.4 %copy-start.4 = (s32[8,128]{1,0:T(8,128)S(1)}, s32[8,128]{1,0:T(8,128)}, u32[]{:S(2)}) copy-start(s32[8,128]{1,0:T(8,128)} %rows_smem.9) | copy-start | bytes 12292
  2.9 8.2 %collective-permute-start.5 = (bf16[512,128]{1,0:T(8,128)(2,1)S(1)}, bf16[512,128]{1,0:T(8,128)(2,1)S(1)}, u32[]{:S(2)}, u32[]{:S(2)}) collective-permute-start(bf16[512,128]{1,0:T(8,128)(2,1)S(1)} %get-tuple-element.54.refs_1_), channel_id=1, source_target_pairs={{0,2},{1,10},{2,0},{3,8},{4,6},{5,14},{6,4},{7,12},{8,3},{9,11},{1... | collective-permute-start | bytes 393224 | tf_op jit(solution)/shard_map/ppermute | solution.py:300
  6.8 8.9 %collective-permute-start.6 = (bf16[512,128]{1,0:T(8,128)(2,1)S(1)}, bf16[512,128]{1,0:T(8,128)(2,1)S(1)}, u32[]{:S(2)}, u32[]{:S(2)}) collective-permute-start(bf16[512,128]{1,0:T(8,128)(2,1)S(1)} %get-tuple-element.55.refs_2_), channel_id=1, source_target_pairs={{0,4},{1,12},{2,6},{3,14},{4,0},{5,8},{6,2},{7,10},{8,5},{9,13},{1... | collective-permute-start | bytes 393224 | tf_op jit(solution)/shard_map/ppermute | solution.py:300
  6.8 11.5 %collective-permute-start.7 = (bf16[512,128]{1,0:T(8,128)(2,1)S(1)}, bf16[512,128]{1,0:T(8,128)(2,1)S(1)}, u32[]{:S(2)}, u32[]{:S(2)}) collective-permute-start(bf16[512,128]{1,0:T(8,128)(2,1)S(1)} %get-tuple-element.56.refs_3_), channel_id=1, source_target_pairs={{0,6},{1,14},{2,4},{3,12},{4,2},{5,10},{6,0},{7,8},{8,7},{9,15},{1... | collective-permute-start | bytes 393224 | tf_op jit(solution)/shard_map/ppermute | solution.py:300
  8.5 12.8 %collective-permute-start.8 = (bf16[512,128]{1,0:T(8,128)(2,1)S(1)}, bf16[512,128]{1,0:T(8,128)(2,1)S(1)}, u32[]{:S(2)}, u32[]{:S(2)}) collective-permute-start(bf16[512,128]{1,0:T(8,128)(2,1)S(1)} %get-tuple-element.57.refs_4_), channel_id=1, source_target_pairs={{0,1},{1,9},{2,3},{3,11},{4,5},{5,13},{6,7},{7,15},{8,0},{9,8},{10... | collective-permute-start | bytes 393224 | tf_op jit(solution)/shard_map/ppermute | solution.py:300
  8.5 14.2 %collective-permute-start.9 = (bf16[512,128]{1,0:T(8,128)(2,1)S(1)}, bf16[512,128]{1,0:T(8,128)(2,1)S(1)}, u32[]{:S(2)}, u32[]{:S(2)}) collective-permute-start(bf16[512,128]{1,0:T(8,128)(2,1)S(1)} %get-tuple-element.58.refs_5_), channel_id=1, source_target_pairs={{0,3},{1,11},{2,1},{3,9},{4,7},{5,15},{6,5},{7,13},{8,2},{9,10},{1... | collective-permute-start | bytes 393224 | tf_op jit(solution)/shard_map/ppermute | solution.py:300
  11.2 13.0 %collective-permute-start.10 = (bf16[512,128]{1,0:T(8,128)(2,1)S(1)}, bf16[512,128]{1,0:T(8,128)(2,1)S(1)}, u32[]{:S(2)}, u32[]{:S(2)}) collective-permute-start(bf16[512,128]{1,0:T(8,128)(2,1)S(1)} %get-tuple-element.59.refs_6_), channel_id=1, source_target_pairs={{0,5},{1,13},{2,7},{3,15},{4,1},{5,9},{6,3},{7,11},{8,4},{9,12},{1... | collective-permute-start | bytes 393224 | tf_op jit(solution)/shard_map/ppermute | solution.py:300
  15.7 29.4 %collective-permute-start.12 = (bf16[2,264,256]{2,1,0:T(8,128)(2,1)S(1)}, bf16[2,264,256]{2,1,0:T(8,128)(2,1)S(1)}, u32[]{:S(2)}, u32[]{:S(2)}) collective-permute-start(bf16[2,264,256]{2,1,0:T(8,128)(2,1)S(1)} %get-tuple-element.69.refs_8_), channel_id=1, source_target_pairs={{0,1},{1,0},{2,3},{3,2},{4,5},{5,4},{6,7},{7,6},{8,9},{9,8},{10,11... | collective-permute-start | bytes 811016 | tf_op jit(solution)/shard_map/ppermute | solution.py:300
  18.3 31.4 %collective-permute-start = (bf16[2,264,256]{2,1,0:T(8,128)(2,1)S(1)}, bf16[2,264,256]{2,1,0:T(8,128)(2,1)S(1)}, u32[]{:S(2)}, u32[]{:S(2)}) collective-permute-start(bf16[2,264,256]{2,1,0:T(8,128)(2,1)S(1)} %get-tuple-element.65), channel_id=1, source_target_pairs={{0,6},{1,7},{2,4},{3,5},{4,2},{5,3},{6,0},{7,1},{8,14},{9,15},{10,... | collective-permute-start | bytes 811016 | tf_op jit(solution)/shard_map/ppermute | solution.py:300
  21.3 28.4 %collective-permute-start.14 = (bf16[2,264,256]{2,1,0:T(8,128)(2,1)S(1)}, bf16[2,264,256]{2,1,0:T(8,128)(2,1)S(1)}, u32[]{:S(2)}, u32[]{:S(2)}) collective-permute-start(bf16[2,264,256]{2,1,0:T(8,128)(2,1)S(1)} %get-tuple-element.72), channel_id=1, source_target_pairs={{0,4},{1,5},{2,6},{3,7},{4,0},{5,1},{6,2},{7,3},{8,12},{9,13},{10,... | collective-permute-start | bytes 811016 | tf_op jit(solution)/shard_map/ppermute | solution.py:300
  22.7 27.0 %collective-permute-start.3 = (bf16[2,264,256]{2,1,0:T(8,128)(2,1)S(1)}, bf16[2,264,256]{2,1,0:T(8,128)(2,1)S(1)}, u32[]{:S(2)}, u32[]{:S(2)}) collective-permute-start(bf16[2,264,256]{2,1,0:T(8,128)(2,1)S(1)} %get-tuple-element.68), channel_id=1, source_target_pairs={{0,2},{1,3},{2,0},{3,1},{4,6},{5,7},{6,4},{7,5},{8,10},{9,11},{10,... | collective-permute-start | bytes 811016 | tf_op jit(solution)/shard_map/ppermute | solution.py:300
  24.1 9.7 %collective-permute-start.11 = (bf16[512,128]{1,0:T(8,128)(2,1)S(1)}, bf16[512,128]{1,0:T(8,128)(2,1)S(1)}, u32[]{:S(2)}, u32[]{:S(2)}) collective-permute-start(bf16[512,128]{1,0:T(8,128)(2,1)S(1)} %get-tuple-element.60.refs_7_), channel_id=1, source_target_pairs={{0,7},{1,15},{2,5},{3,13},{4,3},{5,11},{6,1},{7,9},{8,6},{9,14},{1... | collective-permute-start | bytes 393224 | tf_op jit(solution)/shard_map/ppermute | solution.py:300
  33.8 11.2 %collective-permute-start.4 = (bf16[512,128]{1,0:T(8,128)(2,1)S(1)}, bf16[512,128]{1,0:T(8,128)(2,1)S(1)}, u32[]{:S(2)}, u32[]{:S(2)}) collective-permute-start(bf16[512,128]{1,0:T(8,128)(2,1)S(1)} %get-tuple-element.53.refs_0_), channel_id=1, source_target_pairs={{0,0},{1,8},{2,2},{3,10},{4,4},{5,12},{6,6},{7,14},{8,1},{9,9},{10... | collective-permute-start | bytes 393224 | tf_op jit(solution)/shard_map/ppermute | solution.py:300
  49.7 4.0 %collective-permute-start.13 = (bf16[2,264,256]{2,1,0:T(8,128)(2,1)S(1)}, bf16[2,264,256]{2,1,0:T(8,128)(2,1)S(1)}, u32[]{:S(2)}, u32[]{:S(2)}) collective-permute-start(bf16[2,264,256]{2,1,0:T(8,128)(2,1)S(1)} %collective-permute-done.3.refs_0_), channel_id=1, source_target_pairs={{0,1},{1,0},{2,3},{3,2},{4,5},{5,4},{6,7},{7,6},{8,9},{9,8},{10,11... | collective-permute-start | bytes 811016 | tf_op jit(solution)/shard_map/ppermute | solution.py:300
  49.8 4.7 %collective-permute-start.15 = (bf16[2,264,256]{2,1,0:T(8,128)(2,1)S(1)}, bf16[2,264,256]{2,1,0:T(8,128)(2,1)S(1)}, u32[]{:S(2)}, u32[]{:S(2)}) collective-permute-start(bf16[2,264,256]{2,1,0:T(8,128)(2,1)S(1)} %collective-permute-done.14.refs_2_), channel_id=1, source_target_pairs={{0,1},{1,0},{2,3},{3,2},{4,5},{5,4},{6,7},{7,6},{8,9},{9,8},{10,11... | collective-permute-start | bytes 811016 | tf_op jit(solution)/shard_map/ppermute | solution.py:300
  50.3 4.2 %collective-permute-start.16 = (bf16[2,264,256]{2,1,0:T(8,128)(2,1)S(1)}, bf16[2,264,256]{2,1,0:T(8,128)(2,1)S(1)}, u32[]{:S(2)}, u32[]{:S(2)}) collective-permute-start(bf16[2,264,256]{2,1,0:T(8,128)(2,1)S(1)} %collective-permute-done.refs_4_), channel_id=1, source_target_pairs={{0,1},{1,0},{2,3},{3,2},{4,5},{5,4},{6,7},{7,6},{8,9},{9,8},{10,11... | collective-permute-start | bytes 811016 | tf_op jit(solution)/shard_map/ppermute | solution.py:300
  50.3 25.7 %collective-permute-start.18 = (bf16[2,264,256]{2,1,0:T(8,128)(2,1)S(1)}, bf16[2,264,256]{2,1,0:T(8,128)(2,1)S(1)}, u32[]{:S(2)}, u32[]{:S(2)}) collective-permute-start(bf16[2,264,256]{2,1,0:T(8,128)(2,1)S(1)} %get-tuple-element.79), channel_id=1, source_target_pairs={{0,10},{1,11},{2,8},{3,9},{4,14},{5,15},{6,12},{7,13},{8,2},{9,3},... | collective-permute-start | bytes 811016 | tf_op jit(solution)/shard_map/ppermute | solution.py:300
  53.4 28.4 %collective-permute-start.2 = (bf16[2,264,256]{2,1,0:T(8,128)(2,1)S(1)}, bf16[2,264,256]{2,1,0:T(8,128)(2,1)S(1)}, u32[]{:S(2)}, u32[]{:S(2)}) collective-permute-start(bf16[2,264,256]{2,1,0:T(8,128)(2,1)S(1)} %get-tuple-element.67), channel_id=1, source_target_pairs={{0,8},{1,9},{2,10},{3,11},{4,12},{5,13},{6,14},{7,15},{8,0},{9,1},... | collective-permute-start | bytes 811016 | tf_op jit(solution)/shard_map/ppermute | solution.py:300
  53.7 41.7 %collective-permute-start.21 = (bf16[2,264,256]{2,1,0:T(8,128)(2,1)S(1)}, bf16[2,264,256]{2,1,0:T(8,128)(2,1)S(1)}, u32[]{:S(2)}, u32[]{:S(2)}) collective-permute-start(bf16[2,264,256]{2,1,0:T(8,128)(2,1)S(1)} %get-tuple-element.86), channel_id=1, source_target_pairs={{0,12},{1,13},{2,14},{3,15},{4,8},{5,9},{6,10},{7,11},{8,4},{9,5},... | collective-permute-start | bytes 811016 | tf_op jit(solution)/shard_map/ppermute | solution.py:300
  81.8 14.1 %collective-permute-start.17 = (bf16[2,264,256]{2,1,0:T(8,128)(2,1)S(1)}, bf16[2,264,256]{2,1,0:T(8,128)(2,1)S(1)}, u32[]{:S(2)}, u32[]{:S(2)}) collective-permute-start(bf16[2,264,256]{2,1,0:T(8,128)(2,1)S(1)} %collective-permute-done.2.refs_0_), channel_id=1, source_target_pairs={{0,1},{1,0},{2,3},{3,2},{4,5},{5,4},{6,7},{7,6},{8,9},{9,8},{10,11... | collective-permute-start | bytes 811016 | tf_op jit(solution)/shard_map/ppermute | solution.py:300
  82.3 13.7 %collective-permute-start.19 = (bf16[2,264,256]{2,1,0:T(8,128)(2,1)S(1)}, bf16[2,264,256]{2,1,0:T(8,128)(2,1)S(1)}, u32[]{:S(2)}, u32[]{:S(2)}) collective-permute-start(bf16[2,264,256]{2,1,0:T(8,128)(2,1)S(1)} %collective-permute-done.18.refs_2_), channel_id=1, source_target_pairs={{0,1},{1,0},{2,3},{3,2},{4,5},{5,4},{6,7},{7,6},{8,9},{9,8},{10,11... | collective-permute-start | bytes 811016 | tf_op jit(solution)/shard_map/ppermute | solution.py:300
  82.3 18.8 %collective-permute-start.1 = (bf16[2,264,256]{2,1,0:T(8,128)(2,1)S(1)}, bf16[2,264,256]{2,1,0:T(8,128)(2,1)S(1)}, u32[]{:S(2)}, u32[]{:S(2)}) collective-permute-start(bf16[2,264,256]{2,1,0:T(8,128)(2,1)S(1)} %get-tuple-element.66), channel_id=1, source_target_pairs={{0,14},{1,15},{2,12},{3,13},{4,10},{5,11},{6,8},{7,9},{8,6},{9,7},... | collective-permute-start | bytes 811016 | tf_op jit(solution)/shard_map/ppermute | solution.py:300
  95.4 6.2 %collective-permute-start.22 = (bf16[2,264,256]{2,1,0:T(8,128)(2,1)S(1)}, bf16[2,264,256]{2,1,0:T(8,128)(2,1)S(1)}, u32[]{:S(2)}, u32[]{:S(2)}) collective-permute-start(bf16[2,264,256]{2,1,0:T(8,128)(2,1)S(1)} %collective-permute-done.21.refs_0_), channel_id=1, source_target_pairs={{0,1},{1,0},{2,3},{3,2},{4,5},{5,4},{6,7},{7,6},{8,9},{9,8},{10,11... | collective-permute-start | bytes 811016 | tf_op jit(solution)/shard_map/ppermute | solution.py:300
  101.1 3.1 %collective-permute-start.20 = (bf16[2,264,256]{2,1,0:T(8,128)(2,1)S(1)}, bf16[2,264,256]{2,1,0:T(8,128)(2,1)S(1)}, u32[]{:S(2)}, u32[]{:S(2)}) collective-permute-start(bf16[2,264,256]{2,1,0:T(8,128)(2,1)S(1)} %collective-permute-done.1.refs_0_), channel_id=1, source_target_pairs={{0,1},{1,0},{2,3},{3,2},{4,5},{5,4},{6,7},{7,6},{8,9},{9,8},{10,11... | collective-permute-start | bytes 811016 | tf_op jit(solution)/shard_map/ppermute | solution.py:300
  107.2 9.0 %collective-permute-start.23 = (bf16[528,128]{1,0:T(8,128)(2,1)S(1)}, bf16[528,128]{1,0:T(8,128)(2,1)S(1)}, u32[]{:S(2)}, u32[]{:S(2)}) collective-permute-start(bf16[528,128]{1,0:T(8,128)(2,1)S(1)} %get-tuple-element.93), channel_id=1, source_target_pairs={{0,0},{8,1},{2,2},{10,3},{4,4},{12,5},{6,6},{14,7},{1,8},{9,9},{3,... | collective-permute-start | bytes 405512 | tf_op jit(solution)/shard_map/ppermute | solution.py:300
  109.1 9.8 %collective-permute-start.24 = (bf16[528,128]{1,0:T(8,128)(2,1)S(1)}, bf16[528,128]{1,0:T(8,128)(2,1)S(1)}, u32[]{:S(2)}, u32[]{:S(2)}) collective-permute-start(bf16[528,128]{1,0:T(8,128)(2,1)S(1)} %get-tuple-element.94), channel_id=1, source_target_pairs={{2,0},{10,1},{0,2},{8,3},{6,4},{14,5},{4,6},{12,7},{3,8},{11,9},{1... | collective-permute-start | bytes 405512 | tf_op jit(solution)/shard_map/ppermute | solution.py:300
  112.8 15.4 %collective-permute-start.25 = (bf16[528,128]{1,0:T(8,128)(2,1)S(1)}, bf16[528,128]{1,0:T(8,128)(2,1)S(1)}, u32[]{:S(2)}, u32[]{:S(2)}) collective-permute-start(bf16[528,128]{1,0:T(8,128)(2,1)S(1)} %get-tuple-element.95), channel_id=1, source_target_pairs={{4,0},{12,1},{6,2},{14,3},{0,4},{8,5},{2,6},{10,7},{5,8},{13,9},{7... | collective-permute-start | bytes 405512 | tf_op jit(solution)/shard_map/ppermute | solution.py:300
  113.8 20.1 %collective-permute-start.26 = (bf16[528,128]{1,0:T(8,128)(2,1)S(1)}, bf16[528,128]{1,0:T(8,128)(2,1)S(1)}, u32[]{:S(2)}, u32[]{:S(2)}) collective-permute-start(bf16[528,128]{1,0:T(8,128)(2,1)S(1)} %get-tuple-element.96), channel_id=1, source_target_pairs={{6,0},{14,1},{4,2},{12,3},{2,4},{10,5},{0,6},{8,7},{7,8},{15,9},{5... | collective-permute-start | bytes 405512 | tf_op jit(solution)/shard_map/ppermute | solution.py:300
  114.5 19.5 %collective-permute-start.27 = (bf16[528,128]{1,0:T(8,128)(2,1)S(1)}, bf16[528,128]{1,0:T(8,128)(2,1)S(1)}, u32[]{:S(2)}, u32[]{:S(2)}) collective-permute-start(bf16[528,128]{1,0:T(8,128)(2,1)S(1)} %get-tuple-element.97), channel_id=1, source_target_pairs={{1,0},{9,1},{3,2},{11,3},{5,4},{13,5},{7,6},{15,7},{0,8},{8,9},{2,... | collective-permute-start | bytes 405512 | tf_op jit(solution)/shard_map/ppermute | solution.py:300
  116.2 17.8 %collective-permute-start.28 = (bf16[528,128]{1,0:T(8,128)(2,1)S(1)}, bf16[528,128]{1,0:T(8,128)(2,1)S(1)}, u32[]{:S(2)}, u32[]{:S(2)}) collective-permute-start(bf16[528,128]{1,0:T(8,128)(2,1)S(1)} %get-tuple-element.98), channel_id=1, source_target_pairs={{3,0},{11,1},{1,2},{9,3},{7,4},{15,5},{5,6},{13,7},{2,8},{10,9},{0... | collective-permute-start | bytes 405512 | tf_op jit(solution)/shard_map/ppermute | solution.py:300
  118.9 15.4 %collective-permute-start.29 = (bf16[528,128]{1,0:T(8,128)(2,1)S(1)}, bf16[528,128]{1,0:T(8,128)(2,1)S(1)}, u32[]{:S(2)}, u32[]{:S(2)}) collective-permute-start(bf16[528,128]{1,0:T(8,128)(2,1)S(1)} %get-tuple-element.99), channel_id=1, source_target_pairs={{5,0},{13,1},{7,2},{15,3},{1,4},{9,5},{3,6},{11,7},{4,8},{12,9},{6... | collective-permute-start | bytes 405512 | tf_op jit(solution)/shard_map/ppermute | solution.py:300
  128.2 8.3 %collective-permute-start.30 = (bf16[528,128]{1,0:T(8,128)(2,1)S(1)}, bf16[528,128]{1,0:T(8,128)(2,1)S(1)}, u32[]{:S(2)}, u32[]{:S(2)}) collective-permute-start(bf16[528,128]{1,0:T(8,128)(2,1)S(1)} %get-tuple-element.100), channel_id=1, source_target_pairs={{7,0},{15,1},{5,2},{13,3},{3,4},{11,5},{1,6},{9,7},{6,8},{14,9},{4... | collective-permute-start | bytes 405512 | tf_op jit(solution)/shard_map/ppermute | solution.py:300
  (6 other events, 45.2 us)

commit v3 on v2

--- a/solution.py
+++ b/solution.py
@@ -391,14 +391,13 @@
         pltpu.VMEM((n_req, tiles, half_width, HD), bf16),
     ]
     part_shapes = [jax.ShapeDtypeStruct((width + STATS, HD), bf16)] * n_req
-    state, older = [], []
+    state = []
     for index, masks in enumerate(groups):
         if index == 1:
             for mask in range(half + 3, kv_heads):
                 if mask not in landed:
-                    landed[mask] = at_head(mask, landed[half - 1])
-        gate = state if index <= 2 else older
-        arrived = [from_sub(mask, back, *gate[-1:]) for mask in masks for back in range(n_sub)]
+                    landed[mask] = at_head(mask, landed[half])
+        arrived = [from_sub(mask, back, *state[-1:]) for mask in masks for back in range(n_sub)]
         buffers = [(mask, back) for mask in masks for back in range(n_sub)]
         first, last = index == 0, index == len(groups) - 1
         blocks = len(buffers) * blk_dev
@@ -421,7 +420,7 @@
             ],
             compiler_params=grant,
         )(row_positions, wide_rows, *inputs, *state)
-        older, state = state, list(results)
+        state = list(results)
     returned = [moved(part, [(b, a) for a, b in pairs]) for part, pairs in zip(state, to_compute)]
 
     return pl.pallas_call(

time: 139 us -> 142 us (1.022)
  the two profiles are of different devices: /device:TPU:11 before, /device:TPU:0 now
where the time goes in v3:
time: 142 us
  waiting for transfers between devices  59.5 us (42%)
  starting transfers between devices  50.6 us (36%)
  Pallas kernels  26.8 us (19%)
  local copies, waits for them, and re-layouts  4.82 us (3%)
    ppermute x31, waiting for transfers between devices, moved(): return lax.ppermute(x, 'shard', pairs)  59.5 us
    ppermute x31, starting transfers between devices, moved(): return lax.ppermute(x, 'shard', pairs)  50.6 us
    pallas_call x5, Pallas kernels, shards(): pl.pallas_call(functools.partial(attend, n_sub, len(buffers), first, last...  20.3 us
    unnamed x14, local copies, waits for them, and re-layouts  4.82 us
  transfers between devices with their start and end apart: 31, of which 10 were waited for; matrix products, arithmetic and copies ran while one was open for 0% of the time, Pallas kernels for 14%

profile of v3, /device:TPU:0, one launch (start us, length us, event | category | flops | bytes accessed | tf_op | source)
XLA Modules:
  0.0 141.9 jit_solution(4485100406170962273)
XLA Ops:
  0.0 1.2 copy-done.2
  2.9 3.1 %collective-permute-start.3 = (bf16[512,128]{1,0:T(8,128)(2,1)S(1)}, bf16[512,128]{1,0:T(8,128)(2,1)S(1)}, u32[]{:S(2)}, u32[]{:S(2)}) collective-permute-start(bf16[512,128]{1,0:T(8,128)(2,1)S(1)} %get-tuple-element.54.refs_1_), channel_id=1, source_target_pairs={{0,2},{1,10},{2,0},{3,8},{4,6},{5,14},{6,4},{7,12},{8,3},{9,11},{1... | collective-permute-start | bytes 393224 | tf_op jit(solution)/shard_map/ppermute | solution.py:300
  6.0 1.6 %collective-permute-start.4 = (bf16[512,128]{1,0:T(8,128)(2,1)S(1)}, bf16[512,128]{1,0:T(8,128)(2,1)S(1)}, u32[]{:S(2)}, u32[]{:S(2)}) collective-permute-start(bf16[512,128]{1,0:T(8,128)(2,1)S(1)} %get-tuple-element.55.refs_2_), channel_id=1, source_target_pairs={{0,4},{1,12},{2,6},{3,14},{4,0},{5,8},{6,2},{7,10},{8,5},{9,13},{1... | collective-permute-start | bytes 393224 | tf_op jit(solution)/shard_map/ppermute | solution.py:300
  7.6 4.0 %collective-permute-start.6 = (bf16[512,128]{1,0:T(8,128)(2,1)S(1)}, bf16[512,128]{1,0:T(8,128)(2,1)S(1)}, u32[]{:S(2)}, u32[]{:S(2)}) collective-permute-start(bf16[512,128]{1,0:T(8,128)(2,1)S(1)} %get-tuple-element.57.refs_4_), channel_id=1, source_target_pairs={{0,1},{1,9},{2,3},{3,11},{4,5},{5,13},{6,7},{7,15},{8,0},{9,8},{10... | collective-permute-start | bytes 393224 | tf_op jit(solution)/shard_map/ppermute | solution.py:300
  13.7 1.6 %copy-done = bf16[2,256,2048]{2,1,0:T(8,128)(2,1)S(1)} copy-done((bf16[2,256,2048]{2,1,0:T(8,128)(2,1)S(1)}, bf16[2,256,2048]{2,1,0:T(8,128)(2,1)}, u32[]{:S(2)}) %copy-start) | copy-done | bytes 2097176
  16.6 1.6 %pack_kv.1 = (bf16[2,264,256]{2,1,0:T(8,128)(2,1)S(1)}, bf16[2,264,256]{2,1,0:T(8,128)(2,1)S(1)}, bf16[2,264,256]{2,1,0:T(8,128)(2,1)S(1)}, bf16[2,264,256]{2,1,...) custom-call(s32[2]{0:T(128)S(1)} %copy-done.5, ...), custom_call_target="tpu_custom_call" | custom-call | tf_op jit(solution)/shard_map/pack_kv/pallas_call | solution.py:350
  19.1 5.0 %collective-permute-done.6.refs_4_ = bf16[512,128]{1,0:T(8,128)(2,1)S(1)} collective-permute-done((bf16[512,128]{1,0:T(8,128)(2,1)S(1)}, bf16[512,128]{1,0:T(8,128)(2,1)S(1)}, u32[]{:S(2)}, u32[]{:S(2)}) %collective-permute-start.6) | collective-permute-done | bytes 131104 | tf_op jit(solution)/shard_map/ppermute | solution.py:300
  24.1 1.5 %collective-permute-done.7.refs_5_ = bf16[512,128]{1,0:T(8,128)(2,1)S(1)} collective-permute-done((bf16[512,128]{1,0:T(8,128)(2,1)S(1)}, bf16[512,128]{1,0:T(8,128)(2,1)S(1)}, u32[]{:S(2)}, u32[]{:S(2)}) %collective-permute-start.7) | collective-permute-done | bytes 131104 | tf_op jit(solution)/shard_map/ppermute | solution.py:300
  25.6 1.4 collective-permute-start.11
  26.9 11.7 %collective-permute-done.9.refs_7_ = bf16[512,128]{1,0:T(8,128)(2,1)S(1)} collective-permute-done((bf16[512,128]{1,0:T(8,128)(2,1)S(1)}, bf16[512,128]{1,0:T(8,128)(2,1)S(1)}, u32[]{:S(2)}, u32[]{:S(2)}) %collective-permute-start.9) | collective-permute-done | bytes 131104 | tf_op jit(solution)/shard_map/ppermute | solution.py:300
  39.3 1.5 %own_scores.1 = (f32[128,128]{1,0:T(8,128)S(1)}, s32[16,1,256]{2,1,0:T(1,128)S(1)}) custom-call(s32[8,128]{1,0:T(8,128)S(1)} %copy-done.4, bf16[128,1024]{1,0:T(8,128)(2,1)S(1)} %copy-done.1, bf16[512,128]{1,0:T(8,128)(2,1)S(1)} %get-tuple-element.53.refs_0_, bf16[512,128]{1,0:T(8,128)(2,1)S(1)} %get-tuple-element.54.refs_1_, ...), custom_call_target="tpu_custom_call" | custom-call | tf_op jit(solution)/shard_map/own_scores/pallas_call | solution.py:337
  40.8 4.6 %shard_map.64 = (f32[16,136,256]{2,1,0:T(8,128)S(1)}, f32[16,1,256]{2,1,0:T(1,128)S(1)}, bf16[8,2,256,128]{3,2,1,0:T(8,128)(2,1)S(1)}) custom-call(s32[8,128]{1,0:T(8,128)S(1)} %copy-done.4, s32[16,1,256]{2,1,0:T(1,128)S(1)} %get-tuple-element.62.wide_ref, bf16[512,128]{1,0:T(8,128)(2,1)S(1)} %collective-permute-done.2.refs_0_, ...), custom_call_target="tpu_custom_call" | custom-call | tf_op jit(solution)/shard_map/pallas_call | solution.py:405
  45.4 7.6 %collective-permute-start.13 = (bf16[2,264,256]{2,1,0:T(8,128)(2,1)S(1)}, bf16[2,264,256]{2,1,0:T(8,128)(2,1)S(1)}, u32[]{:S(2)}, u32[]{:S(2)}) collective-permute-start(bf16[2,264,256]{2,1,0:T(8,128)(2,1)S(1)} %collective-permute-done.11.refs_0_), channel_id=1, source_target_pairs={{0,1},{1,0},{2,3},{3,2},{4,5},{5,4},{6,7},{7,6},{8,9},{9,8},{10,11... | collective-permute-start | bytes 811016 | tf_op jit(solution)/shard_map/ppermute | solution.py:300
  53.7 3.1 %collective-permute-start = (bf16[2,264,256]{2,1,0:T(8,128)(2,1)S(1)}, bf16[2,264,256]{2,1,0:T(8,128)(2,1)S(1)}, u32[]{:S(2)}, u32[]{:S(2)}) collective-permute-start(bf16[2,264,256]{2,1,0:T(8,128)(2,1)S(1)} %get-tuple-element.65), channel_id=1, source_target_pairs={{0,8},{1,9},{2,10},{3,11},{4,12},{5,13},{6,14},{7,15},{8,0},{9,1},... | collective-permute-start | bytes 811016 | tf_op jit(solution)/shard_map/ppermute | solution.py:300
  56.8 5.1 %shard_map.65 = (f32[16,136,256]{2,1,0:T(8,128)S(1)}, f32[16,1,256]{2,1,0:T(1,128)S(1)}, bf16[8,2,256,128]{3,2,1,0:T(8,128)(2,1)S(1)}) custom-call(s32[8,128]{1,0:T(8,128)S(1)} %copy-done.4, s32[16,1,256]{2,1,0:T(1,128)S(1)} %get-tuple-element.62.wide_ref, ...), custom_call_target="tpu_custom_call", output_to_operand_aliasing={{0}: (8, {}), {1}: (9, {}), {2}: (10, {})} | custom-call | tf_op jit(solution)/shard_map/pallas_call | solution.py:405
  61.9 12.8 %collective-permute-done.19.refs_2_ = bf16[2,264,256]{2,1,0:T(8,128)(2,1)S(1)} collective-permute-done((bf16[2,264,256]{2,1,0:T(8,128)(2,1)S(1)}, bf16[2,264,256]{2,1,0:T(8,128)(2,1)S(1)}, u32[]{:S(2)}, u32[]{:S(2)}) %collective-permute-start.19) | collective-permute-done | bytes 270368 | tf_op jit(solution)/shard_map/ppermute | solution.py:300
  74.8 5.0 %collective-permute-done.refs_0_ = bf16[2,264,256]{2,1,0:T(8,128)(2,1)S(1)} collective-permute-done((bf16[2,264,256]{2,1,0:T(8,128)(2,1)S(1)}, bf16[2,264,256]{2,1,0:T(8,128)(2,1)S(1)}, u32[]{:S(2)}, u32[]{:S(2)}) %collective-permute-start) | collective-permute-done | bytes 270368 | tf_op jit(solution)/shard_map/ppermute | solution.py:300
  80.3 1.8 %collective-permute-start.10 = (bf16[2,264,256]{2,1,0:T(8,128)(2,1)S(1)}, bf16[2,264,256]{2,1,0:T(8,128)(2,1)S(1)}, u32[]{:S(2)}, u32[]{:S(2)}) collective-permute-start(bf16[2,264,256]{2,1,0:T(8,128)(2,1)S(1)} %get-tuple-element.68), channel_id=1, source_target_pairs={{0,12},{1,13},{2,14},{3,15},{4,8},{5,9},{6,10},{7,11},{8,4},{9,5},... | collective-permute-start | bytes 811016 | tf_op jit(solution)/shard_map/ppermute | solution.py:300
  82.2 4.1 %shard_map.66 = (f32[16,136,256]{2,1,0:T(8,128)S(1)}, f32[16,1,256]{2,1,0:T(1,128)S(1)}, bf16[8,2,256,128]{3,2,1,0:T(8,128)(2,1)S(1)}) custom-call(s32[8,128]{1,0:T(8,128)S(1)} %copy-done.4, s32[16,1,256]{2,1,0:T(1,128)S(1)} %get-tuple-element.62.wide_ref, ...), custom_call_target="tpu_custom_call", output_to_operand_aliasing={{0}: (6, {}), {1}: (7, {}), {2}: (8, {})} | custom-call | tf_op jit(solution)/shard_map/pallas_call | solution.py:405
  86.3 4.4 %collective-permute-done.10.refs_0_ = bf16[2,264,256]{2,1,0:T(8,128)(2,1)S(1)} collective-permute-done((bf16[2,264,256]{2,1,0:T(8,128)(2,1)S(1)}, bf16[2,264,256]{2,1,0:T(8,128)(2,1)S(1)}, u32[]{:S(2)}, u32[]{:S(2)}) %collective-permute-start.10) | collective-permute-done | bytes 270368 | tf_op jit(solution)/shard_map/ppermute | solution.py:300
  90.7 2.0 %collective-permute-start.1 = (bf16[2,264,256]{2,1,0:T(8,128)(2,1)S(1)}, bf16[2,264,256]{2,1,0:T(8,128)(2,1)S(1)}, u32[]{:S(2)}, u32[]{:S(2)}) collective-permute-start(bf16[2,264,256]{2,1,0:T(8,128)(2,1)S(1)} %get-tuple-element.66), channel_id=1, source_target_pairs={{0,14},{1,15},{2,12},{3,13},{4,10},{5,11},{6,8},{7,9},{8,6},{9,7},... | collective-permute-start | bytes 811016 | tf_op jit(solution)/shard_map/ppermute | solution.py:300
  92.6 3.1 %shard_map.67 = (f32[16,136,256]{2,1,0:T(8,128)S(1)}, f32[16,1,256]{2,1,0:T(1,128)S(1)}, bf16[8,2,256,128]{3,2,1,0:T(8,128)(2,1)S(1)}) custom-call(s32[8,128]{1,0:T(8,128)S(1)} %copy-done.4, s32[16,1,256]{2,1,0:T(1,128)S(1)} %get-tuple-element.62.wide_ref, ...), custom_call_target="tpu_custom_call", output_to_operand_aliasing={{0}: (4, {}), {1}: (5, {}), {2}: (6, {})} | custom-call | tf_op jit(solution)/shard_map/pallas_call | solution.py:405
  95.7 6.6 %collective-permute-done.1.refs_0_ = bf16[2,264,256]{2,1,0:T(8,128)(2,1)S(1)} collective-permute-done((bf16[2,264,256]{2,1,0:T(8,128)(2,1)S(1)}, bf16[2,264,256]{2,1,0:T(8,128)(2,1)S(1)}, u32[]{:S(2)}, u32[]{:S(2)}) %collective-permute-start.1) | collective-permute-done | bytes 270368 | tf_op jit(solution)/shard_map/ppermute | solution.py:300
  102.3 1.5 %collective-permute-done.22.refs_1_ = bf16[2,264,256]{2,1,0:T(8,128)(2,1)S(1)} collective-permute-done((bf16[2,264,256]{2,1,0:T(8,128)(2,1)S(1)}, bf16[2,264,256]{2,1,0:T(8,128)(2,1)S(1)}, u32[]{:S(2)}, u32[]{:S(2)}) %collective-permute-start.22) | collective-permute-done | bytes 270368 | tf_op jit(solution)/shard_map/ppermute | solution.py:300
  103.9 3.4 %shard_map.68 = (bf16[528,128]{1,0:T(8,128)(2,1)S(1)}, bf16[528,128]{1,0:T(8,128)(2,1)S(1)}, bf16[528,128]{1,0:T(8,128)(2,1)S(1)}, bf16[528,128]{1,0:T(8,128)(2,...) custom-call(s32[8,128]{1,0:T(8,128)S(1)} %copy-done.4, ...), custom_call_target="tpu_custom_call", output_to_operand_aliasing={{8}: (4, {}), {9}: (5, {}), {10}: (6, {})} | custom-call | tf_op jit(solution)/shard_map/pallas_call | solution.py:405
  108.0 1.3 collective-permute-start.24
  109.3 5.8 %collective-permute-start.25 = (bf16[528,128]{1,0:T(8,128)(2,1)S(1)}, bf16[528,128]{1,0:T(8,128)(2,1)S(1)}, u32[]{:S(2)}, u32[]{:S(2)}) collective-permute-start(bf16[528,128]{1,0:T(8,128)(2,1)S(1)} %get-tuple-element.95), channel_id=1, source_target_pairs={{4,0},{12,1},{6,2},{14,3},{0,4},{8,5},{2,6},{10,7},{5,8},{13,9},{7... | collective-permute-start | bytes 405512 | tf_op jit(solution)/shard_map/ppermute | solution.py:300
  115.3 5.5 %collective-permute-start.27 = (bf16[528,128]{1,0:T(8,128)(2,1)S(1)}, bf16[528,128]{1,0:T(8,128)(2,1)S(1)}, u32[]{:S(2)}, u32[]{:S(2)}) collective-permute-start(bf16[528,128]{1,0:T(8,128)(2,1)S(1)} %get-tuple-element.97), channel_id=1, source_target_pairs={{1,0},{9,1},{3,2},{11,3},{5,4},{13,5},{7,6},{15,7},{0,8},{8,9},{2,... | collective-permute-start | bytes 405512 | tf_op jit(solution)/shard_map/ppermute | solution.py:300
  122.0 2.9 %collective-permute-start.29 = (bf16[528,128]{1,0:T(8,128)(2,1)S(1)}, bf16[528,128]{1,0:T(8,128)(2,1)S(1)}, u32[]{:S(2)}, u32[]{:S(2)}) collective-permute-start(bf16[528,128]{1,0:T(8,128)(2,1)S(1)} %get-tuple-element.99), channel_id=1, source_target_pairs={{5,0},{13,1},{7,2},{15,3},{1,4},{9,5},{3,6},{11,7},{4,8},{12,9},{6... | collective-permute-start | bytes 405512 | tf_op jit(solution)/shard_map/ppermute | solution.py:300
  124.9 3.7 %collective-permute-start.30 = (bf16[528,128]{1,0:T(8,128)(2,1)S(1)}, bf16[528,128]{1,0:T(8,128)(2,1)S(1)}, u32[]{:S(2)}, u32[]{:S(2)}) collective-permute-start(bf16[528,128]{1,0:T(8,128)(2,1)S(1)} %get-tuple-element.100), channel_id=1, source_target_pairs={{7,0},{15,1},{5,2},{13,3},{3,4},{11,5},{1,6},{9,7},{6,8},{14,9},{4... | collective-permute-start | bytes 405512 | tf_op jit(solution)/shard_map/ppermute | solution.py:300
  129.0 10.5 %collective-permute-done.30.refs_7_ = bf16[528,128]{1,0:T(8,128)(2,1)S(1)} collective-permute-done((bf16[528,128]{1,0:T(8,128)(2,1)S(1)}, bf16[528,128]{1,0:T(8,128)(2,1)S(1)}, u32[]{:S(2)}, u32[]{:S(2)}) %collective-permute-start.30) | collective-permute-done | bytes 135200 | tf_op jit(solution)/shard_map/ppermute | solution.py:300
  139.6 2.3 %merge_own.1 = bf16[128,4096]{1,0:T(8,128)(2,1)} custom-call(f32[128,128]{1,0:T(8,128)S(1)} %get-tuple-element.61.own_ref, bf16[128,1024]{1,0:T(8,128)(2,1)S(1)} %copy-done.1, bf16[528,128]{1,0:T(8,128)(2,1)S(1)} %collective-permute-done.23.refs_0_, bf16[528,128]{1,0:T(8,128)(2,1)S(1)} %collective-permute-done.24.refs_1_, ...), custom_call_target="tpu_custom_call" | custom-call | tf_op jit(solution)/shard_map/merge_own/pallas_call | solution.py:426
  (53 shorter events, 10.2 us)
Async XLA Ops:
  1.9 37.4 %copy-start.4 = (s32[8,128]{1,0:T(8,128)S(1)}, s32[8,128]{1,0:T(8,128)}, u32[]{:S(2)}) copy-start(s32[8,128]{1,0:T(8,128)} %rows_smem.9) | copy-start | bytes 12292
  2.9 9.8 %collective-permute-start.3 = (bf16[512,128]{1,0:T(8,128)(2,1)S(1)}, bf16[512,128]{1,0:T(8,128)(2,1)S(1)}, u32[]{:S(2)}, u32[]{:S(2)}) collective-permute-start(bf16[512,128]{1,0:T(8,128)(2,1)S(1)} %get-tuple-element.54.refs_1_), channel_id=1, source_target_pairs={{0,2},{1,10},{2,0},{3,8},{4,6},{5,14},{6,4},{7,12},{8,3},{9,11},{1... | collective-permute-start | bytes 393224 | tf_op jit(solution)/shard_map/ppermute | solution.py:300
  6.0 12.2 %collective-permute-start.4 = (bf16[512,128]{1,0:T(8,128)(2,1)S(1)}, bf16[512,128]{1,0:T(8,128)(2,1)S(1)}, u32[]{:S(2)}, u32[]{:S(2)}) collective-permute-start(bf16[512,128]{1,0:T(8,128)(2,1)S(1)} %get-tuple-element.55.refs_2_), channel_id=1, source_target_pairs={{0,4},{1,12},{2,6},{3,14},{4,0},{5,8},{6,2},{7,10},{8,5},{9,13},{1... | collective-permute-start | bytes 393224 | tf_op jit(solution)/shard_map/ppermute | solution.py:300
  7.6 10.7 %collective-permute-start.5 = (bf16[512,128]{1,0:T(8,128)(2,1)S(1)}, bf16[512,128]{1,0:T(8,128)(2,1)S(1)}, u32[]{:S(2)}, u32[]{:S(2)}) collective-permute-start(bf16[512,128]{1,0:T(8,128)(2,1)S(1)} %get-tuple-element.56.refs_3_), channel_id=1, source_target_pairs={{0,6},{1,14},{2,4},{3,12},{4,2},{5,10},{6,0},{7,8},{8,7},{9,15},{1... | collective-permute-start | bytes 393224 | tf_op jit(solution)/shard_map/ppermute | solution.py:300
  7.6 16.5 %collective-permute-start.6 = (bf16[512,128]{1,0:T(8,128)(2,1)S(1)}, bf16[512,128]{1,0:T(8,128)(2,1)S(1)}, u32[]{:S(2)}, u32[]{:S(2)}) collective-permute-start(bf16[512,128]{1,0:T(8,128)(2,1)S(1)} %get-tuple-element.57.refs_4_), channel_id=1, source_target_pairs={{0,1},{1,9},{2,3},{3,11},{4,5},{5,13},{6,7},{7,15},{8,0},{9,8},{10... | collective-permute-start | bytes 393224 | tf_op jit(solution)/shard_map/ppermute | solution.py:300
  11.6 13.9 %collective-permute-start.7 = (bf16[512,128]{1,0:T(8,128)(2,1)S(1)}, bf16[512,128]{1,0:T(8,128)(2,1)S(1)}, u32[]{:S(2)}, u32[]{:S(2)}) collective-permute-start(bf16[512,128]{1,0:T(8,128)(2,1)S(1)} %get-tuple-element.58.refs_5_), channel_id=1, source_target_pairs={{0,3},{1,11},{2,1},{3,9},{4,7},{5,15},{6,5},{7,13},{8,2},{9,10},{1... | collective-permute-start | bytes 393224 | tf_op jit(solution)/shard_map/ppermute | solution.py:300
  12.8 14.2 %collective-permute-start.8 = (bf16[512,128]{1,0:T(8,128)(2,1)S(1)}, bf16[512,128]{1,0:T(8,128)(2,1)S(1)}, u32[]{:S(2)}, u32[]{:S(2)}) collective-permute-start(bf16[512,128]{1,0:T(8,128)(2,1)S(1)} %get-tuple-element.59.refs_6_), channel_id=1, source_target_pairs={{0,5},{1,13},{2,7},{3,15},{4,1},{5,9},{6,3},{7,11},{8,4},{9,12},{1... | collective-permute-start | bytes 393224 | tf_op jit(solution)/shard_map/ppermute | solution.py:300
  18.2 22.6 %collective-permute-start.12 = (bf16[2,264,256]{2,1,0:T(8,128)(2,1)S(1)}, bf16[2,264,256]{2,1,0:T(8,128)(2,1)S(1)}, u32[]{:S(2)}, u32[]{:S(2)}) collective-permute-start(bf16[2,264,256]{2,1,0:T(8,128)(2,1)S(1)} %get-tuple-element.70.refs_8_), channel_id=1, source_target_pairs={{0,1},{1,0},{2,3},{3,2},{4,5},{5,4},{6,7},{7,6},{8,9},{9,8},{10,11... | collective-permute-start | bytes 811016 | tf_op jit(solution)/shard_map/ppermute | solution.py:300
  18.3 27.1 %collective-permute-start.16 = (bf16[2,264,256]{2,1,0:T(8,128)(2,1)S(1)}, bf16[2,264,256]{2,1,0:T(8,128)(2,1)S(1)}, u32[]{:S(2)}, u32[]{:S(2)}) collective-permute-start(bf16[2,264,256]{2,1,0:T(8,128)(2,1)S(1)} %get-tuple-element.75), channel_id=1, source_target_pairs={{0,6},{1,7},{2,4},{3,5},{4,2},{5,3},{6,0},{7,1},{8,14},{9,15},{10,... | collective-permute-start | bytes 811016 | tf_op jit(solution)/shard_map/ppermute | solution.py:300
  24.1 21.3 %collective-permute-start.14 = (bf16[2,264,256]{2,1,0:T(8,128)(2,1)S(1)}, bf16[2,264,256]{2,1,0:T(8,128)(2,1)S(1)}, u32[]{:S(2)}, u32[]{:S(2)}) collective-permute-start(bf16[2,264,256]{2,1,0:T(8,128)(2,1)S(1)} %get-tuple-element.73), channel_id=1, source_target_pairs={{0,4},{1,5},{2,6},{3,7},{4,0},{5,1},{6,2},{7,3},{8,12},{9,13},{10,... | collective-permute-start | bytes 811016 | tf_op jit(solution)/shard_map/ppermute | solution.py:300
  25.6 19.8 %collective-permute-start.11 = (bf16[2,264,256]{2,1,0:T(8,128)(2,1)S(1)}, bf16[2,264,256]{2,1,0:T(8,128)(2,1)S(1)}, u32[]{:S(2)}, u32[]{:S(2)}) collective-permute-start(bf16[2,264,256]{2,1,0:T(8,128)(2,1)S(1)} %get-tuple-element.69), channel_id=1, source_target_pairs={{0,2},{1,3},{2,0},{3,1},{4,6},{5,7},{6,4},{7,5},{8,10},{9,11},{10,... | collective-permute-start | bytes 811016 | tf_op jit(solution)/shard_map/ppermute | solution.py:300
  26.9 11.7 %collective-permute-start.9 = (bf16[512,128]{1,0:T(8,128)(2,1)S(1)}, bf16[512,128]{1,0:T(8,128)(2,1)S(1)}, u32[]{:S(2)}, u32[]{:S(2)}) collective-permute-start(bf16[512,128]{1,0:T(8,128)(2,1)S(1)} %get-tuple-element.60.refs_7_), channel_id=1, source_target_pairs={{0,7},{1,15},{2,5},{3,13},{4,3},{5,11},{6,1},{7,9},{8,6},{9,14},{1... | collective-permute-start | bytes 393224 | tf_op jit(solution)/shard_map/ppermute | solution.py:300
  38.6 2.2 %collective-permute-start.2 = (bf16[512,128]{1,0:T(8,128)(2,1)S(1)}, bf16[512,128]{1,0:T(8,128)(2,1)S(1)}, u32[]{:S(2)}, u32[]{:S(2)}) collective-permute-start(bf16[512,128]{1,0:T(8,128)(2,1)S(1)} %get-tuple-element.53.refs_0_), channel_id=1, source_target_pairs={{0,0},{1,8},{2,2},{3,10},{4,4},{5,12},{6,6},{7,14},{8,1},{9,9},{10... | collective-permute-start | bytes 393224 | tf_op jit(solution)/shard_map/ppermute | solution.py:300
  45.4 11.4 %collective-permute-start.13 = (bf16[2,264,256]{2,1,0:T(8,128)(2,1)S(1)}, bf16[2,264,256]{2,1,0:T(8,128)(2,1)S(1)}, u32[]{:S(2)}, u32[]{:S(2)}) collective-permute-start(bf16[2,264,256]{2,1,0:T(8,128)(2,1)S(1)} %collective-permute-done.11.refs_0_), channel_id=1, source_target_pairs={{0,1},{1,0},{2,3},{3,2},{4,5},{5,4},{6,7},{7,6},{8,9},{9,8},{10,11... | collective-permute-start | bytes 811016 | tf_op jit(solution)/shard_map/ppermute | solution.py:300
  53.0 3.8 %collective-permute-start.15 = (bf16[2,264,256]{2,1,0:T(8,128)(2,1)S(1)}, bf16[2,264,256]{2,1,0:T(8,128)(2,1)S(1)}, u32[]{:S(2)}, u32[]{:S(2)}) collective-permute-start(bf16[2,264,256]{2,1,0:T(8,128)(2,1)S(1)} %collective-permute-done.14.refs_2_), channel_id=1, source_target_pairs={{0,1},{1,0},{2,3},{3,2},{4,5},{5,4},{6,7},{7,6},{8,9},{9,8},{10,11... | collective-permute-start | bytes 811016 | tf_op jit(solution)/shard_map/ppermute | solution.py:300
  53.1 3.7 %collective-permute-start.17 = (bf16[2,264,256]{2,1,0:T(8,128)(2,1)S(1)}, bf16[2,264,256]{2,1,0:T(8,128)(2,1)S(1)}, u32[]{:S(2)}, u32[]{:S(2)}) collective-permute-start(bf16[2,264,256]{2,1,0:T(8,128)(2,1)S(1)} %collective-permute-done.16.refs_4_), channel_id=1, source_target_pairs={{0,1},{1,0},{2,3},{3,2},{4,5},{5,4},{6,7},{7,6},{8,9},{9,8},{10,11... | collective-permute-start | bytes 811016 | tf_op jit(solution)/shard_map/ppermute | solution.py:300
  53.5 21.3 %collective-permute-start.19 = (bf16[2,264,256]{2,1,0:T(8,128)(2,1)S(1)}, bf16[2,264,256]{2,1,0:T(8,128)(2,1)S(1)}, u32[]{:S(2)}, u32[]{:S(2)}) collective-permute-start(bf16[2,264,256]{2,1,0:T(8,128)(2,1)S(1)} %get-tuple-element.81), channel_id=1, source_target_pairs={{0,10},{1,11},{2,8},{3,9},{4,14},{5,15},{6,12},{7,13},{8,2},{9,3},... | collective-permute-start | bytes 811016 | tf_op jit(solution)/shard_map/ppermute | solution.py:300
  53.7 26.2 %collective-permute-start = (bf16[2,264,256]{2,1,0:T(8,128)(2,1)S(1)}, bf16[2,264,256]{2,1,0:T(8,128)(2,1)S(1)}, u32[]{:S(2)}, u32[]{:S(2)}) collective-permute-start(bf16[2,264,256]{2,1,0:T(8,128)(2,1)S(1)} %get-tuple-element.65), channel_id=1, source_target_pairs={{0,8},{1,9},{2,10},{3,11},{4,12},{5,13},{6,14},{7,15},{8,0},{9,1},... | collective-permute-start | bytes 811016 | tf_op jit(solution)/shard_map/ppermute | solution.py:300
  79.8 2.3 %collective-permute-start.18 = (bf16[2,264,256]{2,1,0:T(8,128)(2,1)S(1)}, bf16[2,264,256]{2,1,0:T(8,128)(2,1)S(1)}, u32[]{:S(2)}, u32[]{:S(2)}) collective-permute-start(bf16[2,264,256]{2,1,0:T(8,128)(2,1)S(1)} %collective-permute-done.refs_0_), channel_id=1, source_target_pairs={{0,1},{1,0},{2,3},{3,2},{4,5},{5,4},{6,7},{7,6},{8,9},{9,8},{10,11... | collective-permute-start | bytes 811016 | tf_op jit(solution)/shard_map/ppermute | solution.py:300
  79.9 2.3 %collective-permute-start.20 = (bf16[2,264,256]{2,1,0:T(8,128)(2,1)S(1)}, bf16[2,264,256]{2,1,0:T(8,128)(2,1)S(1)}, u32[]{:S(2)}, u32[]{:S(2)}) collective-permute-start(bf16[2,264,256]{2,1,0:T(8,128)(2,1)S(1)} %collective-permute-done.19.refs_2_), channel_id=1, source_target_pairs={{0,1},{1,0},{2,3},{3,2},{4,5},{5,4},{6,7},{7,6},{8,9},{9,8},{10,11... | collective-permute-start | bytes 811016 | tf_op jit(solution)/shard_map/ppermute | solution.py:300
  80.3 10.3 %collective-permute-start.10 = (bf16[2,264,256]{2,1,0:T(8,128)(2,1)S(1)}, bf16[2,264,256]{2,1,0:T(8,128)(2,1)S(1)}, u32[]{:S(2)}, u32[]{:S(2)}) collective-permute-start(bf16[2,264,256]{2,1,0:T(8,128)(2,1)S(1)} %get-tuple-element.68), channel_id=1, source_target_pairs={{0,12},{1,13},{2,14},{3,15},{4,8},{5,9},{6,10},{7,11},{8,4},{9,5},... | collective-permute-start | bytes 811016 | tf_op jit(solution)/shard_map/ppermute | solution.py:300
  90.6 2.0 %collective-permute-start.21 = (bf16[2,264,256]{2,1,0:T(8,128)(2,1)S(1)}, bf16[2,264,256]{2,1,0:T(8,128)(2,1)S(1)}, u32[]{:S(2)}, u32[]{:S(2)}) collective-permute-start(bf16[2,264,256]{2,1,0:T(8,128)(2,1)S(1)} %collective-permute-done.10.refs_0_), channel_id=1, source_target_pairs={{0,1},{1,0},{2,3},{3,2},{4,5},{5,4},{6,7},{7,6},{8,9},{9,8},{10,11... | collective-permute-start | bytes 811016 | tf_op jit(solution)/shard_map/ppermute | solution.py:300
  90.7 11.7 %collective-permute-start.1 = (bf16[2,264,256]{2,1,0:T(8,128)(2,1)S(1)}, bf16[2,264,256]{2,1,0:T(8,128)(2,1)S(1)}, u32[]{:S(2)}, u32[]{:S(2)}) collective-permute-start(bf16[2,264,256]{2,1,0:T(8,128)(2,1)S(1)} %get-tuple-element.66), channel_id=1, source_target_pairs={{0,14},{1,15},{2,12},{3,13},{4,10},{5,11},{6,8},{7,9},{8,6},{9,7},... | collective-permute-start | bytes 811016 | tf_op jit(solution)/shard_map/ppermute | solution.py:300
  102.3 1.5 %collective-permute-start.22 = (bf16[2,264,256]{2,1,0:T(8,128)(2,1)S(1)}, bf16[2,264,256]{2,1,0:T(8,128)(2,1)S(1)}, u32[]{:S(2)}, u32[]{:S(2)}) collective-permute-start(bf16[2,264,256]{2,1,0:T(8,128)(2,1)S(1)} %collective-permute-done.1.refs_0_), channel_id=1, source_target_pairs={{0,1},{1,0},{2,3},{3,2},{4,5},{5,4},{6,7},{7,6},{8,9},{9,8},{10,11... | collective-permute-start | bytes 811016 | tf_op jit(solution)/shard_map/ppermute | solution.py:300
  107.3 13.5 %collective-permute-start.23 = (bf16[528,128]{1,0:T(8,128)(2,1)S(1)}, bf16[528,128]{1,0:T(8,128)(2,1)S(1)}, u32[]{:S(2)}, u32[]{:S(2)}) collective-permute-start(bf16[528,128]{1,0:T(8,128)(2,1)S(1)} %get-tuple-element.93), channel_id=1, source_target_pairs={{0,0},{8,1},{2,2},{10,3},{4,4},{12,5},{6,6},{14,7},{1,8},{9,9},{3,... | collective-permute-start | bytes 405512 | tf_op jit(solution)/shard_map/ppermute | solution.py:300
  108.0 13.9 %collective-permute-start.24 = (bf16[528,128]{1,0:T(8,128)(2,1)S(1)}, bf16[528,128]{1,0:T(8,128)(2,1)S(1)}, u32[]{:S(2)}, u32[]{:S(2)}) collective-permute-start(bf16[528,128]{1,0:T(8,128)(2,1)S(1)} %get-tuple-element.94), channel_id=1, source_target_pairs={{2,0},{10,1},{0,2},{8,3},{6,4},{14,5},{4,6},{12,7},{3,8},{11,9},{1... | collective-permute-start | bytes 405512 | tf_op jit(solution)/shard_map/ppermute | solution.py:300
  109.3 15.6 %collective-permute-start.25 = (bf16[528,128]{1,0:T(8,128)(2,1)S(1)}, bf16[528,128]{1,0:T(8,128)(2,1)S(1)}, u32[]{:S(2)}, u32[]{:S(2)}) collective-permute-start(bf16[528,128]{1,0:T(8,128)(2,1)S(1)} %get-tuple-element.95), channel_id=1, source_target_pairs={{4,0},{12,1},{6,2},{14,3},{0,4},{8,5},{2,6},{10,7},{5,8},{13,9},{7... | collective-permute-start | bytes 405512 | tf_op jit(solution)/shard_map/ppermute | solution.py:300
  115.1 13.5 %collective-permute-start.26 = (bf16[528,128]{1,0:T(8,128)(2,1)S(1)}, bf16[528,128]{1,0:T(8,128)(2,1)S(1)}, u32[]{:S(2)}, u32[]{:S(2)}) collective-permute-start(bf16[528,128]{1,0:T(8,128)(2,1)S(1)} %get-tuple-element.96), channel_id=1, source_target_pairs={{6,0},{14,1},{4,2},{12,3},{2,4},{10,5},{0,6},{8,7},{7,8},{15,9},{5... | collective-permute-start | bytes 405512 | tf_op jit(solution)/shard_map/ppermute | solution.py:300
  115.3 13.3 %collective-permute-start.27 = (bf16[528,128]{1,0:T(8,128)(2,1)S(1)}, bf16[528,128]{1,0:T(8,128)(2,1)S(1)}, u32[]{:S(2)}, u32[]{:S(2)}) collective-permute-start(bf16[528,128]{1,0:T(8,128)(2,1)S(1)} %get-tuple-element.97), channel_id=1, source_target_pairs={{1,0},{9,1},{3,2},{11,3},{5,4},{13,5},{7,6},{15,7},{0,8},{8,9},{2,... | collective-permute-start | bytes 405512 | tf_op jit(solution)/shard_map/ppermute | solution.py:300
  120.8 7.9 %collective-permute-start.28 = (bf16[528,128]{1,0:T(8,128)(2,1)S(1)}, bf16[528,128]{1,0:T(8,128)(2,1)S(1)}, u32[]{:S(2)}, u32[]{:S(2)}) collective-permute-start(bf16[528,128]{1,0:T(8,128)(2,1)S(1)} %get-tuple-element.98), channel_id=1, source_target_pairs={{3,0},{11,1},{1,2},{9,3},{7,4},{15,5},{5,6},{13,7},{2,8},{10,9},{0... | collective-permute-start | bytes 405512 | tf_op jit(solution)/shard_map/ppermute | solution.py:300
  122.0 7.0 %collective-permute-start.29 = (bf16[528,128]{1,0:T(8,128)(2,1)S(1)}, bf16[528,128]{1,0:T(8,128)(2,1)S(1)}, u32[]{:S(2)}, u32[]{:S(2)}) collective-permute-start(bf16[528,128]{1,0:T(8,128)(2,1)S(1)} %get-tuple-element.99), channel_id=1, source_target_pairs={{5,0},{13,1},{7,2},{15,3},{1,4},{9,5},{3,6},{11,7},{4,8},{12,9},{6... | collective-permute-start | bytes 405512 | tf_op jit(solution)/shard_map/ppermute | solution.py:300
  124.9 14.7 %collective-permute-start.30 = (bf16[528,128]{1,0:T(8,128)(2,1)S(1)}, bf16[528,128]{1,0:T(8,128)(2,1)S(1)}, u32[]{:S(2)}, u32[]{:S(2)}) collective-permute-start(bf16[528,128]{1,0:T(8,128)(2,1)S(1)} %get-tuple-element.100), channel_id=1, source_target_pairs={{7,0},{15,1},{5,2},{13,3},{3,4},{11,5},{1,6},{9,7},{6,8},{14,9},{4... | collective-permute-start | bytes 405512 | tf_op jit(solution)/shard_map/ppermute | solution.py:300
  (6 other events, 42.2 us)

commit v4 on v3

--- a/solution.py
+++ b/solution.py
@@ -74,18 +74,21 @@
         copy.start()
     my_head = lax.axis_index("shard") // n_sub
     block_len = buf.shape[1]
-    left = lax.broadcasted_iota(jnp.int32, (TAG, 2 * HD), 1) < HD
+    tags = TAG // slots
+    left = lax.broadcasted_iota(jnp.int32, (tags, 2 * HD), 1) < HD
     for slot in range(slots):
         request, position = find_block(order_ref[slot], lengths_ref)
         tag = jnp.where(left, request, position).astype(jnp.float32).astype(jnp.bfloat16)
+        tokens = slice(slot * block_len, (slot + 1) * block_len)
         angle = (position * block_len).astype(jnp.float32) * frequencies()
         cosine, sine = jnp.cos(angle), signed(jnp.sin(angle))
         copies[slot].wait()
         for mask in range(heads):
             column = pl.multiple_of((my_head ^ mask) * (2 * HD), 2 * HD)
-            out_refs[mask][slot, :block_len, :HD] = turn(buf[slot, :, pl.ds(column, HD)], cosine, sine)
-            out_refs[mask][slot, :block_len, HD:] = buf[slot, :, pl.ds(column + HD, HD)]
-            out_refs[mask][slot, block_len:, :] = tag
+            out_refs[mask][tokens, :HD] = turn(buf[slot, :, pl.ds(column, HD)], cosine, sine)
+            out_refs[mask][tokens, HD:] = buf[slot, :, pl.ds(column + HD, HD)]
+            first_tag = slots * block_len + slot * tags
+            out_refs[mask][first_tag : first_tag + tags, :] = tag
 
 
 def row_turns(row):
@@ -138,7 +141,7 @@
         for tile in range(tiles)
     ] if first else []
     kv_copies = [
-        pltpu.make_async_copy(ref, kv_buf.at[pl.ds(i * blk_dev, blk_dev)], kv_sem.at[i]) for i, ref in enumerate(kv_refs)
+        pltpu.make_async_copy(ref, kv_buf.at[i], kv_sem.at[i]) for i, ref in enumerate(kv_refs)
     ]
     for copy in kv_copies + query_copies:
         copy.start()
@@ -146,7 +149,8 @@
     my_head, my_sub = me // n_sub, me % n_sub
     kv_local = n_req // n_sub
     mixed = my_sub * kv_local + my_head % kv_local
-    block_len = kv_buf.shape[1] - TAG
+    block_len = (kv_buf.shape[1] - TAG) // blk_dev
+    tags = TAG // blk_dev
     if first:
         acc_ref[...] = jnp.zeros_like(acc_ref)
         top_ref[...] = jnp.full_like(top_ref, TOP_START)
@@ -154,11 +158,13 @@
         copy.wait()
     count = jnp.int32(0)
     for i in range(n_buf * blk_dev):
-        tag = kv_buf[i, block_len:, :].astype(jnp.float32)
+        first_tag = blk_dev * block_len + (i % blk_dev) * tags
+        tag = kv_buf[i // blk_dev, first_tag : first_tag + tags, :].astype(jnp.float32)
         request = jnp.max(tag[:, :HD]).astype(jnp.int32)
         offset = jnp.max(tag[:, HD:]).astype(jnp.int32) * block_len
         for tile in reversed(range(tiles)):
-            item_ref[0, count] = i
+            item_ref[0, count] = i // blk_dev
+            item_ref[4, count] = (i % blk_dev) * block_len
             item_ref[1, count] = request
             item_ref[2, count] = tile
             item_ref[3, count] = offset
@@ -166,6 +172,7 @@
             count = count + jnp.where(used, 1, 0)
     for pad in range(2):
         item_ref[0, count + pad] = 0
+        item_ref[4, count + pad] = 0
         item_ref[1, count + pad] = 0
         item_ref[2, count + pad] = 0
         item_ref[3, count + pad] = NOWHERE
@@ -174,10 +181,13 @@
     scale = math.log2(math.e) / math.sqrt(HD)
     token = lax.broadcasted_iota(jnp.int32, (block_len, half), 0)
 
+    def tokens_of(item):
+        return pl.ds(pl.multiple_of(item_ref[4, item], 8), block_len)
+
     def score(item, score_ref, best_ref):
         i, request, tile = item_ref[0, item], item_ref[1, item], item_ref[2, item]
         scores = lax.dot_general(
-            kv_buf[i, :block_len, :HD],
+            kv_buf[i, tokens_of(item), :HD],
             query_buf[request ^ mixed, tile],
             (((1,), (1,)), ((), ())),
             preferred_element_type=jnp.float32,
@@ -195,7 +205,7 @@
         factor = jnp.exp2(old_top - new_top)
         weights = jnp.exp2(score_ref[...] - new_top).astype(jnp.bfloat16)
         values = jnp.concatenate(
-            [jnp.transpose(kv_buf[i, :block_len, HD:]), jnp.ones((STATS, block_len), jnp.bfloat16)], axis=0
+            [jnp.transpose(kv_buf[i, tokens_of(item), HD:]), jnp.ones((STATS, block_len), jnp.bfloat16)], axis=0
         )
         summed = jnp.dot(values, weights, preferred_element_type=jnp.float32)
         acc_ref[place] = acc_ref[place] * factor + summed[: HD + 8]
@@ -262,9 +272,10 @@
 
 
 def merge_own(n_sub, group_size, own_ref, fresh_ref, *refs):
-    part_refs, out_ref, level_ref = refs[:-2], refs[-2], refs[-1]
+    part_refs, (out_ref, level_ref, out_buf, out_sem) = refs[:-4], refs[-4:]
     request = lax.axis_index("shard") // n_sub
     rows = out_ref.shape[0]
+    copies = []
     kv_local = fresh_ref.shape[1] // (2 * HD)
     sub_heads = group_size // n_sub
     width = sub_heads * rows
@@ -289,11 +300,16 @@
             line, at = step * lines + flat.start // HD, flat.start % HD
             size = flat.stop - flat.start
             part = part_ref[flat, :].astype(jnp.float32)
-            column = pl.multiple_of((kv_id * group_size + sub * sub_heads + head) * HD, HD)
-            out_ref[row_part, pl.ds(column, HD)] = (
+            out_buf[step, row_part, head * HD : (head + 1) * HD] = (
                 part * share[at : at + size, line : line + 1]
                 + own_value[row_part, :] * own_share[at : at + size, line : line + 1]
             ).astype(jnp.bfloat16)
+        span = sub_heads * HD
+        column = pl.multiple_of((kv_id * group_size + sub * sub_heads) * HD, HD)
+        copies.append(pltpu.make_async_copy(out_buf.at[step], out_ref.at[:, pl.ds(column, span)], out_sem.at[step]))
+        copies[-1].start()
+    for copy in copies:
+        copy.wait()
 
 
 def moved(x, pairs):
@@ -349,7 +365,7 @@
 
     packed_kv = pl.pallas_call(
         functools.partial(pack_kv, n_sub),
-        out_shape=[jax.ShapeDtypeStruct((blk_dev, block_len + TAG, 2 * HD), bf16)] * kv_heads,
+        out_shape=[jax.ShapeDtypeStruct((blk_dev * block_len + TAG, 2 * HD), bf16)] * kv_heads,
         in_specs=[smem, smem, anywhere],
         out_specs=[spec()] * kv_heads,
         scratch_shapes=[pltpu.VMEM((blk_dev, block_len, full_width), bf16), pltpu.SemaphoreType.DMA((blk_dev,))],
@@ -409,12 +425,12 @@
             out_specs=[spec()] * ((n_req if last else 0) + 3),
             input_output_aliases={2 + len(inputs) + k: (n_req if last else 0) + k for k in range(len(state))},
             scratch_shapes=[
-                pltpu.VMEM((blocks, block_len + TAG, 2 * HD), bf16),
+                pltpu.VMEM((len(buffers), blk_dev * block_len + TAG, 2 * HD), bf16),
                 pltpu.VMEM((block_len, half_width), jnp.float32),
                 pltpu.VMEM((block_len, half_width), jnp.float32),
                 pltpu.VMEM((1, half_width), jnp.float32),
                 pltpu.VMEM((1, half_width), jnp.float32),
-                pltpu.SMEM((4, blocks * tiles + 2), jnp.int32),
+                pltpu.SMEM((5, blocks * tiles + 2), jnp.int32),
                 pltpu.SemaphoreType.DMA((n_req, tiles)),
                 pltpu.SemaphoreType.DMA((len(buffers),)),
             ],
@@ -427,8 +443,12 @@
         functools.partial(merge_own, n_sub, group_size),
         out_shape=jax.ShapeDtypeStruct((rows, kv_local * group_size * HD), bf16),
         in_specs=[spec()] * (2 + n_req),
-        out_specs=spec(),
-        scratch_shapes=[pltpu.VMEM((level_rows, rows), jnp.float32)],
+        out_specs=anywhere,
+        scratch_shapes=[
+            pltpu.VMEM((level_rows, rows), jnp.float32),
+            pltpu.VMEM((n_req, rows, sub_heads * HD), bf16),
+            pltpu.SemaphoreType.DMA((n_req,)),
+        ],
         compiler_params=grant,
         name="merge_own",
     )(own, fresh_rows, *returned)

time: 142 us -> 141 us (level)
  no operation moved by 1% of the time
where the time goes in v4:
time: 141 us
  waiting for transfers between devices  58.8 us (42%)
  starting transfers between devices  50.4 us (36%)
  Pallas kernels  26.5 us (19%)
  local copies, waits for them, and re-layouts  4.82 us (3%)
    ppermute x31, waiting for transfers between devices, moved(): return lax.ppermute(x, 'shard', pairs)  58.8 us
    ppermute x31, starting transfers between devices, moved(): return lax.ppermute(x, 'shard', pairs)  50.4 us
    pallas_call x5, Pallas kernels, shards(): pl.pallas_call(functools.partial(attend, n_sub, len(buffers), first, last...  20.3 us
    unnamed x14, local copies, waits for them, and re-layouts  4.82 us
  transfers between devices with their start and end apart: 31, of which 10 were waited for; matrix products, arithmetic and copies ran while one was open for 0% of the time, Pallas kernels for 14%

profile of v4, /device:TPU:0, one launch (start us, length us, event | category | flops | bytes accessed | tf_op | source)
XLA Modules:
  0.0 140.8 jit_solution(2022872566684781358)
XLA Ops:
  0.0 1.2 copy-done.2
  2.9 3.1 %collective-permute-start.3 = (bf16[512,128]{1,0:T(8,128)(2,1)S(1)}, bf16[512,128]{1,0:T(8,128)(2,1)S(1)}, u32[]{:S(2)}, u32[]{:S(2)}) collective-permute-start(bf16[512,128]{1,0:T(8,128)(2,1)S(1)} %get-tuple-element.54.refs_1_), channel_id=1, source_target_pairs={{0,2},{1,10},{2,0},{3,8},{4,6},{5,14},{6,4},{7,12},{8,3},{9,11},{1... | collective-permute-start | bytes 393224 | tf_op jit(solution)/shard_map/ppermute | solution.py:316
  6.0 1.6 %collective-permute-start.4 = (bf16[512,128]{1,0:T(8,128)(2,1)S(1)}, bf16[512,128]{1,0:T(8,128)(2,1)S(1)}, u32[]{:S(2)}, u32[]{:S(2)}) collective-permute-start(bf16[512,128]{1,0:T(8,128)(2,1)S(1)} %get-tuple-element.55.refs_2_), channel_id=1, source_target_pairs={{0,4},{1,12},{2,6},{3,14},{4,0},{5,8},{6,2},{7,10},{8,5},{9,13},{1... | collective-permute-start | bytes 393224 | tf_op jit(solution)/shard_map/ppermute | solution.py:316
  7.6 4.0 %collective-permute-start.6 = (bf16[512,128]{1,0:T(8,128)(2,1)S(1)}, bf16[512,128]{1,0:T(8,128)(2,1)S(1)}, u32[]{:S(2)}, u32[]{:S(2)}) collective-permute-start(bf16[512,128]{1,0:T(8,128)(2,1)S(1)} %get-tuple-element.57.refs_4_), channel_id=1, source_target_pairs={{0,1},{1,9},{2,3},{3,11},{4,5},{5,13},{6,7},{7,15},{8,0},{9,8},{10... | collective-permute-start | bytes 393224 | tf_op jit(solution)/shard_map/ppermute | solution.py:316
  13.7 1.6 %copy-done = bf16[2,256,2048]{2,1,0:T(8,128)(2,1)S(1)} copy-done((bf16[2,256,2048]{2,1,0:T(8,128)(2,1)S(1)}, bf16[2,256,2048]{2,1,0:T(8,128)(2,1)}, u32[]{:S(2)}) %copy-start) | copy-done | bytes 2097176
  16.6 1.6 %pack_kv.1 = (bf16[520,256]{1,0:T(8,128)(2,1)S(1)}, bf16[520,256]{1,0:T(8,128)(2,1)S(1)}, bf16[520,256]{1,0:T(8,128)(2,1)S(1)}, bf16[520,256]{1,0:T(8,128)(2,1)S...) custom-call(s32[2]{0:T(128)S(1)} %copy-done.5, ...), custom_call_target="tpu_custom_call" | custom-call | tf_op jit(solution)/shard_map/pack_kv/pallas_call | solution.py:366
  19.1 5.0 %collective-permute-done.6.refs_4_ = bf16[512,128]{1,0:T(8,128)(2,1)S(1)} collective-permute-done((bf16[512,128]{1,0:T(8,128)(2,1)S(1)}, bf16[512,128]{1,0:T(8,128)(2,1)S(1)}, u32[]{:S(2)}, u32[]{:S(2)}) %collective-permute-start.6) | collective-permute-done | bytes 131104 | tf_op jit(solution)/shard_map/ppermute | solution.py:316
  24.1 1.5 %collective-permute-done.7.refs_5_ = bf16[512,128]{1,0:T(8,128)(2,1)S(1)} collective-permute-done((bf16[512,128]{1,0:T(8,128)(2,1)S(1)}, bf16[512,128]{1,0:T(8,128)(2,1)S(1)}, u32[]{:S(2)}, u32[]{:S(2)}) %collective-permute-start.7) | collective-permute-done | bytes 131104 | tf_op jit(solution)/shard_map/ppermute | solution.py:316
  25.6 1.4 collective-permute-start.11
  26.9 11.5 %collective-permute-done.9.refs_7_ = bf16[512,128]{1,0:T(8,128)(2,1)S(1)} collective-permute-done((bf16[512,128]{1,0:T(8,128)(2,1)S(1)}, bf16[512,128]{1,0:T(8,128)(2,1)S(1)}, u32[]{:S(2)}, u32[]{:S(2)}) %collective-permute-start.9) | collective-permute-done | bytes 131104 | tf_op jit(solution)/shard_map/ppermute | solution.py:316
  39.1 1.5 %own_scores.1 = (f32[128,128]{1,0:T(8,128)S(1)}, s32[16,1,256]{2,1,0:T(1,128)S(1)}) custom-call(s32[8,128]{1,0:T(8,128)S(1)} %copy-done.4, bf16[128,1024]{1,0:T(8,128)(2,1)S(1)} %copy-done.1, bf16[512,128]{1,0:T(8,128)(2,1)S(1)} %get-tuple-element.53.refs_0_, bf16[512,128]{1,0:T(8,128)(2,1)S(1)} %get-tuple-element.54.refs_1_, ...), custom_call_target="tpu_custom_call" | custom-call | tf_op jit(solution)/shard_map/own_scores/pallas_call | solution.py:353
  40.6 4.6 %shard_map.64 = (f32[16,136,256]{2,1,0:T(8,128)S(1)}, f32[16,1,256]{2,1,0:T(1,128)S(1)}, bf16[8,2,256,128]{3,2,1,0:T(8,128)(2,1)S(1)}) custom-call(s32[8,128]{1,0:T(8,128)S(1)} %copy-done.4, s32[16,1,256]{2,1,0:T(1,128)S(1)} %get-tuple-element.62.wide_ref, bf16[512,128]{1,0:T(8,128)(2,1)S(1)} %collective-permute-done.2.refs_0_, ...), custom_call_target="tpu_custom_call" | custom-call | tf_op jit(solution)/shard_map/pallas_call | solution.py:421
  45.2 7.6 %collective-permute-start.13 = (bf16[520,256]{1,0:T(8,128)(2,1)S(1)}, bf16[520,256]{1,0:T(8,128)(2,1)S(1)}, u32[]{:S(2)}, u32[]{:S(2)}) collective-permute-start(bf16[520,256]{1,0:T(8,128)(2,1)S(1)} %collective-permute-done.11.refs_0_), channel_id=1, source_target_pairs={{0,1},{1,0},{2,3},{3,2},{4,5},{5,4},{6,7},{7,6},{8,9},{9,8},{10,11... | collective-permute-start | bytes 798728 | tf_op jit(solution)/shard_map/ppermute | solution.py:316
  53.5 3.1 %collective-permute-start = (bf16[520,256]{1,0:T(8,128)(2,1)S(1)}, bf16[520,256]{1,0:T(8,128)(2,1)S(1)}, u32[]{:S(2)}, u32[]{:S(2)}) collective-permute-start(bf16[520,256]{1,0:T(8,128)(2,1)S(1)} %get-tuple-element.65), channel_id=1, source_target_pairs={{0,8},{1,9},{2,10},{3,11},{4,12},{5,13},{6,14},{7,15},{8,0},{9,1},... | collective-permute-start | bytes 798728 | tf_op jit(solution)/shard_map/ppermute | solution.py:316
  56.6 5.2 %shard_map.65 = (f32[16,136,256]{2,1,0:T(8,128)S(1)}, f32[16,1,256]{2,1,0:T(1,128)S(1)}, bf16[8,2,256,128]{3,2,1,0:T(8,128)(2,1)S(1)}) custom-call(s32[8,128]{1,0:T(8,128)S(1)} %copy-done.4, s32[16,1,256]{2,1,0:T(1,128)S(1)} %get-tuple-element.62.wide_ref, ...), custom_call_target="tpu_custom_call", output_to_operand_aliasing={{0}: (8, {}), {1}: (9, {}), {2}: (10, {})} | custom-call | tf_op jit(solution)/shard_map/pallas_call | solution.py:421
  61.8 12.6 %collective-permute-done.19.refs_2_ = bf16[520,256]{1,0:T(8,128)(2,1)S(1)} collective-permute-done((bf16[520,256]{1,0:T(8,128)(2,1)S(1)}, bf16[520,256]{1,0:T(8,128)(2,1)S(1)}, u32[]{:S(2)}, u32[]{:S(2)}) %collective-permute-start.19) | collective-permute-done | bytes 266272 | tf_op jit(solution)/shard_map/ppermute | solution.py:316
  74.3 5.0 %collective-permute-done.refs_0_ = bf16[520,256]{1,0:T(8,128)(2,1)S(1)} collective-permute-done((bf16[520,256]{1,0:T(8,128)(2,1)S(1)}, bf16[520,256]{1,0:T(8,128)(2,1)S(1)}, u32[]{:S(2)}, u32[]{:S(2)}) %collective-permute-start) | collective-permute-done | bytes 266272 | tf_op jit(solution)/shard_map/ppermute | solution.py:316
  79.8 1.8 %collective-permute-start.10 = (bf16[520,256]{1,0:T(8,128)(2,1)S(1)}, bf16[520,256]{1,0:T(8,128)(2,1)S(1)}, u32[]{:S(2)}, u32[]{:S(2)}) collective-permute-start(bf16[520,256]{1,0:T(8,128)(2,1)S(1)} %get-tuple-element.68), channel_id=1, source_target_pairs={{0,12},{1,13},{2,14},{3,15},{4,8},{5,9},{6,10},{7,11},{8,4},{9,5},... | collective-permute-start | bytes 798728 | tf_op jit(solution)/shard_map/ppermute | solution.py:316
  81.6 4.1 %shard_map.66 = (f32[16,136,256]{2,1,0:T(8,128)S(1)}, f32[16,1,256]{2,1,0:T(1,128)S(1)}, bf16[8,2,256,128]{3,2,1,0:T(8,128)(2,1)S(1)}) custom-call(s32[8,128]{1,0:T(8,128)S(1)} %copy-done.4, s32[16,1,256]{2,1,0:T(1,128)S(1)} %get-tuple-element.62.wide_ref, ...), custom_call_target="tpu_custom_call", output_to_operand_aliasing={{0}: (6, {}), {1}: (7, {}), {2}: (8, {})} | custom-call | tf_op jit(solution)/shard_map/pallas_call | solution.py:421
  85.7 4.3 %collective-permute-done.10.refs_0_ = bf16[520,256]{1,0:T(8,128)(2,1)S(1)} collective-permute-done((bf16[520,256]{1,0:T(8,128)(2,1)S(1)}, bf16[520,256]{1,0:T(8,128)(2,1)S(1)}, u32[]{:S(2)}, u32[]{:S(2)}) %collective-permute-start.10) | collective-permute-done | bytes 266272 | tf_op jit(solution)/shard_map/ppermute | solution.py:316
  90.0 2.0 %collective-permute-start.1 = (bf16[520,256]{1,0:T(8,128)(2,1)S(1)}, bf16[520,256]{1,0:T(8,128)(2,1)S(1)}, u32[]{:S(2)}, u32[]{:S(2)}) collective-permute-start(bf16[520,256]{1,0:T(8,128)(2,1)S(1)} %get-tuple-element.66), channel_id=1, source_target_pairs={{0,14},{1,15},{2,12},{3,13},{4,10},{5,11},{6,8},{7,9},{8,6},{9,7},... | collective-permute-start | bytes 798728 | tf_op jit(solution)/shard_map/ppermute | solution.py:316
  92.0 3.1 %shard_map.67 = (f32[16,136,256]{2,1,0:T(8,128)S(1)}, f32[16,1,256]{2,1,0:T(1,128)S(1)}, bf16[8,2,256,128]{3,2,1,0:T(8,128)(2,1)S(1)}) custom-call(s32[8,128]{1,0:T(8,128)S(1)} %copy-done.4, s32[16,1,256]{2,1,0:T(1,128)S(1)} %get-tuple-element.62.wide_ref, ...), custom_call_target="tpu_custom_call", output_to_operand_aliasing={{0}: (4, {}), {1}: (5, {}), {2}: (6, {})} | custom-call | tf_op jit(solution)/shard_map/pallas_call | solution.py:421
  95.1 6.6 %collective-permute-done.1.refs_0_ = bf16[520,256]{1,0:T(8,128)(2,1)S(1)} collective-permute-done((bf16[520,256]{1,0:T(8,128)(2,1)S(1)}, bf16[520,256]{1,0:T(8,128)(2,1)S(1)}, u32[]{:S(2)}, u32[]{:S(2)}) %collective-permute-start.1) | collective-permute-done | bytes 266272 | tf_op jit(solution)/shard_map/ppermute | solution.py:316
  101.7 1.5 %collective-permute-done.22.refs_1_ = bf16[520,256]{1,0:T(8,128)(2,1)S(1)} collective-permute-done((bf16[520,256]{1,0:T(8,128)(2,1)S(1)}, bf16[520,256]{1,0:T(8,128)(2,1)S(1)}, u32[]{:S(2)}, u32[]{:S(2)}) %collective-permute-start.22) | collective-permute-done | bytes 266272 | tf_op jit(solution)/shard_map/ppermute | solution.py:316
  103.2 3.4 %shard_map.68 = (bf16[528,128]{1,0:T(8,128)(2,1)S(1)}, bf16[528,128]{1,0:T(8,128)(2,1)S(1)}, bf16[528,128]{1,0:T(8,128)(2,1)S(1)}, bf16[528,128]{1,0:T(8,128)(2,...) custom-call(s32[8,128]{1,0:T(8,128)S(1)} %copy-done.4, ...), custom_call_target="tpu_custom_call", output_to_operand_aliasing={{8}: (4, {}), {9}: (5, {}), {10}: (6, {})} | custom-call | tf_op jit(solution)/shard_map/pallas_call | solution.py:421
  107.3 1.3 collective-permute-start.24
  108.6 5.7 %collective-permute-start.25 = (bf16[528,128]{1,0:T(8,128)(2,1)S(1)}, bf16[528,128]{1,0:T(8,128)(2,1)S(1)}, u32[]{:S(2)}, u32[]{:S(2)}) collective-permute-start(bf16[528,128]{1,0:T(8,128)(2,1)S(1)} %get-tuple-element.95), channel_id=1, source_target_pairs={{4,0},{12,1},{6,2},{14,3},{0,4},{8,5},{2,6},{10,7},{5,8},{13,9},{7... | collective-permute-start | bytes 405512 | tf_op jit(solution)/shard_map/ppermute | solution.py:316
  114.6 5.5 %collective-permute-start.27 = (bf16[528,128]{1,0:T(8,128)(2,1)S(1)}, bf16[528,128]{1,0:T(8,128)(2,1)S(1)}, u32[]{:S(2)}, u32[]{:S(2)}) collective-permute-start(bf16[528,128]{1,0:T(8,128)(2,1)S(1)} %get-tuple-element.97), channel_id=1, source_target_pairs={{1,0},{9,1},{3,2},{11,3},{5,4},{13,5},{7,6},{15,7},{0,8},{8,9},{2,... | collective-permute-start | bytes 405512 | tf_op jit(solution)/shard_map/ppermute | solution.py:316
  121.2 2.9 %collective-permute-start.29 = (bf16[528,128]{1,0:T(8,128)(2,1)S(1)}, bf16[528,128]{1,0:T(8,128)(2,1)S(1)}, u32[]{:S(2)}, u32[]{:S(2)}) collective-permute-start(bf16[528,128]{1,0:T(8,128)(2,1)S(1)} %get-tuple-element.99), channel_id=1, source_target_pairs={{5,0},{13,1},{7,2},{15,3},{1,4},{9,5},{3,6},{11,7},{4,8},{12,9},{6... | collective-permute-start | bytes 405512 | tf_op jit(solution)/shard_map/ppermute | solution.py:316
  124.1 3.7 %collective-permute-start.30 = (bf16[528,128]{1,0:T(8,128)(2,1)S(1)}, bf16[528,128]{1,0:T(8,128)(2,1)S(1)}, u32[]{:S(2)}, u32[]{:S(2)}) collective-permute-start(bf16[528,128]{1,0:T(8,128)(2,1)S(1)} %get-tuple-element.100), channel_id=1, source_target_pairs={{7,0},{15,1},{5,2},{13,3},{3,4},{11,5},{1,6},{9,7},{6,8},{14,9},{4... | collective-permute-start | bytes 405512 | tf_op jit(solution)/shard_map/ppermute | solution.py:316
  128.2 10.5 %collective-permute-done.30.refs_7_ = bf16[528,128]{1,0:T(8,128)(2,1)S(1)} collective-permute-done((bf16[528,128]{1,0:T(8,128)(2,1)S(1)}, bf16[528,128]{1,0:T(8,128)(2,1)S(1)}, u32[]{:S(2)}, u32[]{:S(2)}) %collective-permute-start.30) | collective-permute-done | bytes 135200 | tf_op jit(solution)/shard_map/ppermute | solution.py:316
  138.7 2.1 %merge_own.1 = bf16[128,4096]{1,0:T(8,128)(2,1)} custom-call(f32[128,128]{1,0:T(8,128)S(1)} %get-tuple-element.61.own_ref, bf16[128,1024]{1,0:T(8,128)(2,1)S(1)} %copy-done.1, bf16[528,128]{1,0:T(8,128)(2,1)S(1)} %collective-permute-done.23.refs_0_, bf16[528,128]{1,0:T(8,128)(2,1)S(1)} %collective-permute-done.24.refs_1_, ...), custom_call_target="tpu_custom_call" | custom-call | tf_op jit(solution)/shard_map/merge_own/pallas_call | solution.py:442
  (53 shorter events, 10.2 us)
Async XLA Ops:
  1.9 37.2 %copy-start.4 = (s32[8,128]{1,0:T(8,128)S(1)}, s32[8,128]{1,0:T(8,128)}, u32[]{:S(2)}) copy-start(s32[8,128]{1,0:T(8,128)} %rows_smem.9) | copy-start | bytes 12292
  2.9 9.8 %collective-permute-start.3 = (bf16[512,128]{1,0:T(8,128)(2,1)S(1)}, bf16[512,128]{1,0:T(8,128)(2,1)S(1)}, u32[]{:S(2)}, u32[]{:S(2)}) collective-permute-start(bf16[512,128]{1,0:T(8,128)(2,1)S(1)} %get-tuple-element.54.refs_1_), channel_id=1, source_target_pairs={{0,2},{1,10},{2,0},{3,8},{4,6},{5,14},{6,4},{7,12},{8,3},{9,11},{1... | collective-permute-start | bytes 393224 | tf_op jit(solution)/shard_map/ppermute | solution.py:316
  6.0 12.2 %collective-permute-start.4 = (bf16[512,128]{1,0:T(8,128)(2,1)S(1)}, bf16[512,128]{1,0:T(8,128)(2,1)S(1)}, u32[]{:S(2)}, u32[]{:S(2)}) collective-permute-start(bf16[512,128]{1,0:T(8,128)(2,1)S(1)} %get-tuple-element.55.refs_2_), channel_id=1, source_target_pairs={{0,4},{1,12},{2,6},{3,14},{4,0},{5,8},{6,2},{7,10},{8,5},{9,13},{1... | collective-permute-start | bytes 393224 | tf_op jit(solution)/shard_map/ppermute | solution.py:316
  7.6 10.7 %collective-permute-start.5 = (bf16[512,128]{1,0:T(8,128)(2,1)S(1)}, bf16[512,128]{1,0:T(8,128)(2,1)S(1)}, u32[]{:S(2)}, u32[]{:S(2)}) collective-permute-start(bf16[512,128]{1,0:T(8,128)(2,1)S(1)} %get-tuple-element.56.refs_3_), channel_id=1, source_target_pairs={{0,6},{1,14},{2,4},{3,12},{4,2},{5,10},{6,0},{7,8},{8,7},{9,15},{1... | collective-permute-start | bytes 393224 | tf_op jit(solution)/shard_map/ppermute | solution.py:316
  7.6 16.5 %collective-permute-start.6 = (bf16[512,128]{1,0:T(8,128)(2,1)S(1)}, bf16[512,128]{1,0:T(8,128)(2,1)S(1)}, u32[]{:S(2)}, u32[]{:S(2)}) collective-permute-start(bf16[512,128]{1,0:T(8,128)(2,1)S(1)} %get-tuple-element.57.refs_4_), channel_id=1, source_target_pairs={{0,1},{1,9},{2,3},{3,11},{4,5},{5,13},{6,7},{7,15},{8,0},{9,8},{10... | collective-permute-start | bytes 393224 | tf_op jit(solution)/shard_map/ppermute | solution.py:316
  11.6 13.9 %collective-permute-start.7 = (bf16[512,128]{1,0:T(8,128)(2,1)S(1)}, bf16[512,128]{1,0:T(8,128)(2,1)S(1)}, u32[]{:S(2)}, u32[]{:S(2)}) collective-permute-start(bf16[512,128]{1,0:T(8,128)(2,1)S(1)} %get-tuple-element.58.refs_5_), channel_id=1, source_target_pairs={{0,3},{1,11},{2,1},{3,9},{4,7},{5,15},{6,5},{7,13},{8,2},{9,10},{1... | collective-permute-start | bytes 393224 | tf_op jit(solution)/shard_map/ppermute | solution.py:316
  12.8 14.2 %collective-permute-start.8 = (bf16[512,128]{1,0:T(8,128)(2,1)S(1)}, bf16[512,128]{1,0:T(8,128)(2,1)S(1)}, u32[]{:S(2)}, u32[]{:S(2)}) collective-permute-start(bf16[512,128]{1,0:T(8,128)(2,1)S(1)} %get-tuple-element.59.refs_6_), channel_id=1, source_target_pairs={{0,5},{1,13},{2,7},{3,15},{4,1},{5,9},{6,3},{7,11},{8,4},{9,12},{1... | collective-permute-start | bytes 393224 | tf_op jit(solution)/shard_map/ppermute | solution.py:316
  18.2 22.4 %collective-permute-start.12 = (bf16[520,256]{1,0:T(8,128)(2,1)S(1)}, bf16[520,256]{1,0:T(8,128)(2,1)S(1)}, u32[]{:S(2)}, u32[]{:S(2)}) collective-permute-start(bf16[520,256]{1,0:T(8,128)(2,1)S(1)} %get-tuple-element.70.refs_8_), channel_id=1, source_target_pairs={{0,1},{1,0},{2,3},{3,2},{4,5},{5,4},{6,7},{7,6},{8,9},{9,8},{10,11... | collective-permute-start | bytes 798728 | tf_op jit(solution)/shard_map/ppermute | solution.py:316
  18.3 26.9 %collective-permute-start.16 = (bf16[520,256]{1,0:T(8,128)(2,1)S(1)}, bf16[520,256]{1,0:T(8,128)(2,1)S(1)}, u32[]{:S(2)}, u32[]{:S(2)}) collective-permute-start(bf16[520,256]{1,0:T(8,128)(2,1)S(1)} %get-tuple-element.75), channel_id=1, source_target_pairs={{0,6},{1,7},{2,4},{3,5},{4,2},{5,3},{6,0},{7,1},{8,14},{9,15},{10,... | collective-permute-start | bytes 798728 | tf_op jit(solution)/shard_map/ppermute | solution.py:316
  24.1 21.1 %collective-permute-start.14 = (bf16[520,256]{1,0:T(8,128)(2,1)S(1)}, bf16[520,256]{1,0:T(8,128)(2,1)S(1)}, u32[]{:S(2)}, u32[]{:S(2)}) collective-permute-start(bf16[520,256]{1,0:T(8,128)(2,1)S(1)} %get-tuple-element.73), channel_id=1, source_target_pairs={{0,4},{1,5},{2,6},{3,7},{4,0},{5,1},{6,2},{7,3},{8,12},{9,13},{10,... | collective-permute-start | bytes 798728 | tf_op jit(solution)/shard_map/ppermute | solution.py:316
  25.6 19.7 %collective-permute-start.11 = (bf16[520,256]{1,0:T(8,128)(2,1)S(1)}, bf16[520,256]{1,0:T(8,128)(2,1)S(1)}, u32[]{:S(2)}, u32[]{:S(2)}) collective-permute-start(bf16[520,256]{1,0:T(8,128)(2,1)S(1)} %get-tuple-element.69), channel_id=1, source_target_pairs={{0,2},{1,3},{2,0},{3,1},{4,6},{5,7},{6,4},{7,5},{8,10},{9,11},{10,... | collective-permute-start | bytes 798728 | tf_op jit(solution)/shard_map/ppermute | solution.py:316
  26.9 11.5 %collective-permute-start.9 = (bf16[512,128]{1,0:T(8,128)(2,1)S(1)}, bf16[512,128]{1,0:T(8,128)(2,1)S(1)}, u32[]{:S(2)}, u32[]{:S(2)}) collective-permute-start(bf16[512,128]{1,0:T(8,128)(2,1)S(1)} %get-tuple-element.60.refs_7_), channel_id=1, source_target_pairs={{0,7},{1,15},{2,5},{3,13},{4,3},{5,11},{6,1},{7,9},{8,6},{9,14},{1... | collective-permute-start | bytes 393224 | tf_op jit(solution)/shard_map/ppermute | solution.py:316
  38.4 2.2 %collective-permute-start.2 = (bf16[512,128]{1,0:T(8,128)(2,1)S(1)}, bf16[512,128]{1,0:T(8,128)(2,1)S(1)}, u32[]{:S(2)}, u32[]{:S(2)}) collective-permute-start(bf16[512,128]{1,0:T(8,128)(2,1)S(1)} %get-tuple-element.53.refs_0_), channel_id=1, source_target_pairs={{0,0},{1,8},{2,2},{3,10},{4,4},{5,12},{6,6},{7,14},{8,1},{9,9},{10... | collective-permute-start | bytes 393224 | tf_op jit(solution)/shard_map/ppermute | solution.py:316
  45.2 11.4 %collective-permute-start.13 = (bf16[520,256]{1,0:T(8,128)(2,1)S(1)}, bf16[520,256]{1,0:T(8,128)(2,1)S(1)}, u32[]{:S(2)}, u32[]{:S(2)}) collective-permute-start(bf16[520,256]{1,0:T(8,128)(2,1)S(1)} %collective-permute-done.11.refs_0_), channel_id=1, source_target_pairs={{0,1},{1,0},{2,3},{3,2},{4,5},{5,4},{6,7},{7,6},{8,9},{9,8},{10,11... | collective-permute-start | bytes 798728 | tf_op jit(solution)/shard_map/ppermute | solution.py:316
  52.8 3.8 %collective-permute-start.15 = (bf16[520,256]{1,0:T(8,128)(2,1)S(1)}, bf16[520,256]{1,0:T(8,128)(2,1)S(1)}, u32[]{:S(2)}, u32[]{:S(2)}) collective-permute-start(bf16[520,256]{1,0:T(8,128)(2,1)S(1)} %collective-permute-done.14.refs_2_), channel_id=1, source_target_pairs={{0,1},{1,0},{2,3},{3,2},{4,5},{5,4},{6,7},{7,6},{8,9},{9,8},{10,11... | collective-permute-start | bytes 798728 | tf_op jit(solution)/shard_map/ppermute | solution.py:316
  52.9 3.7 %collective-permute-start.17 = (bf16[520,256]{1,0:T(8,128)(2,1)S(1)}, bf16[520,256]{1,0:T(8,128)(2,1)S(1)}, u32[]{:S(2)}, u32[]{:S(2)}) collective-permute-start(bf16[520,256]{1,0:T(8,128)(2,1)S(1)} %collective-permute-done.16.refs_4_), channel_id=1, source_target_pairs={{0,1},{1,0},{2,3},{3,2},{4,5},{5,4},{6,7},{7,6},{8,9},{9,8},{10,11... | collective-permute-start | bytes 798728 | tf_op jit(solution)/shard_map/ppermute | solution.py:316
  53.3 21.0 %collective-permute-start.19 = (bf16[520,256]{1,0:T(8,128)(2,1)S(1)}, bf16[520,256]{1,0:T(8,128)(2,1)S(1)}, u32[]{:S(2)}, u32[]{:S(2)}) collective-permute-start(bf16[520,256]{1,0:T(8,128)(2,1)S(1)} %get-tuple-element.81), channel_id=1, source_target_pairs={{0,10},{1,11},{2,8},{3,9},{4,14},{5,15},{6,12},{7,13},{8,2},{9,3},... | collective-permute-start | bytes 798728 | tf_op jit(solution)/shard_map/ppermute | solution.py:316
  53.5 25.8 %collective-permute-start = (bf16[520,256]{1,0:T(8,128)(2,1)S(1)}, bf16[520,256]{1,0:T(8,128)(2,1)S(1)}, u32[]{:S(2)}, u32[]{:S(2)}) collective-permute-start(bf16[520,256]{1,0:T(8,128)(2,1)S(1)} %get-tuple-element.65), channel_id=1, source_target_pairs={{0,8},{1,9},{2,10},{3,11},{4,12},{5,13},{6,14},{7,15},{8,0},{9,1},... | collective-permute-start | bytes 798728 | tf_op jit(solution)/shard_map/ppermute | solution.py:316
  79.3 2.3 %collective-permute-start.18 = (bf16[520,256]{1,0:T(8,128)(2,1)S(1)}, bf16[520,256]{1,0:T(8,128)(2,1)S(1)}, u32[]{:S(2)}, u32[]{:S(2)}) collective-permute-start(bf16[520,256]{1,0:T(8,128)(2,1)S(1)} %collective-permute-done.refs_0_), channel_id=1, source_target_pairs={{0,1},{1,0},{2,3},{3,2},{4,5},{5,4},{6,7},{7,6},{8,9},{9,8},{10,11... | collective-permute-start | bytes 798728 | tf_op jit(solution)/shard_map/ppermute | solution.py:316
  79.3 2.3 %collective-permute-start.20 = (bf16[520,256]{1,0:T(8,128)(2,1)S(1)}, bf16[520,256]{1,0:T(8,128)(2,1)S(1)}, u32[]{:S(2)}, u32[]{:S(2)}) collective-permute-start(bf16[520,256]{1,0:T(8,128)(2,1)S(1)} %collective-permute-done.19.refs_2_), channel_id=1, source_target_pairs={{0,1},{1,0},{2,3},{3,2},{4,5},{5,4},{6,7},{7,6},{8,9},{9,8},{10,11... | collective-permute-start | bytes 798728 | tf_op jit(solution)/shard_map/ppermute | solution.py:316
  79.8 10.2 %collective-permute-start.10 = (bf16[520,256]{1,0:T(8,128)(2,1)S(1)}, bf16[520,256]{1,0:T(8,128)(2,1)S(1)}, u32[]{:S(2)}, u32[]{:S(2)}) collective-permute-start(bf16[520,256]{1,0:T(8,128)(2,1)S(1)} %get-tuple-element.68), channel_id=1, source_target_pairs={{0,12},{1,13},{2,14},{3,15},{4,8},{5,9},{6,10},{7,11},{8,4},{9,5},... | collective-permute-start | bytes 798728 | tf_op jit(solution)/shard_map/ppermute | solution.py:316
  90.0 2.0 %collective-permute-start.21 = (bf16[520,256]{1,0:T(8,128)(2,1)S(1)}, bf16[520,256]{1,0:T(8,128)(2,1)S(1)}, u32[]{:S(2)}, u32[]{:S(2)}) collective-permute-start(bf16[520,256]{1,0:T(8,128)(2,1)S(1)} %collective-permute-done.10.refs_0_), channel_id=1, source_target_pairs={{0,1},{1,0},{2,3},{3,2},{4,5},{5,4},{6,7},{7,6},{8,9},{9,8},{10,11... | collective-permute-start | bytes 798728 | tf_op jit(solution)/shard_map/ppermute | solution.py:316
  90.0 11.6 %collective-permute-start.1 = (bf16[520,256]{1,0:T(8,128)(2,1)S(1)}, bf16[520,256]{1,0:T(8,128)(2,1)S(1)}, u32[]{:S(2)}, u32[]{:S(2)}) collective-permute-start(bf16[520,256]{1,0:T(8,128)(2,1)S(1)} %get-tuple-element.66), channel_id=1, source_target_pairs={{0,14},{1,15},{2,12},{3,13},{4,10},{5,11},{6,8},{7,9},{8,6},{9,7},... | collective-permute-start | bytes 798728 | tf_op jit(solution)/shard_map/ppermute | solution.py:316
  101.6 1.5 %collective-permute-start.22 = (bf16[520,256]{1,0:T(8,128)(2,1)S(1)}, bf16[520,256]{1,0:T(8,128)(2,1)S(1)}, u32[]{:S(2)}, u32[]{:S(2)}) collective-permute-start(bf16[520,256]{1,0:T(8,128)(2,1)S(1)} %collective-permute-done.1.refs_0_), channel_id=1, source_target_pairs={{0,1},{1,0},{2,3},{3,2},{4,5},{5,4},{6,7},{7,6},{8,9},{9,8},{10,11... | collective-permute-start | bytes 798728 | tf_op jit(solution)/shard_map/ppermute | solution.py:316
  106.6 13.4 %collective-permute-start.23 = (bf16[528,128]{1,0:T(8,128)(2,1)S(1)}, bf16[528,128]{1,0:T(8,128)(2,1)S(1)}, u32[]{:S(2)}, u32[]{:S(2)}) collective-permute-start(bf16[528,128]{1,0:T(8,128)(2,1)S(1)} %get-tuple-element.93), channel_id=1, source_target_pairs={{0,0},{8,1},{2,2},{10,3},{4,4},{12,5},{6,6},{14,7},{1,8},{9,9},{3,... | collective-permute-start | bytes 405512 | tf_op jit(solution)/shard_map/ppermute | solution.py:316
  107.3 13.8 %collective-permute-start.24 = (bf16[528,128]{1,0:T(8,128)(2,1)S(1)}, bf16[528,128]{1,0:T(8,128)(2,1)S(1)}, u32[]{:S(2)}, u32[]{:S(2)}) collective-permute-start(bf16[528,128]{1,0:T(8,128)(2,1)S(1)} %get-tuple-element.94), channel_id=1, source_target_pairs={{2,0},{10,1},{0,2},{8,3},{6,4},{14,5},{4,6},{12,7},{3,8},{11,9},{1... | collective-permute-start | bytes 405512 | tf_op jit(solution)/shard_map/ppermute | solution.py:316
  108.6 15.5 %collective-permute-start.25 = (bf16[528,128]{1,0:T(8,128)(2,1)S(1)}, bf16[528,128]{1,0:T(8,128)(2,1)S(1)}, u32[]{:S(2)}, u32[]{:S(2)}) collective-permute-start(bf16[528,128]{1,0:T(8,128)(2,1)S(1)} %get-tuple-element.95), channel_id=1, source_target_pairs={{4,0},{12,1},{6,2},{14,3},{0,4},{8,5},{2,6},{10,7},{5,8},{13,9},{7... | collective-permute-start | bytes 405512 | tf_op jit(solution)/shard_map/ppermute | solution.py:316
  114.3 13.6 %collective-permute-start.26 = (bf16[528,128]{1,0:T(8,128)(2,1)S(1)}, bf16[528,128]{1,0:T(8,128)(2,1)S(1)}, u32[]{:S(2)}, u32[]{:S(2)}) collective-permute-start(bf16[528,128]{1,0:T(8,128)(2,1)S(1)} %get-tuple-element.96), channel_id=1, source_target_pairs={{6,0},{14,1},{4,2},{12,3},{2,4},{10,5},{0,6},{8,7},{7,8},{15,9},{5... | collective-permute-start | bytes 405512 | tf_op jit(solution)/shard_map/ppermute | solution.py:316
  114.6 13.3 %collective-permute-start.27 = (bf16[528,128]{1,0:T(8,128)(2,1)S(1)}, bf16[528,128]{1,0:T(8,128)(2,1)S(1)}, u32[]{:S(2)}, u32[]{:S(2)}) collective-permute-start(bf16[528,128]{1,0:T(8,128)(2,1)S(1)} %get-tuple-element.97), channel_id=1, source_target_pairs={{1,0},{9,1},{3,2},{11,3},{5,4},{13,5},{7,6},{15,7},{0,8},{8,9},{2,... | collective-permute-start | bytes 405512 | tf_op jit(solution)/shard_map/ppermute | solution.py:316
  120.0 7.8 %collective-permute-start.28 = (bf16[528,128]{1,0:T(8,128)(2,1)S(1)}, bf16[528,128]{1,0:T(8,128)(2,1)S(1)}, u32[]{:S(2)}, u32[]{:S(2)}) collective-permute-start(bf16[528,128]{1,0:T(8,128)(2,1)S(1)} %get-tuple-element.98), channel_id=1, source_target_pairs={{3,0},{11,1},{1,2},{9,3},{7,4},{15,5},{5,6},{13,7},{2,8},{10,9},{0... | collective-permute-start | bytes 405512 | tf_op jit(solution)/shard_map/ppermute | solution.py:316
  121.2 7.1 %collective-permute-start.29 = (bf16[528,128]{1,0:T(8,128)(2,1)S(1)}, bf16[528,128]{1,0:T(8,128)(2,1)S(1)}, u32[]{:S(2)}, u32[]{:S(2)}) collective-permute-start(bf16[528,128]{1,0:T(8,128)(2,1)S(1)} %get-tuple-element.99), channel_id=1, source_target_pairs={{5,0},{13,1},{7,2},{15,3},{1,4},{9,5},{3,6},{11,7},{4,8},{12,9},{6... | collective-permute-start | bytes 405512 | tf_op jit(solution)/shard_map/ppermute | solution.py:316
  124.1 14.6 %collective-permute-start.30 = (bf16[528,128]{1,0:T(8,128)(2,1)S(1)}, bf16[528,128]{1,0:T(8,128)(2,1)S(1)}, u32[]{:S(2)}, u32[]{:S(2)}) collective-permute-start(bf16[528,128]{1,0:T(8,128)(2,1)S(1)} %get-tuple-element.100), channel_id=1, source_target_pairs={{7,0},{15,1},{5,2},{13,3},{3,4},{11,5},{1,6},{9,7},{6,8},{14,9},{4... | collective-permute-start | bytes 405512 | tf_op jit(solution)/shard_map/ppermute | solution.py:316
  (6 other events, 42.0 us)

commit v5 on v4

--- a/solution.py
+++ b/solution.py
@@ -407,15 +407,17 @@
         pltpu.VMEM((n_req, tiles, half_width, HD), bf16),
     ]
     part_shapes = [jax.ShapeDtypeStruct((width + STATS, HD), bf16)] * n_req
-    state = []
-    for index, masks in enumerate(groups):
+    parts = [[(mask, back) for mask in masks for back in range(n_sub)] for masks in groups]
+    parts[-1:] = [parts[-1][:1], parts[-1][1:]]
+    state, gate = [], []
+    for index, buffers in enumerate(parts):
         if index == 1:
             for mask in range(half + 3, kv_heads):
                 if mask not in landed:
                     landed[mask] = at_head(mask, landed[half])
-        arrived = [from_sub(mask, back, *state[-1:]) for mask in masks for back in range(n_sub)]
-        buffers = [(mask, back) for mask in masks for back in range(n_sub)]
-        first, last = index == 0, index == len(groups) - 1
+        first, last = index == 0, index == len(parts) - 1
+        gate = gate if last else state[-1:]
+        arrived = [from_sub(mask, back, *gate) for mask, back in buffers]
         blocks = len(buffers) * blk_dev
         inputs = [*(held_queries if first else []), *arrived]
         results = pl.pallas_call(

time: 141 us -> 141 us (level)
    pallas_call x5 -> x6, Pallas kernels: 20.3 us -> 21.4 us  [shards(): pl.pallas_call(functools.partial(attend, n_sub, len(buffers), first, last...]
  transfers between devices with their start and end apart: 31 -> 31, of which waited for: 10 -> 9; matrix products, arithmetic and copies ran while one was open for 0% -> 0% of each run, Pallas kernels for 14% -> 16%
where the time goes in v5:
time: 141 us
  waiting for transfers between devices  58.2 us (41%)
  starting transfers between devices  50.1 us (36%)
  Pallas kernels  27.6 us (20%)
  local copies, waits for them, and re-layouts  4.82 us (3%)
    ppermute x31, waiting for transfers between devices, moved(): return lax.ppermute(x, 'shard', pairs)  58.2 us
    ppermute x31, starting transfers between devices, moved(): return lax.ppermute(x, 'shard', pairs)  50.1 us
    pallas_call x6, Pallas kernels, shards(): pl.pallas_call(functools.partial(attend, n_sub, len(buffers), first, last...  21.4 us
    unnamed x14, local copies, waits for them, and re-layouts  4.82 us
  transfers between devices with their start and end apart: 31, of which 9 were waited for; matrix products, arithmetic and copies ran while one was open for 0% of the time, Pallas kernels for 16%

profile of v5, /device:TPU:0, one launch (start us, length us, event | category | flops | bytes accessed | tf_op | source)
XLA Modules:
  0.0 140.9 jit_solution(17873692555506795081)
XLA Ops:
  0.0 1.2 copy-done.2
  2.9 3.1 %collective-permute-start.3 = (bf16[512,128]{1,0:T(8,128)(2,1)S(1)}, bf16[512,128]{1,0:T(8,128)(2,1)S(1)}, u32[]{:S(2)}, u32[]{:S(2)}) collective-permute-start(bf16[512,128]{1,0:T(8,128)(2,1)S(1)} %get-tuple-element.57.refs_1_), channel_id=1, source_target_pairs={{0,2},{1,10},{2,0},{3,8},{4,6},{5,14},{6,4},{7,12},{8,3},{9,11},{1... | collective-permute-start | bytes 393224 | tf_op jit(solution)/shard_map/ppermute | solution.py:316
  6.0 1.6 %collective-permute-start.4 = (bf16[512,128]{1,0:T(8,128)(2,1)S(1)}, bf16[512,128]{1,0:T(8,128)(2,1)S(1)}, u32[]{:S(2)}, u32[]{:S(2)}) collective-permute-start(bf16[512,128]{1,0:T(8,128)(2,1)S(1)} %get-tuple-element.58.refs_2_), channel_id=1, source_target_pairs={{0,4},{1,12},{2,6},{3,14},{4,0},{5,8},{6,2},{7,10},{8,5},{9,13},{1... | collective-permute-start | bytes 393224 | tf_op jit(solution)/shard_map/ppermute | solution.py:316
  7.6 4.0 %collective-permute-start.6 = (bf16[512,128]{1,0:T(8,128)(2,1)S(1)}, bf16[512,128]{1,0:T(8,128)(2,1)S(1)}, u32[]{:S(2)}, u32[]{:S(2)}) collective-permute-start(bf16[512,128]{1,0:T(8,128)(2,1)S(1)} %get-tuple-element.60.refs_4_), channel_id=1, source_target_pairs={{0,1},{1,9},{2,3},{3,11},{4,5},{5,13},{6,7},{7,15},{8,0},{9,8},{10... | collective-permute-start | bytes 393224 | tf_op jit(solution)/shard_map/ppermute | solution.py:316
  13.7 1.6 %copy-done = bf16[2,256,2048]{2,1,0:T(8,128)(2,1)S(1)} copy-done((bf16[2,256,2048]{2,1,0:T(8,128)(2,1)S(1)}, bf16[2,256,2048]{2,1,0:T(8,128)(2,1)}, u32[]{:S(2)}) %copy-start) | copy-done | bytes 2097176
  16.6 1.6 %pack_kv.1 = (bf16[520,256]{1,0:T(8,128)(2,1)S(1)}, bf16[520,256]{1,0:T(8,128)(2,1)S(1)}, bf16[520,256]{1,0:T(8,128)(2,1)S(1)}, bf16[520,256]{1,0:T(8,128)(2,1)S...) custom-call(s32[2]{0:T(128)S(1)} %copy-done.5, ...), custom_call_target="tpu_custom_call" | custom-call | tf_op jit(solution)/shard_map/pack_kv/pallas_call | solution.py:366
  19.1 5.0 %collective-permute-done.6.refs_4_ = bf16[512,128]{1,0:T(8,128)(2,1)S(1)} collective-permute-done((bf16[512,128]{1,0:T(8,128)(2,1)S(1)}, bf16[512,128]{1,0:T(8,128)(2,1)S(1)}, u32[]{:S(2)}, u32[]{:S(2)}) %collective-permute-start.6) | collective-permute-done | bytes 131104 | tf_op jit(solution)/shard_map/ppermute | solution.py:316
  24.1 1.5 %collective-permute-done.7.refs_5_ = bf16[512,128]{1,0:T(8,128)(2,1)S(1)} collective-permute-done((bf16[512,128]{1,0:T(8,128)(2,1)S(1)}, bf16[512,128]{1,0:T(8,128)(2,1)S(1)}, u32[]{:S(2)}, u32[]{:S(2)}) %collective-permute-start.7) | collective-permute-done | bytes 131104 | tf_op jit(solution)/shard_map/ppermute | solution.py:316
  25.6 1.4 collective-permute-start.11
  26.9 11.5 %collective-permute-done.9.refs_7_ = bf16[512,128]{1,0:T(8,128)(2,1)S(1)} collective-permute-done((bf16[512,128]{1,0:T(8,128)(2,1)S(1)}, bf16[512,128]{1,0:T(8,128)(2,1)S(1)}, u32[]{:S(2)}, u32[]{:S(2)}) %collective-permute-start.9) | collective-permute-done | bytes 131104 | tf_op jit(solution)/shard_map/ppermute | solution.py:316
  39.1 1.5 %own_scores.1 = (f32[128,128]{1,0:T(8,128)S(1)}, s32[16,1,256]{2,1,0:T(1,128)S(1)}) custom-call(s32[8,128]{1,0:T(8,128)S(1)} %copy-done.4, bf16[128,1024]{1,0:T(8,128)(2,1)S(1)} %copy-done.1, bf16[512,128]{1,0:T(8,128)(2,1)S(1)} %get-tuple-element.56.refs_0_, bf16[512,128]{1,0:T(8,128)(2,1)S(1)} %get-tuple-element.57.refs_1_, ...), custom_call_target="tpu_custom_call" | custom-call | tf_op jit(solution)/shard_map/own_scores/pallas_call | solution.py:353
  40.6 4.6 %shard_map.64 = (f32[16,136,256]{2,1,0:T(8,128)S(1)}, f32[16,1,256]{2,1,0:T(1,128)S(1)}, bf16[8,2,256,128]{3,2,1,0:T(8,128)(2,1)S(1)}) custom-call(s32[8,128]{1,0:T(8,128)S(1)} %copy-done.4, s32[16,1,256]{2,1,0:T(1,128)S(1)} %get-tuple-element.65.wide_ref, bf16[512,128]{1,0:T(8,128)(2,1)S(1)} %collective-permute-done.2.refs_0_, ...), custom_call_target="tpu_custom_call" | custom-call | tf_op jit(solution)/shard_map/pallas_call | solution.py:423
  45.2 7.6 %collective-permute-start.13 = (bf16[520,256]{1,0:T(8,128)(2,1)S(1)}, bf16[520,256]{1,0:T(8,128)(2,1)S(1)}, u32[]{:S(2)}, u32[]{:S(2)}) collective-permute-start(bf16[520,256]{1,0:T(8,128)(2,1)S(1)} %collective-permute-done.11.refs_0_), channel_id=1, source_target_pairs={{0,1},{1,0},{2,3},{3,2},{4,5},{5,4},{6,7},{7,6},{8,9},{9,8},{10,11... | collective-permute-start | bytes 798728 | tf_op jit(solution)/shard_map/ppermute | solution.py:316
  53.5 3.1 %collective-permute-start = (bf16[520,256]{1,0:T(8,128)(2,1)S(1)}, bf16[520,256]{1,0:T(8,128)(2,1)S(1)}, u32[]{:S(2)}, u32[]{:S(2)}) collective-permute-start(bf16[520,256]{1,0:T(8,128)(2,1)S(1)} %get-tuple-element.68), channel_id=1, source_target_pairs={{0,8},{1,9},{2,10},{3,11},{4,12},{5,13},{6,14},{7,15},{8,0},{9,1},... | collective-permute-start | bytes 798728 | tf_op jit(solution)/shard_map/ppermute | solution.py:316
  56.6 5.2 %shard_map.65 = (f32[16,136,256]{2,1,0:T(8,128)S(1)}, f32[16,1,256]{2,1,0:T(1,128)S(1)}, bf16[8,2,256,128]{3,2,1,0:T(8,128)(2,1)S(1)}) custom-call(s32[8,128]{1,0:T(8,128)S(1)} %copy-done.4, s32[16,1,256]{2,1,0:T(1,128)S(1)} %get-tuple-element.65.wide_ref, ...), custom_call_target="tpu_custom_call", output_to_operand_aliasing={{0}: (8, {}), {1}: (9, {}), {2}: (10, {})} | custom-call | tf_op jit(solution)/shard_map/pallas_call | solution.py:423
  61.8 12.6 %collective-permute-done.19.refs_2_ = bf16[520,256]{1,0:T(8,128)(2,1)S(1)} collective-permute-done((bf16[520,256]{1,0:T(8,128)(2,1)S(1)}, bf16[520,256]{1,0:T(8,128)(2,1)S(1)}, u32[]{:S(2)}, u32[]{:S(2)}) %collective-permute-start.19) | collective-permute-done | bytes 266272 | tf_op jit(solution)/shard_map/ppermute | solution.py:316
  74.3 5.0 %collective-permute-done.refs_0_ = bf16[520,256]{1,0:T(8,128)(2,1)S(1)} collective-permute-done((bf16[520,256]{1,0:T(8,128)(2,1)S(1)}, bf16[520,256]{1,0:T(8,128)(2,1)S(1)}, u32[]{:S(2)}, u32[]{:S(2)}) %collective-permute-start) | collective-permute-done | bytes 266272 | tf_op jit(solution)/shard_map/ppermute | solution.py:316
  79.8 1.8 %collective-permute-start.10 = (bf16[520,256]{1,0:T(8,128)(2,1)S(1)}, bf16[520,256]{1,0:T(8,128)(2,1)S(1)}, u32[]{:S(2)}, u32[]{:S(2)}) collective-permute-start(bf16[520,256]{1,0:T(8,128)(2,1)S(1)} %get-tuple-element.71), channel_id=1, source_target_pairs={{0,12},{1,13},{2,14},{3,15},{4,8},{5,9},{6,10},{7,11},{8,4},{9,5},... | collective-permute-start | bytes 798728 | tf_op jit(solution)/shard_map/ppermute | solution.py:316
  81.6 4.1 %shard_map.66 = (f32[16,136,256]{2,1,0:T(8,128)S(1)}, f32[16,1,256]{2,1,0:T(1,128)S(1)}, bf16[8,2,256,128]{3,2,1,0:T(8,128)(2,1)S(1)}) custom-call(s32[8,128]{1,0:T(8,128)S(1)} %copy-done.4, s32[16,1,256]{2,1,0:T(1,128)S(1)} %get-tuple-element.65.wide_ref, ...), custom_call_target="tpu_custom_call", output_to_operand_aliasing={{0}: (6, {}), {1}: (7, {}), {2}: (8, {})} | custom-call | tf_op jit(solution)/shard_map/pallas_call | solution.py:423
  85.7 4.3 %collective-permute-done.10.refs_0_ = bf16[520,256]{1,0:T(8,128)(2,1)S(1)} collective-permute-done((bf16[520,256]{1,0:T(8,128)(2,1)S(1)}, bf16[520,256]{1,0:T(8,128)(2,1)S(1)}, u32[]{:S(2)}, u32[]{:S(2)}) %collective-permute-start.10) | collective-permute-done | bytes 266272 | tf_op jit(solution)/shard_map/ppermute | solution.py:316
  90.0 2.0 %collective-permute-start.1 = (bf16[520,256]{1,0:T(8,128)(2,1)S(1)}, bf16[520,256]{1,0:T(8,128)(2,1)S(1)}, u32[]{:S(2)}, u32[]{:S(2)}) collective-permute-start(bf16[520,256]{1,0:T(8,128)(2,1)S(1)} %get-tuple-element.69), channel_id=1, source_target_pairs={{0,14},{1,15},{2,12},{3,13},{4,10},{5,11},{6,8},{7,9},{8,6},{9,7},... | collective-permute-start | bytes 798728 | tf_op jit(solution)/shard_map/ppermute | solution.py:316
  92.0 3.1 %shard_map.67 = (f32[16,136,256]{2,1,0:T(8,128)S(1)}, f32[16,1,256]{2,1,0:T(1,128)S(1)}, bf16[8,2,256,128]{3,2,1,0:T(8,128)(2,1)S(1)}) custom-call(s32[8,128]{1,0:T(8,128)S(1)} %copy-done.4, s32[16,1,256]{2,1,0:T(1,128)S(1)} %get-tuple-element.65.wide_ref, ...), custom_call_target="tpu_custom_call", output_to_operand_aliasing={{0}: (4, {}), {1}: (5, {}), {2}: (6, {})} | custom-call | tf_op jit(solution)/shard_map/pallas_call | solution.py:423
  95.1 6.6 %collective-permute-done.1.refs_0_ = bf16[520,256]{1,0:T(8,128)(2,1)S(1)} collective-permute-done((bf16[520,256]{1,0:T(8,128)(2,1)S(1)}, bf16[520,256]{1,0:T(8,128)(2,1)S(1)}, u32[]{:S(2)}, u32[]{:S(2)}) %collective-permute-start.1) | collective-permute-done | bytes 266272 | tf_op jit(solution)/shard_map/ppermute | solution.py:316
  101.7 2.1 %shard_map.68 = (f32[16,136,256]{2,1,0:T(8,128)S(1)}, f32[16,1,256]{2,1,0:T(1,128)S(1)}, bf16[8,2,256,128]{3,2,1,0:T(8,128)(2,1)S(1)}) custom-call(s32[8,128]{1,0:T(8,128)S(1)} %copy-done.4, s32[16,1,256]{2,1,0:T(1,128)S(1)} %get-tuple-element.65.wide_ref, ...), custom_call_target="tpu_custom_call", output_to_operand_aliasing={{0}: (3, {}), {1}: (4, {}), {2}: (5, {})} | custom-call | tf_op jit(solution)/shard_map/pallas_call | solution.py:423
  103.7 2.5 %shard_map.69 = (bf16[528,128]{1,0:T(8,128)(2,1)S(1)}, bf16[528,128]{1,0:T(8,128)(2,1)S(1)}, bf16[528,128]{1,0:T(8,128)(2,1)S(1)}, bf16[528,128]{1,0:T(8,128)(2,...) custom-call(s32[8,128]{1,0:T(8,128)S(1)} %copy-done.4, ...), custom_call_target="tpu_custom_call", output_to_operand_aliasing={{8}: (3, {}), {9}: (4, {}), {10}: (5, {})} | custom-call | tf_op jit(solution)/shard_map/pallas_call | solution.py:423
  106.9 1.3 collective-permute-start.24
  108.2 6.1 %collective-permute-start.25 = (bf16[528,128]{1,0:T(8,128)(2,1)S(1)}, bf16[528,128]{1,0:T(8,128)(2,1)S(1)}, u32[]{:S(2)}, u32[]{:S(2)}) collective-permute-start(bf16[528,128]{1,0:T(8,128)(2,1)S(1)} %get-tuple-element.101), channel_id=1, source_target_pairs={{4,0},{12,1},{6,2},{14,3},{0,4},{8,5},{2,6},{10,7},{5,8},{13,9},{7... | collective-permute-start | bytes 405512 | tf_op jit(solution)/shard_map/ppermute | solution.py:316
  114.6 5.0 %collective-permute-start.27 = (bf16[528,128]{1,0:T(8,128)(2,1)S(1)}, bf16[528,128]{1,0:T(8,128)(2,1)S(1)}, u32[]{:S(2)}, u32[]{:S(2)}) collective-permute-start(bf16[528,128]{1,0:T(8,128)(2,1)S(1)} %get-tuple-element.103), channel_id=1, source_target_pairs={{1,0},{9,1},{3,2},{11,3},{5,4},{13,5},{7,6},{15,7},{0,8},{8,9},{2,... | collective-permute-start | bytes 405512 | tf_op jit(solution)/shard_map/ppermute | solution.py:316
  120.4 4.3 %collective-permute-start.29 = (bf16[528,128]{1,0:T(8,128)(2,1)S(1)}, bf16[528,128]{1,0:T(8,128)(2,1)S(1)}, u32[]{:S(2)}, u32[]{:S(2)}) collective-permute-start(bf16[528,128]{1,0:T(8,128)(2,1)S(1)} %get-tuple-element.105), channel_id=1, source_target_pairs={{5,0},{13,1},{7,2},{15,3},{1,4},{9,5},{3,6},{11,7},{4,8},{12,9},{6... | collective-permute-start | bytes 405512 | tf_op jit(solution)/shard_map/ppermute | solution.py:316
  124.6 2.4 %collective-permute-start.30 = (bf16[528,128]{1,0:T(8,128)(2,1)S(1)}, bf16[528,128]{1,0:T(8,128)(2,1)S(1)}, u32[]{:S(2)}, u32[]{:S(2)}) collective-permute-start(bf16[528,128]{1,0:T(8,128)(2,1)S(1)} %get-tuple-element.106), channel_id=1, source_target_pairs={{7,0},{15,1},{5,2},{13,3},{3,4},{11,5},{1,6},{9,7},{6,8},{14,9},{4... | collective-permute-start | bytes 405512 | tf_op jit(solution)/shard_map/ppermute | solution.py:316
  127.8 11.0 %collective-permute-done.30.refs_7_ = bf16[528,128]{1,0:T(8,128)(2,1)S(1)} collective-permute-done((bf16[528,128]{1,0:T(8,128)(2,1)S(1)}, bf16[528,128]{1,0:T(8,128)(2,1)S(1)}, u32[]{:S(2)}, u32[]{:S(2)}) %collective-permute-start.30) | collective-permute-done | bytes 135200 | tf_op jit(solution)/shard_map/ppermute | solution.py:316
  138.8 2.1 %merge_own.1 = bf16[128,4096]{1,0:T(8,128)(2,1)} custom-call(f32[128,128]{1,0:T(8,128)S(1)} %get-tuple-element.64.own_ref, bf16[128,1024]{1,0:T(8,128)(2,1)S(1)} %copy-done.1, bf16[528,128]{1,0:T(8,128)(2,1)S(1)} %collective-permute-done.23.refs_0_, bf16[528,128]{1,0:T(8,128)(2,1)S(1)} %collective-permute-done.24.refs_1_, ...), custom_call_target="tpu_custom_call" | custom-call | tf_op jit(solution)/shard_map/merge_own/pallas_call | solution.py:444
  (54 shorter events, 10.3 us)
Async XLA Ops:
  1.9 37.2 %copy-start.4 = (s32[8,128]{1,0:T(8,128)S(1)}, s32[8,128]{1,0:T(8,128)}, u32[]{:S(2)}) copy-start(s32[8,128]{1,0:T(8,128)} %rows_smem.11) | copy-start | bytes 12292
  2.9 9.8 %collective-permute-start.3 = (bf16[512,128]{1,0:T(8,128)(2,1)S(1)}, bf16[512,128]{1,0:T(8,128)(2,1)S(1)}, u32[]{:S(2)}, u32[]{:S(2)}) collective-permute-start(bf16[512,128]{1,0:T(8,128)(2,1)S(1)} %get-tuple-element.57.refs_1_), channel_id=1, source_target_pairs={{0,2},{1,10},{2,0},{3,8},{4,6},{5,14},{6,4},{7,12},{8,3},{9,11},{1... | collective-permute-start | bytes 393224 | tf_op jit(solution)/shard_map/ppermute | solution.py:316
  6.0 12.2 %collective-permute-start.4 = (bf16[512,128]{1,0:T(8,128)(2,1)S(1)}, bf16[512,128]{1,0:T(8,128)(2,1)S(1)}, u32[]{:S(2)}, u32[]{:S(2)}) collective-permute-start(bf16[512,128]{1,0:T(8,128)(2,1)S(1)} %get-tuple-element.58.refs_2_), channel_id=1, source_target_pairs={{0,4},{1,12},{2,6},{3,14},{4,0},{5,8},{6,2},{7,10},{8,5},{9,13},{1... | collective-permute-start | bytes 393224 | tf_op jit(solution)/shard_map/ppermute | solution.py:316
  7.6 10.7 %collective-permute-start.5 = (bf16[512,128]{1,0:T(8,128)(2,1)S(1)}, bf16[512,128]{1,0:T(8,128)(2,1)S(1)}, u32[]{:S(2)}, u32[]{:S(2)}) collective-permute-start(bf16[512,128]{1,0:T(8,128)(2,1)S(1)} %get-tuple-element.59.refs_3_), channel_id=1, source_target_pairs={{0,6},{1,14},{2,4},{3,12},{4,2},{5,10},{6,0},{7,8},{8,7},{9,15},{1... | collective-permute-start | bytes 393224 | tf_op jit(solution)/shard_map/ppermute | solution.py:316
  7.6 16.5 %collective-permute-start.6 = (bf16[512,128]{1,0:T(8,128)(2,1)S(1)}, bf16[512,128]{1,0:T(8,128)(2,1)S(1)}, u32[]{:S(2)}, u32[]{:S(2)}) collective-permute-start(bf16[512,128]{1,0:T(8,128)(2,1)S(1)} %get-tuple-element.60.refs_4_), channel_id=1, source_target_pairs={{0,1},{1,9},{2,3},{3,11},{4,5},{5,13},{6,7},{7,15},{8,0},{9,8},{10... | collective-permute-start | bytes 393224 | tf_op jit(solution)/shard_map/ppermute | solution.py:316
  11.6 13.9 %collective-permute-start.7 = (bf16[512,128]{1,0:T(8,128)(2,1)S(1)}, bf16[512,128]{1,0:T(8,128)(2,1)S(1)}, u32[]{:S(2)}, u32[]{:S(2)}) collective-permute-start(bf16[512,128]{1,0:T(8,128)(2,1)S(1)} %get-tuple-element.61.refs_5_), channel_id=1, source_target_pairs={{0,3},{1,11},{2,1},{3,9},{4,7},{5,15},{6,5},{7,13},{8,2},{9,10},{1... | collective-permute-start | bytes 393224 | tf_op jit(solution)/shard_map/ppermute | solution.py:316
  12.8 14.2 %collective-permute-start.8 = (bf16[512,128]{1,0:T(8,128)(2,1)S(1)}, bf16[512,128]{1,0:T(8,128)(2,1)S(1)}, u32[]{:S(2)}, u32[]{:S(2)}) collective-permute-start(bf16[512,128]{1,0:T(8,128)(2,1)S(1)} %get-tuple-element.62.refs_6_), channel_id=1, source_target_pairs={{0,5},{1,13},{2,7},{3,15},{4,1},{5,9},{6,3},{7,11},{8,4},{9,12},{1... | collective-permute-start | bytes 393224 | tf_op jit(solution)/shard_map/ppermute | solution.py:316
  18.2 22.4 %collective-permute-start.12 = (bf16[520,256]{1,0:T(8,128)(2,1)S(1)}, bf16[520,256]{1,0:T(8,128)(2,1)S(1)}, u32[]{:S(2)}, u32[]{:S(2)}) collective-permute-start(bf16[520,256]{1,0:T(8,128)(2,1)S(1)} %get-tuple-element.73.refs_8_), channel_id=1, source_target_pairs={{0,1},{1,0},{2,3},{3,2},{4,5},{5,4},{6,7},{7,6},{8,9},{9,8},{10,11... | collective-permute-start | bytes 798728 | tf_op jit(solution)/shard_map/ppermute | solution.py:316
  18.3 26.9 %collective-permute-start.16 = (bf16[520,256]{1,0:T(8,128)(2,1)S(1)}, bf16[520,256]{1,0:T(8,128)(2,1)S(1)}, u32[]{:S(2)}, u32[]{:S(2)}) collective-permute-start(bf16[520,256]{1,0:T(8,128)(2,1)S(1)} %get-tuple-element.78), channel_id=1, source_target_pairs={{0,6},{1,7},{2,4},{3,5},{4,2},{5,3},{6,0},{7,1},{8,14},{9,15},{10,... | collective-permute-start | bytes 798728 | tf_op jit(solution)/shard_map/ppermute | solution.py:316
  24.1 21.1 %collective-permute-start.14 = (bf16[520,256]{1,0:T(8,128)(2,1)S(1)}, bf16[520,256]{1,0:T(8,128)(2,1)S(1)}, u32[]{:S(2)}, u32[]{:S(2)}) collective-permute-start(bf16[520,256]{1,0:T(8,128)(2,1)S(1)} %get-tuple-element.76), channel_id=1, source_target_pairs={{0,4},{1,5},{2,6},{3,7},{4,0},{5,1},{6,2},{7,3},{8,12},{9,13},{10,... | collective-permute-start | bytes 798728 | tf_op jit(solution)/shard_map/ppermute | solution.py:316
  25.6 19.7 %collective-permute-start.11 = (bf16[520,256]{1,0:T(8,128)(2,1)S(1)}, bf16[520,256]{1,0:T(8,128)(2,1)S(1)}, u32[]{:S(2)}, u32[]{:S(2)}) collective-permute-start(bf16[520,256]{1,0:T(8,128)(2,1)S(1)} %get-tuple-element.72), channel_id=1, source_target_pairs={{0,2},{1,3},{2,0},{3,1},{4,6},{5,7},{6,4},{7,5},{8,10},{9,11},{10,... | collective-permute-start | bytes 798728 | tf_op jit(solution)/shard_map/ppermute | solution.py:316
  26.9 11.5 %collective-permute-start.9 = (bf16[512,128]{1,0:T(8,128)(2,1)S(1)}, bf16[512,128]{1,0:T(8,128)(2,1)S(1)}, u32[]{:S(2)}, u32[]{:S(2)}) collective-permute-start(bf16[512,128]{1,0:T(8,128)(2,1)S(1)} %get-tuple-element.63.refs_7_), channel_id=1, source_target_pairs={{0,7},{1,15},{2,5},{3,13},{4,3},{5,11},{6,1},{7,9},{8,6},{9,14},{1... | collective-permute-start | bytes 393224 | tf_op jit(solution)/shard_map/ppermute | solution.py:316
  38.4 2.2 %collective-permute-start.2 = (bf16[512,128]{1,0:T(8,128)(2,1)S(1)}, bf16[512,128]{1,0:T(8,128)(2,1)S(1)}, u32[]{:S(2)}, u32[]{:S(2)}) collective-permute-start(bf16[512,128]{1,0:T(8,128)(2,1)S(1)} %get-tuple-element.56.refs_0_), channel_id=1, source_target_pairs={{0,0},{1,8},{2,2},{3,10},{4,4},{5,12},{6,6},{7,14},{8,1},{9,9},{10... | collective-permute-start | bytes 393224 | tf_op jit(solution)/shard_map/ppermute | solution.py:316
  45.2 11.4 %collective-permute-start.13 = (bf16[520,256]{1,0:T(8,128)(2,1)S(1)}, bf16[520,256]{1,0:T(8,128)(2,1)S(1)}, u32[]{:S(2)}, u32[]{:S(2)}) collective-permute-start(bf16[520,256]{1,0:T(8,128)(2,1)S(1)} %collective-permute-done.11.refs_0_), channel_id=1, source_target_pairs={{0,1},{1,0},{2,3},{3,2},{4,5},{5,4},{6,7},{7,6},{8,9},{9,8},{10,11... | collective-permute-start | bytes 798728 | tf_op jit(solution)/shard_map/ppermute | solution.py:316
  52.8 3.8 %collective-permute-start.15 = (bf16[520,256]{1,0:T(8,128)(2,1)S(1)}, bf16[520,256]{1,0:T(8,128)(2,1)S(1)}, u32[]{:S(2)}, u32[]{:S(2)}) collective-permute-start(bf16[520,256]{1,0:T(8,128)(2,1)S(1)} %collective-permute-done.14.refs_2_), channel_id=1, source_target_pairs={{0,1},{1,0},{2,3},{3,2},{4,5},{5,4},{6,7},{7,6},{8,9},{9,8},{10,11... | collective-permute-start | bytes 798728 | tf_op jit(solution)/shard_map/ppermute | solution.py:316
  52.9 3.7 %collective-permute-start.17 = (bf16[520,256]{1,0:T(8,128)(2,1)S(1)}, bf16[520,256]{1,0:T(8,128)(2,1)S(1)}, u32[]{:S(2)}, u32[]{:S(2)}) collective-permute-start(bf16[520,256]{1,0:T(8,128)(2,1)S(1)} %collective-permute-done.16.refs_4_), channel_id=1, source_target_pairs={{0,1},{1,0},{2,3},{3,2},{4,5},{5,4},{6,7},{7,6},{8,9},{9,8},{10,11... | collective-permute-start | bytes 798728 | tf_op jit(solution)/shard_map/ppermute | solution.py:316
  53.3 21.0 %collective-permute-start.19 = (bf16[520,256]{1,0:T(8,128)(2,1)S(1)}, bf16[520,256]{1,0:T(8,128)(2,1)S(1)}, u32[]{:S(2)}, u32[]{:S(2)}) collective-permute-start(bf16[520,256]{1,0:T(8,128)(2,1)S(1)} %get-tuple-element.84), channel_id=1, source_target_pairs={{0,10},{1,11},{2,8},{3,9},{4,14},{5,15},{6,12},{7,13},{8,2},{9,3},... | collective-permute-start | bytes 798728 | tf_op jit(solution)/shard_map/ppermute | solution.py:316
  53.5 25.8 %collective-permute-start = (bf16[520,256]{1,0:T(8,128)(2,1)S(1)}, bf16[520,256]{1,0:T(8,128)(2,1)S(1)}, u32[]{:S(2)}, u32[]{:S(2)}) collective-permute-start(bf16[520,256]{1,0:T(8,128)(2,1)S(1)} %get-tuple-element.68), channel_id=1, source_target_pairs={{0,8},{1,9},{2,10},{3,11},{4,12},{5,13},{6,14},{7,15},{8,0},{9,1},... | collective-permute-start | bytes 798728 | tf_op jit(solution)/shard_map/ppermute | solution.py:316
  79.3 2.3 %collective-permute-start.18 = (bf16[520,256]{1,0:T(8,128)(2,1)S(1)}, bf16[520,256]{1,0:T(8,128)(2,1)S(1)}, u32[]{:S(2)}, u32[]{:S(2)}) collective-permute-start(bf16[520,256]{1,0:T(8,128)(2,1)S(1)} %collective-permute-done.refs_0_), channel_id=1, source_target_pairs={{0,1},{1,0},{2,3},{3,2},{4,5},{5,4},{6,7},{7,6},{8,9},{9,8},{10,11... | collective-permute-start | bytes 798728 | tf_op jit(solution)/shard_map/ppermute | solution.py:316
  79.3 2.3 %collective-permute-start.20 = (bf16[520,256]{1,0:T(8,128)(2,1)S(1)}, bf16[520,256]{1,0:T(8,128)(2,1)S(1)}, u32[]{:S(2)}, u32[]{:S(2)}) collective-permute-start(bf16[520,256]{1,0:T(8,128)(2,1)S(1)} %collective-permute-done.19.refs_2_), channel_id=1, source_target_pairs={{0,1},{1,0},{2,3},{3,2},{4,5},{5,4},{6,7},{7,6},{8,9},{9,8},{10,11... | collective-permute-start | bytes 798728 | tf_op jit(solution)/shard_map/ppermute | solution.py:316
  79.8 10.2 %collective-permute-start.10 = (bf16[520,256]{1,0:T(8,128)(2,1)S(1)}, bf16[520,256]{1,0:T(8,128)(2,1)S(1)}, u32[]{:S(2)}, u32[]{:S(2)}) collective-permute-start(bf16[520,256]{1,0:T(8,128)(2,1)S(1)} %get-tuple-element.71), channel_id=1, source_target_pairs={{0,12},{1,13},{2,14},{3,15},{4,8},{5,9},{6,10},{7,11},{8,4},{9,5},... | collective-permute-start | bytes 798728 | tf_op jit(solution)/shard_map/ppermute | solution.py:316
  90.0 2.0 %collective-permute-start.21 = (bf16[520,256]{1,0:T(8,128)(2,1)S(1)}, bf16[520,256]{1,0:T(8,128)(2,1)S(1)}, u32[]{:S(2)}, u32[]{:S(2)}) collective-permute-start(bf16[520,256]{1,0:T(8,128)(2,1)S(1)} %collective-permute-done.10.refs_0_), channel_id=1, source_target_pairs={{0,1},{1,0},{2,3},{3,2},{4,5},{5,4},{6,7},{7,6},{8,9},{9,8},{10,11... | collective-permute-start | bytes 798728 | tf_op jit(solution)/shard_map/ppermute | solution.py:316
  90.0 11.6 %collective-permute-start.1 = (bf16[520,256]{1,0:T(8,128)(2,1)S(1)}, bf16[520,256]{1,0:T(8,128)(2,1)S(1)}, u32[]{:S(2)}, u32[]{:S(2)}) collective-permute-start(bf16[520,256]{1,0:T(8,128)(2,1)S(1)} %get-tuple-element.69), channel_id=1, source_target_pairs={{0,14},{1,15},{2,12},{3,13},{4,10},{5,11},{6,8},{7,9},{8,6},{9,7},... | collective-permute-start | bytes 798728 | tf_op jit(solution)/shard_map/ppermute | solution.py:316
  101.6 2.1 %collective-permute-start.22 = (bf16[520,256]{1,0:T(8,128)(2,1)S(1)}, bf16[520,256]{1,0:T(8,128)(2,1)S(1)}, u32[]{:S(2)}, u32[]{:S(2)}) collective-permute-start(bf16[520,256]{1,0:T(8,128)(2,1)S(1)} %collective-permute-done.1.refs_0_), channel_id=1, source_target_pairs={{0,1},{1,0},{2,3},{3,2},{4,5},{5,4},{6,7},{7,6},{8,9},{9,8},{10,11... | collective-permute-start | bytes 798728 | tf_op jit(solution)/shard_map/ppermute | solution.py:316
  106.2 13.4 %collective-permute-start.23 = (bf16[528,128]{1,0:T(8,128)(2,1)S(1)}, bf16[528,128]{1,0:T(8,128)(2,1)S(1)}, u32[]{:S(2)}, u32[]{:S(2)}) collective-permute-start(bf16[528,128]{1,0:T(8,128)(2,1)S(1)} %get-tuple-element.99), channel_id=1, source_target_pairs={{0,0},{8,1},{2,2},{10,3},{4,4},{12,5},{6,6},{14,7},{1,8},{9,9},{3,... | collective-permute-start | bytes 405512 | tf_op jit(solution)/shard_map/ppermute | solution.py:316
  106.9 13.5 %collective-permute-start.24 = (bf16[528,128]{1,0:T(8,128)(2,1)S(1)}, bf16[528,128]{1,0:T(8,128)(2,1)S(1)}, u32[]{:S(2)}, u32[]{:S(2)}) collective-permute-start(bf16[528,128]{1,0:T(8,128)(2,1)S(1)} %get-tuple-element.100), channel_id=1, source_target_pairs={{2,0},{10,1},{0,2},{8,3},{6,4},{14,5},{4,6},{12,7},{3,8},{11,9},{1... | collective-permute-start | bytes 405512 | tf_op jit(solution)/shard_map/ppermute | solution.py:316
  108.2 16.5 %collective-permute-start.25 = (bf16[528,128]{1,0:T(8,128)(2,1)S(1)}, bf16[528,128]{1,0:T(8,128)(2,1)S(1)}, u32[]{:S(2)}, u32[]{:S(2)}) collective-permute-start(bf16[528,128]{1,0:T(8,128)(2,1)S(1)} %get-tuple-element.101), channel_id=1, source_target_pairs={{4,0},{12,1},{6,2},{14,3},{0,4},{8,5},{2,6},{10,7},{5,8},{13,9},{7... | collective-permute-start | bytes 405512 | tf_op jit(solution)/shard_map/ppermute | solution.py:316
  114.3 12.8 %collective-permute-start.26 = (bf16[528,128]{1,0:T(8,128)(2,1)S(1)}, bf16[528,128]{1,0:T(8,128)(2,1)S(1)}, u32[]{:S(2)}, u32[]{:S(2)}) collective-permute-start(bf16[528,128]{1,0:T(8,128)(2,1)S(1)} %get-tuple-element.102), channel_id=1, source_target_pairs={{6,0},{14,1},{4,2},{12,3},{2,4},{10,5},{0,6},{8,7},{7,8},{15,9},{5... | collective-permute-start | bytes 405512 | tf_op jit(solution)/shard_map/ppermute | solution.py:316
  114.6 12.4 %collective-permute-start.27 = (bf16[528,128]{1,0:T(8,128)(2,1)S(1)}, bf16[528,128]{1,0:T(8,128)(2,1)S(1)}, u32[]{:S(2)}, u32[]{:S(2)}) collective-permute-start(bf16[528,128]{1,0:T(8,128)(2,1)S(1)} %get-tuple-element.103), channel_id=1, source_target_pairs={{1,0},{9,1},{3,2},{11,3},{5,4},{13,5},{7,6},{15,7},{0,8},{8,9},{2,... | collective-permute-start | bytes 405512 | tf_op jit(solution)/shard_map/ppermute | solution.py:316
  119.7 7.4 %collective-permute-start.28 = (bf16[528,128]{1,0:T(8,128)(2,1)S(1)}, bf16[528,128]{1,0:T(8,128)(2,1)S(1)}, u32[]{:S(2)}, u32[]{:S(2)}) collective-permute-start(bf16[528,128]{1,0:T(8,128)(2,1)S(1)} %get-tuple-element.104), channel_id=1, source_target_pairs={{3,0},{11,1},{1,2},{9,3},{7,4},{15,5},{5,6},{13,7},{2,8},{10,9},{0... | collective-permute-start | bytes 405512 | tf_op jit(solution)/shard_map/ppermute | solution.py:316
  120.4 7.4 %collective-permute-start.29 = (bf16[528,128]{1,0:T(8,128)(2,1)S(1)}, bf16[528,128]{1,0:T(8,128)(2,1)S(1)}, u32[]{:S(2)}, u32[]{:S(2)}) collective-permute-start(bf16[528,128]{1,0:T(8,128)(2,1)S(1)} %get-tuple-element.105), channel_id=1, source_target_pairs={{5,0},{13,1},{7,2},{15,3},{1,4},{9,5},{3,6},{11,7},{4,8},{12,9},{6... | collective-permute-start | bytes 405512 | tf_op jit(solution)/shard_map/ppermute | solution.py:316
  124.6 14.2 %collective-permute-start.30 = (bf16[528,128]{1,0:T(8,128)(2,1)S(1)}, bf16[528,128]{1,0:T(8,128)(2,1)S(1)}, u32[]{:S(2)}, u32[]{:S(2)}) collective-permute-start(bf16[528,128]{1,0:T(8,128)(2,1)S(1)} %get-tuple-element.106), channel_id=1, source_target_pairs={{7,0},{15,1},{5,2},{13,3},{3,4},{11,5},{1,6},{9,7},{6,8},{14,9},{4... | collective-permute-start | bytes 405512 | tf_op jit(solution)/shard_map/ppermute | solution.py:316
  (6 other events, 42.0 us)
